TPU v7x, 512 devices: a whole 4x8x8 slice. The times are simulated.
512 devices in a mesh: section: 16 (over x_lo, z), dp: 32 (over x_hi, y, core).
Axes of the slice: x: 4 (x_hi: 2, x_lo: 2; x = x_hi * 2 + x_lo), y: 8, z: 8, core: 2. Of those that a mesh axis runs over, the one named last changes fastest.
Arguments:
- acts_down: bfloat16 [3, 16, 32, 16, 16, 256], P(None, 'section', 'dp'), may hold values from -6 to 6
- acts_up: bfloat16 [3, 16, 32, 16, 16, 256], P(None, 'section', 'dp'), may hold values from -6 to 6
- front_down: bfloat16 [16, 32, 16, 16, 256], P('section', 'dp'), may hold values from -6 to 6
- front_up: bfloat16 [16, 32, 16, 16, 256], P('section', 'dp'), may hold values from -6 to 6
- master: float32 [16, 2304, 256], P('section', 'dp'), may hold values from -4 to 4
- moment_first: float32 [16, 2304, 256], P('section', 'dp'), may hold values from -36 to 36
- moment_second: float32 [16, 2304, 256], P('section', 'dp'), may hold values from 10 to 100
Outputs:
- dx_down: bfloat16 [3, 16, 32, 16, 16, 256], P(None, 'section', 'dp')
- dx_up: bfloat16 [3, 16, 32, 16, 16, 256], P(None, 'section', 'dp')
- new_weight: bfloat16 [16, 2304, 256], P('section', 'dp')
- new_master: float32 [16, 2304, 256], P('section', 'dp')
- new_first: float32 [16, 2304, 256], P('section', 'dp')
- new_second: float32 [16, 2304, 256], P('section', 'dp')
All inputs are finite; a program needn't handle non-finite values.
Results may differ from a plain program's by a relative error of at most 0.0025.
The roundings to bfloat16 on the way count: a program that leaves them out, or rounds other values in their place, can miss the bound.
Values may be sent and summed in bfloat16 or wider, within the bound.
No kernel may reach another device: no remote copies, remote signals or barrier semaphores. Data moves between devices by JAX's collectives and lax.ppermute only.
A program may use at most 64 MiB of HBM per device.

v0:
```python
import jax
import jax.numpy as jnp
from jax import lax
from jax.sharding import PartitionSpec as P

TICKS = 3


beta_first = 0.9
beta_second = 0.95
learn_rate = 0.01
decay_rate = 0.1
epsilon = 1e-08


def from_partner(value, axis, stride):
    return lax.ppermute(value, axis, [(i, i ^ 1 << stride) for i in range(lax.axis_size(axis))])


def passed_along(value, axis, by):
    length = lax.axis_size(axis)
    pairs = [(i, i + by) for i in range(length) if 0 <= i + by < length]
    return lax.ppermute(value, axis, pairs)


def shifted_taps(feature, direction):
    images, height, columns, channels = feature.shape
    padded = jnp.pad(feature, ((0, 0), (1, 1), (1, 1), (0, 0)))
    pieces = []
    for row_step in range(3):
        for col_step in range(3):
            row_start = 1 + direction * (row_step - 1)
            col_start = 1 + direction * (col_step - 1)
            pieces.append(
                padded[:, row_start : row_start + height, col_start : col_start + columns, :]
            )
    return jnp.concatenate(pieces, axis=3).reshape(images * height * columns, 9 * channels)


def section_front(inputs, incoming, weight):
    channels = inputs.shape[-1]
    factor = (9 * channels) ** (-0.5)
    taps_front = shifted_taps(incoming, -1).reshape(-1, 9, channels)
    kernel = weight.reshape(9, channels, channels)
    grad_hidden = lax.dot_general(
        taps_front, kernel, (((1, 2), (0, 2)), ((), ())), preferred_element_type=jnp.float32
    )
    grad_hidden = factor * grad_hidden.reshape(inputs.shape)
    widened = inputs.astype(jnp.float32)
    hidden, pullback = jax.vjp(jax.nn.gelu, widened)
    outgoing = (incoming.astype(jnp.float32) + pullback(grad_hidden)[0]).astype(jnp.bfloat16)
    return (outgoing, hidden.astype(jnp.bfloat16))


def weight_term(hiddens, seen):
    channels = hiddens[0].shape[-1]
    factor = (9 * channels) ** (-0.5)
    summed = jnp.zeros((9 * channels, channels), jnp.float32)
    for hidden, incoming in zip(hiddens, seen):
        taps_hidden = shifted_taps(hidden, 1)
        summed = summed + lax.dot_general(
            taps_hidden,
            incoming.reshape(-1, channels),
            (((0,), (0,)), ((), ())),
            preferred_element_type=jnp.float32,
        )
    return factor * summed


def per_device(acts_down, acts_up, front_down, front_up, master, moment_first, moment_second):
    sections = lax.axis_size("section")
    own_rows = master[0].astype(jnp.bfloat16)
    mirror_rows = own_rows
    for bit_number in range(sections.bit_length() - 1):
        mirror_rows = from_partner(mirror_rows, "section", bit_number)
    own_weight, mirror_weight = (
        lax.all_gather(own_rows, "dp", axis=0, tiled=True),
        lax.all_gather(mirror_rows, "dp", axis=0, tiled=True),
    )
    grad_down = front_down[0]
    grad_up = front_up[0]
    seen_down = []
    seen_up = []
    hidden_down = []
    hidden_up = []
    outs_down = []
    outs_up = []
    for tick_index in range(TICKS):
        seen_down.append(grad_down)
        seen_up.append(grad_up)
        next_down, hid_down = section_front(acts_down[tick_index, 0], grad_down, own_weight)
        next_up, hid_up = section_front(acts_up[tick_index, 0], grad_up, mirror_weight)
        hidden_down.append(hid_down)
        hidden_up.append(hid_up)
        outs_down.append(next_down)
        outs_up.append(next_up)
        if tick_index + 1 < TICKS:
            grad_down = passed_along(next_down, "section", -1)
            grad_up = passed_along(next_up, "section", 1)
    term_down = weight_term(hidden_down, seen_down)
    term_up = weight_term(hidden_up, seen_up)
    full_down, full_up = (
        lax.psum(term_down.astype(jnp.bfloat16), "dp").astype(jnp.float32),
        lax.psum(term_up.astype(jnp.bfloat16), "dp").astype(jnp.float32),
    )
    shard_rows = term_down.shape[0] // lax.axis_size("dp")
    row_start = lax.axis_index("dp") * shard_rows
    down_rows = lax.dynamic_slice_in_dim(full_down, row_start, shard_rows, 0)
    up_rows = lax.dynamic_slice_in_dim(full_up, row_start, shard_rows, 0)
    mirror_grad = up_rows
    for bit_number in range(sections.bit_length() - 1):
        mirror_grad = from_partner(mirror_grad.astype(jnp.bfloat16), "section", bit_number).astype(
            mirror_grad.dtype
        )
    gradient = down_rows + mirror_grad
    old_master = master[0]
    new_first = beta_first * moment_first[0] + (1.0 - beta_first) * gradient
    new_second = beta_second * moment_second[0] + (1.0 - beta_second) * gradient * gradient
    new_master = old_master - learn_rate * (
        new_first / (jnp.sqrt(new_second) + epsilon) + decay_rate * old_master
    )
    return (
        jnp.stack(outs_down)[:, None],
        jnp.stack(outs_up)[:, None],
        new_master.astype(jnp.bfloat16)[None],
        new_master[None],
        new_first[None],
        new_second[None],
    )


def solution(mesh):
    placed = (
        P(None, "section", "dp", None, None, None),
        P(None, "section", "dp", None, None, None),
        P("section", "dp", None, None, None),
        P("section", "dp", None, None, None),
        P("section", "dp", None),
        P("section", "dp", None),
        P("section", "dp", None),
    )
    return jax.shard_map(
        per_device,
        mesh=mesh,
        in_specs=placed,
        out_specs=(
            P(None, "section", "dp", None, None, None),
            P(None, "section", "dp", None, None, None),
            P("section", "dp", None),
            P("section", "dp", None),
            P("section", "dp", None),
            P("section", "dp", None),
        ),
        check_vma=False,
    )
```

profile of v0, /device:TPU:6, one launch (start us, length us, event | category | flops | bytes accessed | tf_op | source)
XLA Modules:
  0.0 533.7 jit_solution(15789119350843120180)
XLA Ops:
  8.8 4.3 collective-permute-start.2
  32.8 6.1 %collective-permute-start.3 = (bf16[72,256]{1,0:T(8,128)(2,1)S(1)}, bf16[72,256]{1,0:T(8,128)(2,1)S(1)}, u32[]{:S(2)}, u32[]{:S(2)}) collective-permute-start(bf16[72,256]{1,0:T(8,128)(2,1)S(1)} %collective-permute-done.2), channel_id=1, source_target_pairs={{0,64},{32,96},{64,0},{96,32},{128,192},{160,224},{192,128},{224,1... | collective-permute-start | bytes 110600 | tf_op jit(solution)/shard_map/ppermute | solution.py:17
  40.8 9.1 %collective-permute-start.4 = (bf16[72,256]{1,0:T(8,128)(2,1)S(1)}, bf16[72,256]{1,0:T(8,128)(2,1)S(1)}, u32[]{:S(2)}, u32[]{:S(2)}) collective-permute-start(bf16[72,256]{1,0:T(8,128)(2,1)S(1)} %collective-permute-done.3), channel_id=1, source_target_pairs={{0,128},{32,160},{64,192},{96,224},{128,0},{160,32},{192,64},{224,... | collective-permute-start | bytes 110600 | tf_op jit(solution)/shard_map/ppermute | solution.py:17
  51.9 2.7 collective-permute-start.5
  55.3 3.5 dot_general.48
  60.2 3.3 fusion.219
  63.4 34.8 %all-gather.3.cloned.1.call-done = bf16[2304,256]{1,0:T(8,128)(2,1)} async-done(((bf16[72,256]{1,0:T(8,128)(2,1)}), bf16[2304,256]{1,0:T(8,128)(2,1)}) %all-gather.3.cloned.1.call-update) | async-done | bytes 1179664 | tf_op jit(solution)/shard_map/all_gather | solution.py:77
  98.3 2.9 fusion.119
  101.1 5.5 %collective-permute-start = (bf16[1,16,16,256]{3,2,1,0:T(8,128)(2,1)S(1)}, bf16[1,16,16,256]{3,2,1,0:T(8,128)(2,1)S(1)}, u32[]{:S(2)}, u32[]{:S(2)}) collective-permute-start(bf16[1,16,16,256]{3,2,1,0:T(8,128)(2,1)S(1)} %bitcast.548), channel_id=1, source_target_pairs={{32,0},{64,32},{96,64},{128,96},{160,128},{192,160},{224,192},{256... | collective-permute-start | bytes 393224 | tf_op jit(solution)/shard_map/ppermute | solution.py:23
  107.3 3.6 dot_general.54
  118.0 3.5 dot_general.50
  121.5 3.5 fusion.125
  125.0 4.6 collective-permute-start.1
  129.6 52.7 %all-gather.5.cloned.1.call-done = bf16[2304,256]{1,0:T(8,128)(2,1)} async-done(((bf16[72,256]{1,0:T(8,128)(2,1)}), bf16[2304,256]{1,0:T(8,128)(2,1)}) %all-gather.5.cloned.1.call-update) | async-done | bytes 1179664 | tf_op jit(solution)/shard_map/all_gather | solution.py:78
  182.4 3.0 fusion.139
  185.4 3.7 collective-permute-start.6
  191.1 3.9 collective-permute-done.6
  201.3 3.5 dot_general.56
  204.8 3.0 fusion.145
  207.9 2.1 collective-permute-start.7
  210.0 3.7 fusion.7
  213.7 3.3 collective-permute-done.7
  225.6 2.4 dot_general.52
  228.1 2.2 fusion.211
  236.9 258.5 %all-reduce.15.cloned.1.call-done = (bf16[2304,256]{1,0:T(8,128)(2,1)}, bf16[2304,256]{1,0:T(8,128)(2,1)}) async-done(((bf16[2304,256]{1,0:T(8,128)(2,1)}, bf16[2304,256]{1,0:T(8,128)(2,1)}), (bf16[2304,256]{1,0:T(8,128)(2,1)}, bf16[2304,256]{1,0:T(8,128)(2,1)})) %all-reduce.15.cloned.1.call-update) | async-done | bytes 2359312 | tf_op jit(solution)/shard_map/psum | solution.py:104
  496.2 3.5 collective-permute-start.8
  502.0 4.6 collective-permute-start.9
  507.3 2.4 dot_general.58
  509.8 7.3 %collective-permute-start.10 = (bf16[72,256]{1,0:T(8,128)(2,1)S(1)}, bf16[72,256]{1,0:T(8,128)(2,1)S(1)}, u32[]{:S(2)}, u32[]{:S(2)}) collective-permute-start(bf16[72,256]{1,0:T(8,128)(2,1)S(1)} %collective-permute-done.9), channel_id=1, source_target_pairs={{0,128},{32,160},{64,192},{96,224},{128,0},{160,32},{192,64},{224,... | collective-permute-start | bytes 110600 | tf_op jit(solution)/shard_map/ppermute | solution.py:17
  517.1 2.2 fusion.194
  519.8 2.7 collective-permute-start.11
  523.3 2.3 collective-permute-done.11
  (170 shorter events, 64.4 us)
Async XLA Ops:
  7.2 9.8 %copy-start = (bf16[1,1,16,16,256]{4,3,2,1,0:T(8,128)(2,1)S(1)}, bf16[1,1,16,16,256]{4,3,2,1,0:T(8,128)(2,1)}, u32[]{:S(2)}) copy-start(bf16[1,1,16,16,256]{4,3,2,1,0:T(8,128)(2,1)} %param.9) | copy-start | bytes 393220
  7.2 91.1 %all-gather.3.cloned.1.call-start = ((), (), s32[]{:S(2)}) async-start(), calls=%async_computation | async-start | bytes 1216512 | tf_op jit(solution)/shard_map/all_gather | solution.py:77
  8.8 173.6 %all-gather.5.cloned.1.call-start = ((), (), s32[]{:S(2)}) async-start(), calls=%async_computation.1 | async-start | bytes 1216512 | tf_op jit(solution)/shard_map/all_gather | solution.py:78
  8.8 23.9 %collective-permute-start.2 = (bf16[72,256]{1,0:T(8,128)(2,1)}, bf16[72,256]{1,0:T(8,128)(2,1)S(1)}, u32[]{:S(2)}, u32[]{:S(2)}) collective-permute-start(bf16[72,256]{1,0:T(8,128)(2,1)} %bitcast_convert_fusion), channel_id=1, source_target_pairs={{0,32},{32,0},{64,96},{96,64},{128,160},{160,128},{192,224},{224,1... | collective-permute-start | bytes 110600 | tf_op jit(solution)/shard_map/ppermute | solution.py:17
  13.1 5.0 copy-start.1
  17.1 1.0 copy-start.5
  18.1 1.0 copy-start.4
  19.1 1.0 copy-start.6
  20.6 1.0 copy-start.15
  22.6 3.3 copy-start.13
  32.7 17.9 %copy-start.17 = (bf16[1,16,16,2304]{3,2,1,0:T(8,128)(2,1)}, bf16[1,16,16,2304]{3,2,1,0:T(8,128)(2,1)S(1)}, u32[]{:S(2)}) copy-start(bf16[1,16,16,2304]{3,2,1,0:T(8,128)(2,1)S(1)} %constant_dynamic-update-slice_fusion.72) | copy-start | bytes 3538948
  32.8 8.0 %collective-permute-start.3 = (bf16[72,256]{1,0:T(8,128)(2,1)S(1)}, bf16[72,256]{1,0:T(8,128)(2,1)S(1)}, u32[]{:S(2)}, u32[]{:S(2)}) collective-permute-start(bf16[72,256]{1,0:T(8,128)(2,1)S(1)} %collective-permute-done.2), channel_id=1, source_target_pairs={{0,64},{32,96},{64,0},{96,32},{128,192},{160,224},{192,128},{224,1... | collective-permute-start | bytes 110600 | tf_op jit(solution)/shard_map/ppermute | solution.py:17
  40.8 11.1 %collective-permute-start.4 = (bf16[72,256]{1,0:T(8,128)(2,1)S(1)}, bf16[72,256]{1,0:T(8,128)(2,1)S(1)}, u32[]{:S(2)}, u32[]{:S(2)}) collective-permute-start(bf16[72,256]{1,0:T(8,128)(2,1)S(1)} %collective-permute-done.3), channel_id=1, source_target_pairs={{0,128},{32,160},{64,192},{96,224},{128,0},{160,32},{192,64},{224,... | collective-permute-start | bytes 110600 | tf_op jit(solution)/shard_map/ppermute | solution.py:17
  51.9 6.9 %collective-permute-start.5 = (bf16[72,256]{1,0:T(8,128)(2,1)S(1)}, bf16[72,256]{1,0:T(8,128)(2,1)S(1)}, u32[]{:S(2)}, u32[]{:S(2)}) collective-permute-start(bf16[72,256]{1,0:T(8,128)(2,1)S(1)} %collective-permute-done.4), channel_id=1, source_target_pairs={{0,256},{32,288},{64,320},{96,352},{128,384},{160,416},{192,448},{... | collective-permute-start | bytes 110600 | tf_op jit(solution)/shard_map/ppermute | solution.py:17
  59.4 435.9 %all-reduce.15.cloned.1.call-start = ((), (), s32[]{:S(2)}) async-start(), calls=%async_computation.2 | async-start | bytes 4718592 | tf_op jit(solution)/shard_map/psum | solution.py:104
  101.1 10.5 %collective-permute-start = (bf16[1,16,16,256]{3,2,1,0:T(8,128)(2,1)S(1)}, bf16[1,16,16,256]{3,2,1,0:T(8,128)(2,1)S(1)}, u32[]{:S(2)}, u32[]{:S(2)}) collective-permute-start(bf16[1,16,16,256]{3,2,1,0:T(8,128)(2,1)S(1)} %bitcast.548), channel_id=1, source_target_pairs={{32,0},{64,32},{96,64},{128,96},{160,128},{192,160},{224,192},{256... | collective-permute-start | bytes 393224 | tf_op jit(solution)/shard_map/ppermute | solution.py:23
  125.0 64.1 %collective-permute-start.1 = (bf16[1,16,16,256]{3,2,1,0:T(8,128)(2,1)}, bf16[1,16,16,256]{3,2,1,0:T(8,128)(2,1)S(1)}, u32[]{:S(2)}, u32[]{:S(2)}) collective-permute-start(bf16[1,16,16,256]{3,2,1,0:T(8,128)(2,1)} %fusion.125), channel_id=1, source_target_pairs={{32,0},{64,32},{96,64},{128,96},{160,128},{192,160},{224,192},{256... | collective-permute-start | bytes 393224 | tf_op jit(solution)/shard_map/ppermute | solution.py:23
  182.4 6.8 %copy-start.18 = (bf16[1,16,16,2304]{3,2,1,0:T(8,128)(2,1)S(1)}, bf16[1,16,16,2304]{3,2,1,0:T(8,128)(2,1)}, u32[]{:S(2)}) copy-start(bf16[1,16,16,2304]{3,2,1,0:T(8,128)(2,1)} %copy-done.17) | copy-start | bytes 3538948
  185.4 9.6 %collective-permute-start.6 = (bf16[1,16,16,256]{3,2,1,0:T(8,128)(2,1)S(1)}, bf16[1,16,16,256]{3,2,1,0:T(8,128)(2,1)S(1)}, u32[]{:S(2)}, u32[]{:S(2)}) collective-permute-start(bf16[1,16,16,256]{3,2,1,0:T(8,128)(2,1)S(1)} %bitcast.546), channel_id=1, source_target_pairs={{0,32},{32,64},{64,96},{96,128},{128,160},{160,192},{192,224},{224... | collective-permute-start | bytes 393224 | tf_op jit(solution)/shard_map/ppermute | solution.py:23
  204.8 5.1 copy-start.2
  207.9 5.8 %copy-start.8 = (bf16[1,16,16,256]{3,2,1,0:T(8,128)(2,1)}, bf16[1,16,16,256]{3,2,1,0:T(8,128)(2,1)S(1)}, u32[]{:S(2)}) copy-start(bf16[1,16,16,256]{3,2,1,0:T(8,128)(2,1)S(1)} %fusion.145) | copy-start | bytes 393220
  207.9 9.1 %copy-start.16 = (bf16[1,16,16,2304]{3,2,1,0:T(8,128)(2,1)S(1)}, bf16[1,16,16,2304]{3,2,1,0:T(8,128)(2,1)}, u32[]{:S(2)}) copy-start(bf16[1,16,16,2304]{3,2,1,0:T(8,128)(2,1)} %copy-done.15) | copy-start | bytes 3538948
  207.9 9.1 %collective-permute-start.7 = (bf16[1,16,16,256]{3,2,1,0:T(8,128)(2,1)S(1)}, bf16[1,16,16,256]{3,2,1,0:T(8,128)(2,1)S(1)}, u32[]{:S(2)}, u32[]{:S(2)}) collective-permute-start(bf16[1,16,16,256]{3,2,1,0:T(8,128)(2,1)S(1)} %fusion.145), channel_id=1, source_target_pairs={{0,32},{32,64},{64,96},{96,128},{128,160},{160,192},{192,224},{224... | collective-permute-start | bytes 393224 | tf_op jit(solution)/shard_map/ppermute | solution.py:23
  213.7 3.9 copy-start.14
  496.2 5.8 %collective-permute-start.8 = (bf16[72,256]{1,0:T(8,128)(2,1)S(1)}, bf16[72,256]{1,0:T(8,128)(2,1)S(1)}, u32[]{:S(2)}, u32[]{:S(2)}) collective-permute-start(bf16[72,256]{1,0:T(8,128)(2,1)S(1)} %convert_convert_fusion), channel_id=1, source_target_pairs={{0,32},{32,0},{64,96},{96,64},{128,160},{160,128},{192,224},{224,1... | collective-permute-start | bytes 110600 | tf_op jit(solution)/shard_map/ppermute | solution.py:17
  502.0 7.8 %collective-permute-start.9 = (bf16[72,256]{1,0:T(8,128)(2,1)S(1)}, bf16[72,256]{1,0:T(8,128)(2,1)S(1)}, u32[]{:S(2)}, u32[]{:S(2)}) collective-permute-start(bf16[72,256]{1,0:T(8,128)(2,1)S(1)} %collective-permute-done.8), channel_id=1, source_target_pairs={{0,64},{32,96},{64,0},{96,32},{128,192},{160,224},{192,128},{224,1... | collective-permute-start | bytes 110600 | tf_op jit(solution)/shard_map/ppermute | solution.py:17
  509.8 12.7 %copy-start.9 = (bf16[1,16,16,256]{3,2,1,0:T(8,128)(2,1)S(1)}, bf16[1,16,16,256]{3,2,1,0:T(8,128)(2,1)}, u32[]{:S(2)}) copy-start(bf16[1,16,16,256]{3,2,1,0:T(8,128)(2,1)} %copy-done.8) | copy-start | bytes 393220
  509.8 15.8 %copy-start.7 = (f32[1,72,256]{2,1,0:T(8,128)S(1)}, f32[1,72,256]{2,1,0:T(8,128)}, u32[]{:S(2)}) copy-start(f32[1,72,256]{2,1,0:T(8,128)} %param.11) | copy-start | bytes 221188
  509.8 15.8 %copy-start.10 = (f32[1,72,256]{2,1,0:T(8,128)S(1)}, f32[1,72,256]{2,1,0:T(8,128)}, u32[]{:S(2)}) copy-start(f32[1,72,256]{2,1,0:T(8,128)} %param.13) | copy-start | bytes 221188
  509.8 15.8 %copy-start.11 = (f32[1,72,256]{2,1,0:T(8,128)S(1)}, f32[1,72,256]{2,1,0:T(8,128)}, u32[]{:S(2)}) copy-start(f32[1,72,256]{2,1,0:T(8,128)} %param.12) | copy-start | bytes 221188
  509.8 9.9 %collective-permute-start.10 = (bf16[72,256]{1,0:T(8,128)(2,1)S(1)}, bf16[72,256]{1,0:T(8,128)(2,1)S(1)}, u32[]{:S(2)}, u32[]{:S(2)}) collective-permute-start(bf16[72,256]{1,0:T(8,128)(2,1)S(1)} %collective-permute-done.9), channel_id=1, source_target_pairs={{0,128},{32,160},{64,192},{96,224},{128,0},{160,32},{192,64},{224,... | collective-permute-start | bytes 110600 | tf_op jit(solution)/shard_map/ppermute | solution.py:17
  519.8 5.8 %collective-permute-start.11 = (bf16[72,256]{1,0:T(8,128)(2,1)S(1)}, bf16[72,256]{1,0:T(8,128)(2,1)S(1)}, u32[]{:S(2)}, u32[]{:S(2)}) collective-permute-start(bf16[72,256]{1,0:T(8,128)(2,1)S(1)} %collective-permute-done.10), channel_id=1, source_target_pairs={{0,256},{32,288},{64,320},{96,352},{128,384},{160,416},{192,448},{... | collective-permute-start | bytes 110600 | tf_op jit(solution)/shard_map/ppermute | solution.py:17
  (2 other events, 1.6 us)
Sparse Core Ops, SparseCore 0:
  11.8 86.3 all-gather.2
  102.1 80.2 all-gather.4
  219.4 275.9 all-reduce.14
where the time goes:
time: 535 us; the launch traced here: 534 us
  waiting for transfers between devices  360 us (67%)
  local copies, waits for them, and re-layouts  65.3 us (12%)
  starting transfers between devices  56.4 us (11%)
  matrix products  28.5 us (5%)
  between operations  14.5 us (3%)
  other arithmetic  8.8 us (2%)
    psum x1, waiting for transfers between devices, per_device(): lax.psum(term_up.astype(jnp.bfloat16), 'dp').astype(jnp.float32)  258 us
    all_gather x1, waiting for transfers between devices, per_device(): lax.all_gather(mirror_rows, 'dp', axis=0, tiled=True)  52.7 us
    unnamed x126, local copies, waits for them, and re-layouts  40.9 us
    ppermute x8, starting transfers between devices, from_partner(): lax.ppermute(value, axis, [(i, i ^ 1 << stride) for i in range(lax.axis_s...  40.4 us
    all_gather x1, waiting for transfers between devices, per_device(): lax.all_gather(own_rows, 'dp', axis=0, tiled=True)  34.8 us
    dot_general x6, local copies, waits for them, and re-layouts, section_front(): lax.dot_general(taps_front, kernel, (((1, 2), (0, 2)), ((), ())), preferr...  19.1 us
    dot_general x6, matrix products, section_front(): lax.dot_general(taps_front, kernel, (((1, 2), (0, 2)), ((), ())), preferr...  16.8 us
    ppermute x4, starting transfers between devices, passed_along(): return lax.ppermute(value, axis, pairs)  15.9 us
  transfers between devices with their start and end apart: 15, of which 10 were waited for; matrix products, arithmetic and copies ran while one was open for 15% of the time, Pallas kernels for 0%

commit v1 on v0

v1 whole, which is shorter than its diff:
```python
import functools
import jax
import jax.numpy as jnp
from jax import lax
from jax.experimental import pallas as pl
from jax.experimental.pallas import tpu as pltpu
from jax.sharding import Mesh, PartitionSpec as P


def gelu_kernel(act_ref, hid_ref, slope_ref):
    x = act_ref[0].astype(jnp.float32)
    cube = 0.044715 * x * x * x
    t = jnp.tanh(0.7978845608028654 * (x + cube))
    half = 0.5 * (1.0 + t)
    hidden = (x * half).astype(jnp.bfloat16)
    hid_ref[0] = hidden.astype(jnp.float32).T.astype(jnp.bfloat16)
    inner = 0.7978845608028654 * (1.0 + 3.0 * 0.044715 * x * x)
    slope_ref[0] = half + 0.5 * x * (1.0 - t * t) * inner


def gelu_parts(acts):
    n, pixels, channels = acts.shape
    return pl.pallas_call(
        gelu_kernel,
        grid=(n,),
        in_specs=[pl.BlockSpec((1, pixels, channels), lambda i: (i, 0, 0))],
        out_specs=[
            pl.BlockSpec((1, channels, pixels), lambda i: (i, 0, 0)),
            pl.BlockSpec((1, pixels, channels), lambda i: (i, 0, 0)),
        ],
        out_shape=[
            jax.ShapeDtypeStruct((n, channels, pixels), jnp.bfloat16),
            jax.ShapeDtypeStruct((n, pixels, channels), jnp.float32),
        ],
        name="gelu_parts",
    )(acts)


def fill_taps(front, pad_ref, width):
    pixels = front.shape[0]
    wide = front.astype(jnp.float32)
    column = lax.broadcasted_iota(jnp.int32, wide.shape, 0) % width
    after = jnp.where(column == width - 1, 0.0, pltpu.roll(wide, pixels - 1, 0))
    before = jnp.where(column == 0, 0.0, pltpu.roll(wide, 1, 0))
    empty = jnp.zeros((width, front.shape[1]), jnp.bfloat16)
    for b, piece in enumerate((after.astype(jnp.bfloat16), front, before.astype(jnp.bfloat16))):
        pad_ref[b, 0:width] = empty
        pad_ref[b, width : width + pixels] = piece
        pad_ref[b, width + pixels : 2 * width + pixels] = empty


def tick_kernel(width, factor, front_ref, weight_ref, slope_ref, out_ref, pad_ref):
    front = front_ref[0]
    pixels, channels = front.shape
    fill_taps(front, pad_ref, width)
    total = jnp.zeros((pixels, channels), jnp.float32)
    for a in range(3):
        for b in range(3):
            row = (3 * a + b) * channels
            total += lax.dot_general(
                pad_ref[b, (2 - a) * width : (2 - a) * width + pixels],
                weight_ref[0, row : row + channels],
                (((1,), (1,)), ((), ())),
                preferred_element_type=jnp.float32,
            )
    out_ref[0] = (front.astype(jnp.float32) + slope_ref[0] * (factor * total)).astype(jnp.bfloat16)


def tick(fronts, weights, slopes, width):
    n, pixels, channels = fronts.shape
    factor = (9 * channels) ** -0.5
    whole = lambda i: (i, 0, 0)
    shared = weights.shape[0] == 1
    return pl.pallas_call(
        functools.partial(tick_kernel, width, factor),
        grid=(n,),
        in_specs=[
            pl.BlockSpec((1, pixels, channels), whole),
            pl.BlockSpec((1, 9 * channels, channels), (lambda i: (0, 0, 0)) if shared else whole),
            pl.BlockSpec((1, pixels, channels), whole),
        ],
        out_specs=pl.BlockSpec((1, pixels, channels), whole),
        out_shape=jax.ShapeDtypeStruct(fronts.shape, jnp.bfloat16),
        scratch_shapes=[pltpu.VMEM((3, pixels + 2 * width, channels), jnp.bfloat16)],
        name="tick",
    )(fronts, weights, slopes)


def term_kernel(parts, ticks, width, factor, *refs):
    hid_refs, front_refs, out_ref, pad_ref = refs[:parts], refs[parts:-2], refs[-2], refs[-1]
    for t, front_ref in enumerate(front_refs):
        fill_taps(front_ref[0], pad_ref.at[t], width)
    hiddens = [ref.at[t] for ref in hid_refs for t in range(ref.shape[0])]
    channels, pixels = hiddens[0].shape
    for a in range(3):
        for b in range(3):
            row = (3 * a + b) * channels
            total = jnp.zeros((channels, channels), jnp.float32)
            for t, hidden in enumerate(hiddens):
                total += lax.dot_general(
                    hidden[...],
                    pad_ref[t, b, (2 - a) * width : (2 - a) * width + pixels],
                    (((1,), (0,)), ((), ())),
                    preferred_element_type=jnp.float32,
                )
            out_ref[row : row + channels] = (factor * total).astype(jnp.bfloat16)


def weight_term(hiddens, fronts, width):
    channels, pixels = hiddens[0].shape[1:]
    factor = (9 * channels) ** -0.5
    return pl.pallas_call(
        functools.partial(term_kernel, len(hiddens), len(fronts), width, factor),
        out_shape=jax.ShapeDtypeStruct((9 * channels, channels), jnp.bfloat16),
        scratch_shapes=[
            pltpu.VMEM((len(fronts), 3, pixels + 2 * width, channels), jnp.bfloat16)
        ],
        name="weight_term",
    )(*hiddens, *fronts)


beta_first = 0.9
beta_second = 0.95
learn_rate = 0.01
decay_rate = 0.1
epsilon = 1e-08

SECTION = ("x_lo", "z")
CHIPS = ("x_hi", "y")


def to_mirror(value):
    length = lax.axis_size(SECTION)
    return lax.ppermute(value, SECTION, [(i, length - 1 - i) for i in range(length)])


def from_next(value):
    length = lax.axis_size(SECTION)
    return lax.ppermute(value, SECTION, [(i + 1, i) for i in range(length - 1)])


def to_partner(value):
    return lax.ppermute(value, "core", [(0, 1), (1, 0)])


def gather_rows(rows):
    chips = lax.axis_size(CHIPS)
    spread = jnp.broadcast_to(rows[None], (chips, *rows.shape))
    mine = lax.all_to_all(spread, CHIPS, 0, 0, tiled=True)
    other = to_partner(mine)
    first = lax.axis_index("core") == 0
    whole = jnp.stack([jnp.where(first, mine, other), jnp.where(first, other, mine)], axis=1)
    return whole.reshape(-1, rows.shape[1])


def scatter_sum(part):
    chips = lax.axis_size(CHIPS)
    core = lax.axis_index("core")
    split = part.reshape(chips, 2, -1, part.shape[1])
    given = lax.dynamic_index_in_dim(split, 1 - core, 1, keepdims=False)
    kept = lax.dynamic_index_in_dim(split, core, 1, keepdims=False)
    pair = (kept.astype(jnp.float32) + to_partner(given).astype(jnp.float32)).astype(jnp.bfloat16)
    pieces = lax.all_to_all(pair, CHIPS, 0, 0, tiled=True)
    return jnp.sum(pieces.astype(jnp.float32), axis=0)


def per_device(acts_down, acts_up, front_down, front_up, master, moment_first, moment_second):
    ticks, _, _, height, width, channels = acts_down.shape
    pixels = height * width
    flat = (1, pixels, channels)
    front_down = front_down.reshape(flat)
    front_up = to_mirror(front_up.reshape(flat))
    far_acts = [to_mirror(acts_up[t].reshape(flat)) for t in range(ticks)]
    weight = gather_rows(master[0].astype(jnp.bfloat16))[None]
    hid_down, slope_down = gelu_parts(acts_down.reshape(ticks, pixels, channels))
    hid_up, slope_up = [], []
    for t in range(ticks):
        hidden, slope = gelu_parts(far_acts[t])
        hid_up.append(hidden)
        slope_up.append(slope)
    seen_down, seen_up = [front_down], [front_up]
    outs_down, outs_up = [], []
    for t in range(ticks):
        next_down = tick(seen_down[t], weight, slope_down[t : t + 1], width)
        next_up = tick(seen_up[t], weight, slope_up[t], width)
        outs_down.append(next_down)
        outs_up.append(to_mirror(next_up))
        if t + 1 < ticks:
            seen_down.append(from_next(next_down))
            seen_up.append(from_next(next_up))
    part = weight_term([hid_down, *hid_up], seen_down + seen_up, width)
    gradient = scatter_sum(part)
    old_master = master[0]
    new_first = beta_first * moment_first[0] + (1.0 - beta_first) * gradient
    new_second = beta_second * moment_second[0] + (1.0 - beta_second) * gradient * gradient
    new_master = old_master - learn_rate * (
        new_first / (jnp.sqrt(new_second) + epsilon) + decay_rate * old_master
    )
    shape = (ticks, 1, 1, height, width, channels)
    return (
        jnp.concatenate(outs_down).reshape(shape),
        jnp.concatenate(outs_up).reshape(shape),
        new_master.astype(jnp.bfloat16)[None],
        new_master[None],
        new_first[None],
        new_second[None],
    )


def solution(mesh):
    fine = Mesh(
        mesh.devices.reshape(2, 8, 2, 8, 2), ("x_lo", "z", "x_hi", "y", "core")
    )
    dp = (*CHIPS, "core")
    images = P(None, SECTION, dp, None, None, None)
    fronts = P(SECTION, dp, None, None, None)
    rows = P(SECTION, dp, None)
    return jax.shard_map(
        per_device,
        mesh=fine,
        in_specs=(images, images, fronts, fronts, rows, rows, rows),
        out_specs=(images, images, rows, rows, rows, rows),
        check_vma=False,
    )
```

time: 535 us -> 143 us (0.27)
  waiting for transfers between devices: 360 us -> 7.26 us
  local copies, waits for them, and re-layouts: 65.3 us -> 7.89 us
  matrix products: 28.5 us -> 0 us
  Pallas kernels: 0 us -> 28.2 us
  blocking collectives: 0 us -> 27.9 us
  between operations: 14.5 us -> 0.95 us
  starting transfers between devices: 56.4 us -> 63.7 us
    psum x1 -> x0, waiting for transfers between devices: 258 us -> none  [per_device(): lax.psum(term_up.astype(jnp.bfloat16), 'dp').astype(jnp.float32)]
    all_gather x2 -> x0, waiting for transfers between devices: 87.6 us -> none  [the longest x1 52.7 us: per_device(): lax.all_gather(mirror_rows, 'dp', axis=0, tiled=True)]
    unnamed x126 -> x36, local copies, waits for them, and re-layouts: 40.9 us -> 4.61 us
    dot_general x12 -> x0, matrix products: 28.5 us -> none  [the longest x6 16.8 us: section_front(): lax.dot_general(taps_front, kernel, (((1, 2), (0, 2)), ((), ())), preferr...]
    pallas_call x0 -> x11, Pallas kernels: none -> 28.2 us  [the longest x6 15.1 us: tick(): pl.pallas_call(functools.partial(tick_kernel, width, factor), grid=(n,),...]
    all_to_all x0 -> x1, blocking collectives: none -> 27.9 us  [gather_rows(): mine = lax.all_to_all(spread, CHIPS, 0, 0, tiled=True)]
    dot_general x6 -> x0, local copies, waits for them, and re-layouts: 19.1 us -> none  [section_front(): lax.dot_general(taps_front, kernel, (((1, 2), (0, 2)), ((), ())), preferr...]
    ppermute x12 -> x13, waiting for transfers between devices: 14.1 us -> 7.26 us  [the longest x7 5.03 us: to_mirror(): lax.ppermute(value, SECTION, [(i, length - 1 - i) for i in range(length)])]
  transfers between devices with their start and end apart: 15 -> 14, of which waited for: 10 -> 4; matrix products, arithmetic and copies ran while one was open for 15% -> 4% of each run, Pallas kernels for 0% -> 17%
where the time goes in v1:
time: 143 us; the launch traced here: 142 us
  starting transfers between devices  63.7 us (45%)
  Pallas kernels  28.2 us (20%)
  blocking collectives  27.9 us (20%)
  local copies, waits for them, and re-layouts  7.89 us (6%)
  waiting for transfers between devices  7.26 us (5%)
  other arithmetic  6.5 us (5%)
    ppermute x7, starting transfers between devices, to_mirror(): lax.ppermute(value, SECTION, [(i, length - 1 - i) for i in range(length)])  34.9 us
    all_to_all x1, blocking collectives, gather_rows(): mine = lax.all_to_all(spread, CHIPS, 0, 0, tiled=True)  27.9 us
    ppermute x4, starting transfers between devices, from_next(): return lax.ppermute(value, SECTION, [(i + 1, i) for i in range(length - 1)])  18.3 us
    pallas_call x6, Pallas kernels, tick(): pl.pallas_call(functools.partial(tick_kernel, width, factor), grid=(n,),...  15.1 us
    pallas_call x4, Pallas kernels, gelu_parts(): pl.pallas_call(gelu_kernel, grid=(n,), in_specs=[pl.BlockSpec((1, pixels,...  8.62 us
    all_to_all x1, starting transfers between devices, scatter_sum(): pieces = lax.all_to_all(pair, CHIPS, 0, 0, tiled=True)  6.68 us
    ppermute x7, waiting for transfers between devices, to_mirror(): lax.ppermute(value, SECTION, [(i, length - 1 - i) for i in range(length)])  5.03 us
    unnamed x36, local copies, waits for them, and re-layouts  4.61 us
  transfers between devices with their start and end apart: 14, of which 4 were waited for; matrix products, arithmetic and copies ran while one was open for 4% of the time, Pallas kernels for 17%

profile of v1, /device:TPU:6, one launch (start us, length us, event | category | flops | bytes accessed | tf_op | source)
XLA Modules:
  0.0 142.4 jit_solution(15802793526693849311)
XLA Ops:
  1.6 27.9 %all_to_all.10 = bf16[16,72,256]{2,1,0:T(8,128)(2,1)S(1)} all-to-all(bf16[16,72,256]{2,1,0:T(8,128)(2,1)S(1)} %broadcast_in_dim.5), channel_id=1, replica_groups=mesh['x_lo'=2,'z'=8,'x_hi'=2,'y'=8,'core'=2] {'x_hi','y'}, dimensions={0} | all-to-all | bytes 1179648 | tf_op jit(solution)/shard_map/all_to_all | solution.py:149
  29.5 1.9 %collective-permute-start = (bf16[16,72,256]{2,1,0:T(8,128)(2,1)S(1)}, bf16[16,72,256]{2,1,0:T(8,128)(2,1)S(1)}, u32[]{:S(2)}, u32[]{:S(2)}) collective-permute-start(bf16[16,72,256]{2,1,0:T(8,128)(2,1)S(1)} %all_to_all.10), channel_id=1, source_target_pairs={{0,1},{1,0},{2,3},{3,2},{4,5},{5,4},{6,7},{7,6},{8,9},{9,8},{10,11... | collective-permute-start | bytes 1769480 | tf_op jit(solution)/shard_map/ppermute | solution.py:143
  31.5 11.2 %collective-permute-start.3 = (bf16[1,256,256]{2,1,0:T(8,128)(2,1)S(1)}, bf16[1,256,256]{2,1,0:T(8,128)(2,1)S(1)}, u32[]{:S(2)}, u32[]{:S(2)}) collective-permute-start(bf16[1,256,256]{2,1,0:T(8,128)(2,1)S(1)} %bitcast.50), channel_id=1, source_target_pairs={{0,480},{32,448},{64,416},{96,384},{128,352},{160,320},{192,288},{... | collective-permute-start | bytes 393224 | tf_op jit(solution)/shard_map/ppermute | solution.py:134
  42.7 1.9 %collective-permute-start.4 = (bf16[1,256,256]{2,1,0:T(8,128)(2,1)S(1)}, bf16[1,256,256]{2,1,0:T(8,128)(2,1)S(1)}, u32[]{:S(2)}, u32[]{:S(2)}) collective-permute-start(bf16[1,256,256]{2,1,0:T(8,128)(2,1)S(1)} %bitcast.49), channel_id=1, source_target_pairs={{0,480},{32,448},{64,416},{96,384},{128,352},{160,320},{192,288},{... | collective-permute-start | bytes 393224 | tf_op jit(solution)/shard_map/ppermute | solution.py:134
  44.7 6.0 %collective-permute-start.7 = (bf16[1,256,256]{2,1,0:T(8,128)(2,1)S(1)}, bf16[1,256,256]{2,1,0:T(8,128)(2,1)S(1)}, u32[]{:S(2)}, u32[]{:S(2)}) collective-permute-start(bf16[1,256,256]{2,1,0:T(8,128)(2,1)S(1)} %bitcast.48), channel_id=1, source_target_pairs={{0,480},{32,448},{64,416},{96,384},{128,352},{160,320},{192,288},{... | collective-permute-start | bytes 393224 | tf_op jit(solution)/shard_map/ppermute | solution.py:134
  50.7 3.1 %gelu_parts.4 = (bf16[3,256,256]{2,1,0:T(8,128)(2,1)}, f32[3,256,256]{2,1,0:T(8,128)}) custom-call(bf16[3,256,256]{2,1,0:T(8,128)(2,1)} %bitcast.44), custom_call_target="tpu_custom_call" | custom-call | tf_op jit(solution)/shard_map/gelu_parts/pallas_call | solution.py:23
  53.8 2.0 %fusion.6 = (f32[1,256,256]{2,1,0:T(8,128)}, f32[1,256,256]{2,1,0:T(8,128)}, f32[1,256,256]{2,1,0:T(8,128)}) fusion(f32[3,256,256]{2,1,0:T(8,128)} %get-tuple-element.14), kind=kLoop, calls=%fused_computation.16 | loop fusion | bytes 1572864 | tf_op jit(solution)/shard_map/slice | solution.py:184
  55.8 2.9 %collective-permute-done.4.act_ref = bf16[1,256,256]{2,1,0:T(8,128)(2,1)S(1)} collective-permute-done((bf16[1,256,256]{2,1,0:T(8,128)(2,1)S(1)}, bf16[1,256,256]{2,1,0:T(8,128)(2,1)S(1)}, u32[]{:S(2)}, u32[]{:S(2)}) %collective-permute-start.4) | collective-permute-done | bytes 131104 | tf_op jit(solution)/shard_map/ppermute | solution.py:134
  59.4 1.8 %gelu_parts.5 = (bf16[1,256,256]{2,1,0:T(8,128)(2,1)}, f32[1,256,256]{2,1,0:T(8,128)}) custom-call(bf16[1,256,256]{2,1,0:T(8,128)(2,1)} %copy-done.12), custom_call_target="tpu_custom_call" | custom-call | tf_op jit(solution)/shard_map/gelu_parts/pallas_call | solution.py:23
  62.5 2.5 %tick.6 = bf16[1,256,256]{2,1,0:T(8,128)(2,1)} custom-call(bf16[1,256,256]{2,1,0:T(8,128)(2,1)} %bitcast.42, bf16[1,2304,256]{2,1,0:T(8,128)(2,1)} %bitcast.34, f32[1,256,256]{2,1,0:T(8,128)} %get-tuple-element.36.slope_ref), custom_call_target="tpu_custom_call" | custom-call | tf_op jit(solution)/shard_map/tick/pallas_call | solution.py:74
  65.0 5.6 %collective-permute-start.1 = (bf16[1,256,256]{2,1,0:T(8,128)(2,1)}, bf16[1,256,256]{2,1,0:T(8,128)(2,1)S(1)}, u32[]{:S(2)}, u32[]{:S(2)}) collective-permute-start(bf16[1,256,256]{2,1,0:T(8,128)(2,1)} %tick.6), channel_id=1, source_target_pairs={{32,0},{64,32},{96,64},{128,96},{160,128},{192,160},{224,192},{256... | collective-permute-start | bytes 393224 | tf_op jit(solution)/shard_map/ppermute | solution.py:139
  71.2 2.5 %tick.9 = bf16[1,256,256]{2,1,0:T(8,128)(2,1)} custom-call(bf16[1,256,256]{2,1,0:T(8,128)(2,1)} %copy-done.3, bf16[1,2304,256]{2,1,0:T(8,128)(2,1)} %bitcast.35, f32[1,256,256]{2,1,0:T(8,128)} %get-tuple-element.15.slope_ref), custom_call_target="tpu_custom_call" | custom-call | tf_op jit(solution)/shard_map/tick/pallas_call | solution.py:74
  73.7 1.9 %collective-permute-start.6 = (bf16[1,256,256]{2,1,0:T(8,128)(2,1)}, bf16[1,256,256]{2,1,0:T(8,128)(2,1)S(1)}, u32[]{:S(2)}, u32[]{:S(2)}) collective-permute-start(bf16[1,256,256]{2,1,0:T(8,128)(2,1)} %tick.9), channel_id=1, source_target_pairs={{32,0},{64,32},{96,64},{128,96},{160,128},{192,160},{224,192},{256... | collective-permute-start | bytes 393224 | tf_op jit(solution)/shard_map/ppermute | solution.py:139
  75.6 1.9 %collective-permute-start.10 = (bf16[1,256,256]{2,1,0:T(8,128)(2,1)S(1)}, bf16[1,256,256]{2,1,0:T(8,128)(2,1)S(1)}, u32[]{:S(2)}, u32[]{:S(2)}) collective-permute-start(bf16[1,256,256]{2,1,0:T(8,128)(2,1)S(1)} %bitcast.47), channel_id=1, source_target_pairs={{0,480},{32,448},{64,416},{96,384},{128,352},{160,320},{192,288},{... | collective-permute-start | bytes 393224 | tf_op jit(solution)/shard_map/ppermute | solution.py:134
  78.2 1.8 %gelu_parts.6 = (bf16[1,256,256]{2,1,0:T(8,128)(2,1)}, f32[1,256,256]{2,1,0:T(8,128)}) custom-call(bf16[1,256,256]{2,1,0:T(8,128)(2,1)} %copy-done.10), custom_call_target="tpu_custom_call" | custom-call | tf_op jit(solution)/shard_map/gelu_parts/pallas_call | solution.py:23
  80.7 2.5 %tick.7 = bf16[1,256,256]{2,1,0:T(8,128)(2,1)} custom-call(bf16[1,256,256]{2,1,0:T(8,128)(2,1)} %copy-done.6, bf16[1,2304,256]{2,1,0:T(8,128)(2,1)} %bitcast.36, f32[1,256,256]{2,1,0:T(8,128)} %get-tuple-element.35.slope_ref), custom_call_target="tpu_custom_call" | custom-call | tf_op jit(solution)/shard_map/tick/pallas_call | solution.py:74
  83.3 6.0 %collective-permute-start.2 = (bf16[1,256,256]{2,1,0:T(8,128)(2,1)}, bf16[1,256,256]{2,1,0:T(8,128)(2,1)S(1)}, u32[]{:S(2)}, u32[]{:S(2)}) collective-permute-start(bf16[1,256,256]{2,1,0:T(8,128)(2,1)} %tick.7), channel_id=1, source_target_pairs={{32,0},{64,32},{96,64},{128,96},{160,128},{192,160},{224,192},{256... | collective-permute-start | bytes 393224 | tf_op jit(solution)/shard_map/ppermute | solution.py:139
  90.0 2.5 %tick.10 = bf16[1,256,256]{2,1,0:T(8,128)(2,1)} custom-call(bf16[1,256,256]{2,1,0:T(8,128)(2,1)} %copy-done.7, bf16[1,2304,256]{2,1,0:T(8,128)(2,1)} %bitcast.37, f32[1,256,256]{2,1,0:T(8,128)} %get-tuple-element.16.slope_ref), custom_call_target="tpu_custom_call" | custom-call | tf_op jit(solution)/shard_map/tick/pallas_call | solution.py:74
  92.5 4.8 %collective-permute-start.9 = (bf16[1,256,256]{2,1,0:T(8,128)(2,1)}, bf16[1,256,256]{2,1,0:T(8,128)(2,1)S(1)}, u32[]{:S(2)}, u32[]{:S(2)}) collective-permute-start(bf16[1,256,256]{2,1,0:T(8,128)(2,1)} %tick.10), channel_id=1, source_target_pairs={{32,0},{64,32},{96,64},{128,96},{160,128},{192,160},{224,192},{256... | collective-permute-start | bytes 393224 | tf_op jit(solution)/shard_map/ppermute | solution.py:139
  98.0 1.9 %gelu_parts.7 = (bf16[1,256,256]{2,1,0:T(8,128)(2,1)}, f32[1,256,256]{2,1,0:T(8,128)}) custom-call(bf16[1,256,256]{2,1,0:T(8,128)(2,1)} %copy-done.11), custom_call_target="tpu_custom_call" | custom-call | tf_op jit(solution)/shard_map/gelu_parts/pallas_call | solution.py:23
  100.8 4.5 %weight_term.1 = bf16[2304,256]{1,0:T(8,128)(2,1)} custom-call(bf16[3,256,256]{2,1,0:T(8,128)(2,1)} %get-tuple-element.18.refs_0_, bf16[1,256,256]{2,1,0:T(8,128)(2,1)} %get-tuple-element.19.refs_1_, bf16[1,256,256]{2,1,0:T(8,128)(2,1)} %get-tuple-element.20.refs_2_, bf16[1,256,256]{2,1,0:T(8,128)(2,1)} %get-tuple-element.21.refs_3_, ...), custom_call_target="tpu_custom_call" | custom-call | tf_op jit(solution)/shard_map/weight_term/pallas_call | solution.py:112
  105.3 1.2 dynamic-slice_bitcast_fusion
  106.5 1.9 %collective-permute-start.12 = (bf16[16,72,256]{2,1,0:T(8,128)(2,1)S(1)}, bf16[16,72,256]{2,1,0:T(8,128)(2,1)S(1)}, u32[]{:S(2)}, u32[]{:S(2)}) collective-permute-start(bf16[16,72,256]{2,1,0:T(8,128)(2,1)S(1)} %dynamic-slice_bitcast_fusion), channel_id=1, source_target_pairs={{0,1},{1,0},{2,3},{3,2},{4,5},{5,4},{6,7},{7,6},{8,9},{9,8},{10,11... | collective-permute-start | bytes 1769480 | tf_op jit(solution)/shard_map/ppermute | solution.py:143
  108.4 1.9 %collective-permute-done.12 = bf16[16,72,256]{2,1,0:T(8,128)(2,1)S(1)} collective-permute-done((bf16[16,72,256]{2,1,0:T(8,128)(2,1)S(1)}, bf16[16,72,256]{2,1,0:T(8,128)(2,1)S(1)}, u32[]{:S(2)}, u32[]{:S(2)}) %collective-permute-start.12) | collective-permute-done | bytes 589856 | tf_op jit(solution)/shard_map/ppermute | solution.py:143
  111.4 6.7 %all-to-all-start.1 = ((bf16[16,72,256]{2,1,0:T(8,128)(2,1)}), bf16[16,72,256]{2,1,0:T(8,128)(2,1)S(1)}, u32[]{:S(2)}, u32[]{:S(2)}) async-start(bf16[16,72,256]{2,1,0:T(8,128)(2,1)} %fusion), calls=%async_computation.1 | async-start | bytes 1179648 | tf_op jit(solution)/shard_map/all_to_all | solution.py:163
  118.0 5.7 %collective-permute-start.5 = (bf16[1,256,256]{2,1,0:T(8,128)(2,1)S(1)}, bf16[1,256,256]{2,1,0:T(8,128)(2,1)S(1)}, u32[]{:S(2)}, u32[]{:S(2)}) collective-permute-start(bf16[1,256,256]{2,1,0:T(8,128)(2,1)S(1)} %copy-done.13), channel_id=1, source_target_pairs={{0,480},{32,448},{64,416},{96,384},{128,352},{160,320},{192,288},{... | collective-permute-start | bytes 393224 | tf_op jit(solution)/shard_map/ppermute | solution.py:134
  123.8 2.2 %collective-permute-start.8 = (bf16[1,256,256]{2,1,0:T(8,128)(2,1)S(1)}, bf16[1,256,256]{2,1,0:T(8,128)(2,1)S(1)}, u32[]{:S(2)}, u32[]{:S(2)}) collective-permute-start(bf16[1,256,256]{2,1,0:T(8,128)(2,1)S(1)} %copy-done.14), channel_id=1, source_target_pairs={{0,480},{32,448},{64,416},{96,384},{128,352},{160,320},{192,288},{... | collective-permute-start | bytes 393224 | tf_op jit(solution)/shard_map/ppermute | solution.py:134
  126.0 2.5 %tick.11 = bf16[1,256,256]{2,1,0:T(8,128)(2,1)} custom-call(bf16[1,256,256]{2,1,0:T(8,128)(2,1)} %copy-done.5, bf16[1,2304,256]{2,1,0:T(8,128)(2,1)} %bitcast.38, f32[1,256,256]{2,1,0:T(8,128)} %get-tuple-element.17.slope_ref), custom_call_target="tpu_custom_call" | custom-call | tf_op jit(solution)/shard_map/tick/pallas_call | solution.py:74
  128.5 5.9 %collective-permute-start.11 = (bf16[1,256,256]{2,1,0:T(8,128)(2,1)}, bf16[1,256,256]{2,1,0:T(8,128)(2,1)S(1)}, u32[]{:S(2)}, u32[]{:S(2)}) collective-permute-start(bf16[1,256,256]{2,1,0:T(8,128)(2,1)} %tick.11), channel_id=1, source_target_pairs={{0,480},{32,448},{64,416},{96,384},{128,352},{160,320},{192,288},{... | collective-permute-start | bytes 393224 | tf_op jit(solution)/shard_map/ppermute | solution.py:134
  134.4 2.5 %tick.8 = bf16[1,256,256]{2,1,0:T(8,128)(2,1)} custom-call(bf16[1,256,256]{2,1,0:T(8,128)(2,1)} %copy-done.4, bf16[1,2304,256]{2,1,0:T(8,128)(2,1)} %bitcast.39, f32[1,256,256]{2,1,0:T(8,128)} %get-tuple-element.34.slope_ref), custom_call_target="tpu_custom_call" | custom-call | tf_op jit(solution)/shard_map/tick/pallas_call | solution.py:74
  137.0 1.7 %pad_maximum_fusion.1 = bf16[3,256,256]{2,1,0:T(8,128)(2,1)} fusion(bf16[1,256,256]{2,1,0:T(8,128)(2,1)} %tick.8, bf16[1,256,256]{2,1,0:T(8,128)(2,1)S(1)} %copy-done.2, bf16[1,256,256]{2,1,0:T(8,128)(2,1)S(1)} %copy-done.1), kind=kLoop, calls=%fused_computation.7 | loop fusion | flops 393216 | bytes 786432 | tf_op jit(solution)/shard_map/concatenate | solution.py:201
  138.7 2.1 %collective-permute-done.11 = bf16[1,256,256]{2,1,0:T(8,128)(2,1)S(1)} collective-permute-done((bf16[1,256,256]{2,1,0:T(8,128)(2,1)}, bf16[1,256,256]{2,1,0:T(8,128)(2,1)S(1)}, u32[]{:S(2)}, u32[]{:S(2)}) %collective-permute-start.11) | collective-permute-done | bytes 131104 | tf_op jit(solution)/shard_map/ppermute | solution.py:134
  (56 shorter events, 9.7 us)
Async XLA Ops:
  0.6 30.8 %copy-start.17 = (bf16[1,1,16,16,256]{4,3,2,1,0:T(8,128)(2,1)S(1)}, bf16[1,1,16,16,256]{4,3,2,1,0:T(8,128)(2,1)}, u32[]{:S(2)}) copy-start(bf16[1,1,16,16,256]{4,3,2,1,0:T(8,128)(2,1)} %param.10) | copy-start | bytes 393220
  0.6 42.1 %copy-start.8 = (bf16[3,1,1,16,16,256]{5,4,3,2,1,0:T(8,128)(2,1)S(1)}, bf16[3,1,1,16,16,256]{5,4,3,2,1,0:T(8,128)(2,1)}, u32[]{:S(2)}) copy-start(bf16[3,1,1,16,16,256]{5,4,3,2,1,0:T(8,128)(2,1)} %param.8) | copy-start | bytes 1179652
  29.5 31.7 %collective-permute-start = (bf16[16,72,256]{2,1,0:T(8,128)(2,1)S(1)}, bf16[16,72,256]{2,1,0:T(8,128)(2,1)S(1)}, u32[]{:S(2)}, u32[]{:S(2)}) collective-permute-start(bf16[16,72,256]{2,1,0:T(8,128)(2,1)S(1)} %all_to_all.10), channel_id=1, source_target_pairs={{0,1},{1,0},{2,3},{3,2},{4,5},{5,4},{6,7},{7,6},{8,9},{9,8},{10,11... | collective-permute-start | bytes 1769480 | tf_op jit(solution)/shard_map/ppermute | solution.py:143
  31.5 39.1 %collective-permute-start.3 = (bf16[1,256,256]{2,1,0:T(8,128)(2,1)S(1)}, bf16[1,256,256]{2,1,0:T(8,128)(2,1)S(1)}, u32[]{:S(2)}, u32[]{:S(2)}) collective-permute-start(bf16[1,256,256]{2,1,0:T(8,128)(2,1)S(1)} %bitcast.50), channel_id=1, source_target_pairs={{0,480},{32,448},{64,416},{96,384},{128,352},{160,320},{192,288},{... | collective-permute-start | bytes 393224 | tf_op jit(solution)/shard_map/ppermute | solution.py:134
  42.7 16.0 %collective-permute-start.4 = (bf16[1,256,256]{2,1,0:T(8,128)(2,1)S(1)}, bf16[1,256,256]{2,1,0:T(8,128)(2,1)S(1)}, u32[]{:S(2)}, u32[]{:S(2)}) collective-permute-start(bf16[1,256,256]{2,1,0:T(8,128)(2,1)S(1)} %bitcast.49), channel_id=1, source_target_pairs={{0,480},{32,448},{64,416},{96,384},{128,352},{160,320},{192,288},{... | collective-permute-start | bytes 393224 | tf_op jit(solution)/shard_map/ppermute | solution.py:134
  44.7 32.9 %collective-permute-start.7 = (bf16[1,256,256]{2,1,0:T(8,128)(2,1)S(1)}, bf16[1,256,256]{2,1,0:T(8,128)(2,1)S(1)}, u32[]{:S(2)}, u32[]{:S(2)}) collective-permute-start(bf16[1,256,256]{2,1,0:T(8,128)(2,1)S(1)} %bitcast.48), channel_id=1, source_target_pairs={{0,480},{32,448},{64,416},{96,384},{128,352},{160,320},{192,288},{... | collective-permute-start | bytes 393224 | tf_op jit(solution)/shard_map/ppermute | solution.py:134
  58.7 0.6 copy-start.12
  65.0 15.1 %collective-permute-start.1 = (bf16[1,256,256]{2,1,0:T(8,128)(2,1)}, bf16[1,256,256]{2,1,0:T(8,128)(2,1)S(1)}, u32[]{:S(2)}, u32[]{:S(2)}) collective-permute-start(bf16[1,256,256]{2,1,0:T(8,128)(2,1)} %tick.6), channel_id=1, source_target_pairs={{32,0},{64,32},{96,64},{128,96},{160,128},{192,160},{224,192},{256... | collective-permute-start | bytes 393224 | tf_op jit(solution)/shard_map/ppermute | solution.py:139
  70.6 0.6 copy-start.3
  73.7 15.6 %collective-permute-start.6 = (bf16[1,256,256]{2,1,0:T(8,128)(2,1)}, bf16[1,256,256]{2,1,0:T(8,128)(2,1)S(1)}, u32[]{:S(2)}, u32[]{:S(2)}) collective-permute-start(bf16[1,256,256]{2,1,0:T(8,128)(2,1)} %tick.9), channel_id=1, source_target_pairs={{32,0},{64,32},{96,64},{128,96},{160,128},{192,160},{224,192},{256... | collective-permute-start | bytes 393224 | tf_op jit(solution)/shard_map/ppermute | solution.py:139
  75.6 21.6 %collective-permute-start.10 = (bf16[1,256,256]{2,1,0:T(8,128)(2,1)S(1)}, bf16[1,256,256]{2,1,0:T(8,128)(2,1)S(1)}, u32[]{:S(2)}, u32[]{:S(2)}) collective-permute-start(bf16[1,256,256]{2,1,0:T(8,128)(2,1)S(1)} %bitcast.47), channel_id=1, source_target_pairs={{0,480},{32,448},{64,416},{96,384},{128,352},{160,320},{192,288},{... | collective-permute-start | bytes 393224 | tf_op jit(solution)/shard_map/ppermute | solution.py:134
  77.6 0.7 copy-start.10
  80.1 0.6 copy-start.6
  83.3 16.6 %collective-permute-start.2 = (bf16[1,256,256]{2,1,0:T(8,128)(2,1)}, bf16[1,256,256]{2,1,0:T(8,128)(2,1)S(1)}, u32[]{:S(2)}, u32[]{:S(2)}) collective-permute-start(bf16[1,256,256]{2,1,0:T(8,128)(2,1)} %tick.7), channel_id=1, source_target_pairs={{32,0},{64,32},{96,64},{128,96},{160,128},{192,160},{224,192},{256... | collective-permute-start | bytes 393224 | tf_op jit(solution)/shard_map/ppermute | solution.py:139
  89.3 0.7 copy-start.7
  92.5 7.6 %collective-permute-start.9 = (bf16[1,256,256]{2,1,0:T(8,128)(2,1)}, bf16[1,256,256]{2,1,0:T(8,128)(2,1)S(1)}, u32[]{:S(2)}, u32[]{:S(2)}) collective-permute-start(bf16[1,256,256]{2,1,0:T(8,128)(2,1)} %tick.10), channel_id=1, source_target_pairs={{32,0},{64,32},{96,64},{128,96},{160,128},{192,160},{224,192},{256... | collective-permute-start | bytes 393224 | tf_op jit(solution)/shard_map/ppermute | solution.py:139
  97.3 0.7 copy-start.11
  99.8 0.7 copy-start.4
  100.1 0.7 copy-start.5
  105.3 5.1 %copy-start = (bf16[2304,256]{1,0:T(8,128)(2,1)S(1)}, bf16[2304,256]{1,0:T(8,128)(2,1)}, u32[]{:S(2)}) copy-start(bf16[2304,256]{1,0:T(8,128)(2,1)} %weight_term.1) | copy-start | bytes 3538948
  106.5 3.9 %collective-permute-start.12 = (bf16[16,72,256]{2,1,0:T(8,128)(2,1)S(1)}, bf16[16,72,256]{2,1,0:T(8,128)(2,1)S(1)}, u32[]{:S(2)}, u32[]{:S(2)}) collective-permute-start(bf16[16,72,256]{2,1,0:T(8,128)(2,1)S(1)} %dynamic-slice_bitcast_fusion), channel_id=1, source_target_pairs={{0,1},{1,0},{2,3},{3,2},{4,5},{5,4},{6,7},{7,6},{8,9},{9,8},{10,11... | collective-permute-start | bytes 1769480 | tf_op jit(solution)/shard_map/ppermute | solution.py:143
  108.4 9.6 %copy-start.13 = (bf16[1,256,256]{2,1,0:T(8,128)(2,1)S(1)}, bf16[1,256,256]{2,1,0:T(8,128)(2,1)}, u32[]{:S(2)}) copy-start(bf16[1,256,256]{2,1,0:T(8,128)(2,1)} %tick.9) | copy-start | bytes 393220
  108.4 15.4 %copy-start.14 = (bf16[1,256,256]{2,1,0:T(8,128)(2,1)S(1)}, bf16[1,256,256]{2,1,0:T(8,128)(2,1)}, u32[]{:S(2)}) copy-start(bf16[1,256,256]{2,1,0:T(8,128)(2,1)} %tick.10) | copy-start | bytes 393220
  111.4 30.2 %all-to-all-start.1 = ((bf16[16,72,256]{2,1,0:T(8,128)(2,1)}), bf16[16,72,256]{2,1,0:T(8,128)(2,1)S(1)}, u32[]{:S(2)}, u32[]{:S(2)}) async-start(bf16[16,72,256]{2,1,0:T(8,128)(2,1)} %fusion), calls=%async_computation.1 | async-start | bytes 1179648 | tf_op jit(solution)/shard_map/all_to_all | solution.py:163
  118.0 20.7 %collective-permute-start.5 = (bf16[1,256,256]{2,1,0:T(8,128)(2,1)S(1)}, bf16[1,256,256]{2,1,0:T(8,128)(2,1)S(1)}, u32[]{:S(2)}, u32[]{:S(2)}) collective-permute-start(bf16[1,256,256]{2,1,0:T(8,128)(2,1)S(1)} %copy-done.13), channel_id=1, source_target_pairs={{0,480},{32,448},{64,416},{96,384},{128,352},{160,320},{192,288},{... | collective-permute-start | bytes 393224 | tf_op jit(solution)/shard_map/ppermute | solution.py:134
  123.8 14.9 %collective-permute-start.8 = (bf16[1,256,256]{2,1,0:T(8,128)(2,1)S(1)}, bf16[1,256,256]{2,1,0:T(8,128)(2,1)S(1)}, u32[]{:S(2)}, u32[]{:S(2)}) collective-permute-start(bf16[1,256,256]{2,1,0:T(8,128)(2,1)S(1)} %copy-done.14), channel_id=1, source_target_pairs={{0,480},{32,448},{64,416},{96,384},{128,352},{160,320},{192,288},{... | collective-permute-start | bytes 393224 | tf_op jit(solution)/shard_map/ppermute | solution.py:134
  128.5 8.4 %copy-start.1 = (bf16[1,256,256]{2,1,0:T(8,128)(2,1)S(1)}, bf16[1,256,256]{2,1,0:T(8,128)(2,1)}, u32[]{:S(2)}) copy-start(bf16[1,256,256]{2,1,0:T(8,128)(2,1)} %tick.6) | copy-start | bytes 393220
  128.5 8.4 %copy-start.2 = (bf16[1,256,256]{2,1,0:T(8,128)(2,1)S(1)}, bf16[1,256,256]{2,1,0:T(8,128)(2,1)}, u32[]{:S(2)}) copy-start(bf16[1,256,256]{2,1,0:T(8,128)(2,1)} %tick.7) | copy-start | bytes 393220
  128.5 12.3 %collective-permute-start.11 = (bf16[1,256,256]{2,1,0:T(8,128)(2,1)}, bf16[1,256,256]{2,1,0:T(8,128)(2,1)S(1)}, u32[]{:S(2)}, u32[]{:S(2)}) collective-permute-start(bf16[1,256,256]{2,1,0:T(8,128)(2,1)} %tick.11), channel_id=1, source_target_pairs={{0,480},{32,448},{64,416},{96,384},{128,352},{160,320},{192,288},{... | collective-permute-start | bytes 393224 | tf_op jit(solution)/shard_map/ppermute | solution.py:134
  136.9 4.7 %copy-start.9 = (f32[1,72,256]{2,1,0:T(8,128)S(1)}, f32[1,72,256]{2,1,0:T(8,128)}, u32[]{:S(2)}) copy-start(f32[1,72,256]{2,1,0:T(8,128)} %param.11) | copy-start | bytes 221188
  137.0 4.8 %copy-start.15 = (f32[1,72,256]{2,1,0:T(8,128)S(1)}, f32[1,72,256]{2,1,0:T(8,128)}, u32[]{:S(2)}) copy-start(f32[1,72,256]{2,1,0:T(8,128)} %param.13) | copy-start | bytes 221188
  137.0 4.8 %copy-start.16 = (f32[1,72,256]{2,1,0:T(8,128)S(1)}, f32[1,72,256]{2,1,0:T(8,128)}, u32[]{:S(2)}) copy-start(f32[1,72,256]{2,1,0:T(8,128)} %param.12) | copy-start | bytes 221188

commit v2 on v1

v2 whole, which is shorter than its diff:
```python
import functools
import jax
import jax.numpy as jnp
from jax import lax
from jax.experimental import pallas as pl
from jax.experimental.pallas import tpu as pltpu
from jax.sharding import Mesh, PartitionSpec as P


VMEM = pl.BlockSpec(memory_space=pltpu.VMEM)
SMEM = pl.BlockSpec(memory_space=pltpu.SMEM)


def on_chip(value):
    return pltpu.with_memory_space_constraint(value, pltpu.VMEM)


def call(body, outs, args, scratch=(), scalars=0, alias=None):
    specs = [SMEM] * scalars + [VMEM] * (len(args) - scalars)
    args = [*args[:scalars], *map(on_chip, args[scalars:])]
    return pl.pallas_call(
        body,
        in_specs=specs,
        out_specs=[VMEM] * len(outs),
        out_shape=[pltpu.VMEM(shape, dtype) for shape, dtype in outs],
        scratch_shapes=list(scratch),
        input_output_aliases=alias or {},
        compiler_params=pltpu.CompilerParams(vmem_limit_bytes=16 << 20),
    )(*args)


def gelu_kernel(act_ref, hid_ref, slope_ref):
    for t in range(act_ref.shape[0]):
        x = act_ref[t].astype(jnp.float32)
        cube = 0.044715 * x * x * x
        bent = jnp.tanh(0.7978845608028654 * (x + cube))
        half = 0.5 * (1.0 + bent)
        hidden = (x * half).astype(jnp.bfloat16)
        hid_ref[t] = hidden.astype(jnp.float32).T.astype(jnp.bfloat16)
        inner = 0.7978845608028654 * (1.0 + 3.0 * 0.044715 * x * x)
        slope_ref[t] = half + 0.5 * x * (1.0 - bent * bent) * inner


def gelu_parts(acts):
    n, pixels, channels = acts.shape
    outs = [((n, channels, pixels), jnp.bfloat16), ((n, pixels, channels), jnp.float32)]
    return call(gelu_kernel, outs, [acts])


def fill_taps(front, pad_ref, width):
    pixels = front.shape[0]
    wide = front.astype(jnp.float32)
    column = lax.broadcasted_iota(jnp.int32, wide.shape, 0) % width
    after = jnp.where(column == width - 1, 0.0, pltpu.roll(wide, pixels - 1, 0))
    before = jnp.where(column == 0, 0.0, pltpu.roll(wide, 1, 0))
    empty = jnp.zeros((width, front.shape[1]), jnp.bfloat16)
    for b, piece in enumerate((after.astype(jnp.bfloat16), front, before.astype(jnp.bfloat16))):
        pad_ref[b, 0:width] = empty
        pad_ref[b, width : width + pixels] = piece
        pad_ref[b, width + pixels : 2 * width + pixels] = empty


def pads(count, pixels, width, channels):
    return pltpu.VMEM((count, 3, pixels + 2 * width, channels), jnp.bfloat16)


def tick_kernel(t, width, factor, front_ref, weight_ref, slope_ref, *refs):
    earlier, (out_ref, *pair, pad_ref) = refs[: len(refs) // 2 - 1], refs[len(refs) // 2 - 1 :]
    front = front_ref[...]
    pixels, channels = front.shape
    fill_taps(front, pad_ref.at[0], width)
    total = jnp.zeros((pixels, channels), jnp.float32)
    for a in range(3):
        for b in range(3):
            row = (3 * a + b) * channels
            total += lax.dot_general(
                pad_ref[0, b, (2 - a) * width : (2 - a) * width + pixels],
                weight_ref[row : row + channels],
                (((1,), (1,)), ((), ())),
                preferred_element_type=jnp.float32,
            )
    out = (front.astype(jnp.float32) + slope_ref[t] * (factor * total)).astype(jnp.bfloat16)
    out_ref[...] = out
    if pair:
        pair[0][0] = earlier[0][...]
        pair[0][1] = out


def tick(front, weight, slopes, t, width, earlier=None):
    pixels, channels = front.shape
    factor = (9 * channels) ** -0.5
    outs = [(front.shape, jnp.bfloat16)]
    args = [front, weight, slopes]
    if earlier is not None:
        outs.append(((2, *front.shape), jnp.bfloat16))
        args.append(earlier)
    return call(
        functools.partial(tick_kernel, t, width, factor),
        outs,
        args,
        [pads(1, pixels, width, channels)],
    )


def add_terms(hiddens, front_refs, pad_ref, width, write):
    for j, front_ref in enumerate(front_refs):
        fill_taps(front_ref[...], pad_ref.at[j], width)
    channels, pixels = hiddens[0].shape
    for a in range(3):
        for b in range(3):
            total = jnp.zeros((channels, channels), jnp.float32)
            for j, hidden in enumerate(hiddens):
                total += lax.dot_general(
                    hidden[...],
                    pad_ref[j, b, (2 - a) * width : (2 - a) * width + pixels],
                    (((1,), (0,)), ((), ())),
                    preferred_element_type=jnp.float32,
                )
            write((3 * a + b) * channels, total)


def early_kernel(ticks, width, hid_down_ref, hid_up_ref, *refs):
    front_refs, (out_ref, pad_ref) = refs[:-2], refs[-2:]
    hiddens = [hid_down_ref.at[t] for t in ticks] + [hid_up_ref.at[t] for t in ticks]

    def write(row, total):
        out_ref[row : row + total.shape[0]] = total

    add_terms(hiddens, front_refs, pad_ref, width, write)


def early_terms(hid_down, hid_up, fronts, ticks, width):
    channels, pixels = hid_down.shape[1:]
    return call(
        functools.partial(early_kernel, ticks, width),
        [((9 * channels, channels), jnp.float32)],
        [hid_down, hid_up, *fronts],
        [pads(len(fronts), pixels, width, channels)],
    )[0]


def last_kernel(t, width, factor, core_ref, hid_down_ref, hid_up_ref, total_ref, *refs):
    front_refs, (kept_ref, given_ref, sum_ref, pad_ref) = refs[:-4], refs[-4:]
    rows = kept_ref.shape[1]

    def write(row, total):
        at = slice(row, row + total.shape[0])
        sum_ref[at] = factor * (total_ref[at] + total)

    add_terms([hid_down_ref.at[t], hid_up_ref.at[t]], front_refs, pad_ref, width, write)
    for core, places in enumerate(((kept_ref, given_ref), (given_ref, kept_ref))):

        @pl.when(core_ref[0] == core)
        def _():
            for i in range(2 * kept_ref.shape[0]):
                places[i % 2][i // 2] = sum_ref[i * rows : (i + 1) * rows].astype(jnp.bfloat16)


def last_terms(core, hid_down, hid_up, total, fronts, t, chips, width):
    channels, pixels = hid_down.shape[1:]
    half = (chips, 9 * channels // (2 * chips), channels)
    return call(
        functools.partial(last_kernel, t, width, (9 * channels) ** -0.5),
        [(half, jnp.bfloat16), (half, jnp.bfloat16)],
        [core, hid_down, hid_up, total, *fronts],
        [pltpu.VMEM((9 * channels, channels), jnp.float32), pads(len(fronts), pixels, width, channels)],
        scalars=1,
    )


def weave_kernel(core_ref, mine_ref, other_ref, out_ref):
    core = core_ref[0]
    for i in range(mine_ref.shape[0]):
        out_ref[i, core] = mine_ref[i]
        out_ref[i, 1 - core] = other_ref[i]


def weave(core, mine, other):
    chips, rows, channels = mine.shape
    whole = call(
        weave_kernel, [((chips, 2, rows, channels), jnp.bfloat16)], [core, mine, other], scalars=1
    )[0]
    return whole.reshape(-1, channels)


beta_first = 0.9
beta_second = 0.95
learn_rate = 0.01
decay_rate = 0.1
epsilon = 1e-08

SECTION = ("x_lo", "z")
CHIPS = ("x_hi", "y")


def to_mirror(value):
    length = lax.axis_size(SECTION)
    return lax.ppermute(value, SECTION, [(i, length - 1 - i) for i in range(length)])


def from_next(value):
    length = lax.axis_size(SECTION)
    return lax.ppermute(value, SECTION, [(i + 1, i) for i in range(length - 1)])


def to_partner(value):
    return lax.ppermute(value, "core", [(0, 1), (1, 0)])


def step(acts_down, acts_up, front_down, front_up, master, moment_first, moment_second):
    ticks, _, _, height, width, channels = acts_down.shape
    flat = (height * width, channels)
    chips = lax.axis_size(CHIPS)
    core = lax.axis_index("core").astype(jnp.int32).reshape(1)
    front_up = to_mirror(front_up.reshape(flat))
    acts_up = to_mirror(acts_up.reshape(ticks, *flat))
    rows = master[0].astype(jnp.bfloat16)
    mine = lax.all_to_all(jnp.broadcast_to(rows[None], (chips, *rows.shape)), CHIPS, 0, 0, tiled=True)
    hid_down, slope_down = gelu_parts(acts_down.reshape(ticks, *flat))
    hid_up, slope_up = gelu_parts(acts_up)
    other = to_partner(mine)
    weight = weave(core, mine, other)
    down, up = [front_down.reshape(flat)], [front_up]
    outs_down, outs_up = [], []
    for t in range(ticks):
        next_down = tick(down[t], weight, slope_down, t, width)[0]
        if t == 1:
            next_up, pair = tick(up[t], weight, slope_up, t, width, outs_up[0])
        else:
            next_up = tick(up[t], weight, slope_up, t, width)[0]
        outs_down.append(next_down)
        outs_up.append(next_up)
        if t + 1 < ticks:
            down.append(from_next(next_down))
            up.append(from_next(next_up))
    total = early_terms(hid_down, hid_up, down[:2] + up[:2], (0, 1), width)
    pair = to_mirror(pair)
    kept, given = last_terms(core, hid_down, hid_up, total, [down[2], up[2]], 2, chips, width)
    taken = to_partner(given)
    both = (kept.astype(jnp.float32) + taken.astype(jnp.float32)).astype(jnp.bfloat16)
    pieces = lax.all_to_all(both, CHIPS, 0, 0, tiled=True)
    last = to_mirror(outs_up[2])
    gradient = jnp.sum(pieces.astype(jnp.float32), axis=0)
    old_master = master[0]
    new_first = beta_first * moment_first[0] + (1.0 - beta_first) * gradient
    new_second = beta_second * moment_second[0] + (1.0 - beta_second) * gradient * gradient
    new_master = old_master - learn_rate * (
        new_first / (jnp.sqrt(new_second) + epsilon) + decay_rate * old_master
    )
    shape = (ticks, 1, 1, height, width, channels)
    return (
        jnp.stack(outs_down).reshape(shape),
        jnp.concatenate([pair, last[None]]).reshape(shape),
        new_master.astype(jnp.bfloat16)[None],
        new_master[None],
        new_first[None],
        new_second[None],
    )


def solution(mesh):
    fine = Mesh(
        mesh.devices.reshape(2, 8, 2, 8, 2), ("x_lo", "z", "x_hi", "y", "core")
    )
    dp = (*CHIPS, "core")
    images = P(None, SECTION, dp, None, None, None)
    fronts = P(SECTION, dp, None, None, None)
    rows = P(SECTION, dp, None)
    return jax.shard_map(
        step,
        mesh=fine,
        in_specs=(images, images, fronts, fronts, rows, rows, rows),
        out_specs=(images, images, rows, rows, rows, rows),
        check_vma=False,
    )
```

time: 143 us -> 132 us (0.923)
  waiting for transfers between devices: 7.26 us -> 37.8 us
  Pallas kernels: 28.2 us -> 6.87 us
  starting transfers between devices: 63.7 us -> 48.9 us
  local copies, waits for them, and re-layouts: 7.89 us -> 3.74 us
    ppermute x7 -> x4, waiting for transfers between devices: 5.03 us -> 31.6 us  [to_mirror(): lax.ppermute(value, SECTION, [(i, length - 1 - i) for i in range(length)])]
    pallas_call x11, Pallas kernels: 28.2 us -> 6.87 us  [call(): pl.pallas_call(body, in_specs=specs, out_specs=[VMEM] * len(outs), out_sh...]
    ppermute x7 -> x4, starting transfers between devices: 34.9 us -> 21.2 us  [to_mirror(): lax.ppermute(value, SECTION, [(i, length - 1 - i) for i in range(length)])]
    ppermute x4, waiting for transfers between devices: 0.28 us -> 4.17 us  [from_next(): return lax.ppermute(value, SECTION, [(i + 1, i) for i in range(length - 1)])]
    slice x2 -> x0, local copies, waits for them, and re-layouts: 2.05 us -> none  [the longest x1 2.02 us: per_device(): next_down = tick(seen_down[t], weight, slope_down[t:t + 1], width)]
    concatenate x2 -> x1, other arithmetic: 2.53 us -> 0.78 us  [step(): jnp.concatenate([pair, last[None]]).reshape(shape)]
    ppermute x4, starting transfers between devices: 18.3 us -> 16.6 us  [from_next(): return lax.ppermute(value, SECTION, [(i + 1, i) for i in range(length - 1)])]
    unnamed x36 -> x28, local copies, waits for them, and re-layouts: 4.61 us -> 3.7 us
  transfers between devices with their start and end apart: 14 -> 11, of which waited for: 4 -> 6; matrix products, arithmetic and copies ran while one was open for 4% -> 1% of each run, Pallas kernels for 17% -> 4%
where the time goes in v2:
time: 132 us
  starting transfers between devices  48.9 us (37%)
  waiting for transfers between devices  37.8 us (29%)
  blocking collectives  27.9 us (21%)
  Pallas kernels  6.87 us (5%)
  other arithmetic  5.38 us (4%)
  local copies, waits for them, and re-layouts  3.74 us (3%)
    ppermute x4, waiting for transfers between devices, to_mirror(): lax.ppermute(value, SECTION, [(i, length - 1 - i) for i in range(length)])  31.6 us
    all_to_all x1, blocking collectives, step(): lax.all_to_all(jnp.broadcast_to(rows[None], (chips, *rows.shape)), CHIPS,...  27.9 us
    ppermute x4, starting transfers between devices, to_mirror(): lax.ppermute(value, SECTION, [(i, length - 1 - i) for i in range(length)])  21.2 us
    ppermute x4, starting transfers between devices, from_next(): return lax.ppermute(value, SECTION, [(i + 1, i) for i in range(length - 1)])  16.6 us
    all_to_all x1, starting transfers between devices, step(): pieces = lax.all_to_all(both, CHIPS, 0, 0, tiled=True)  7.29 us
    pallas_call x11, Pallas kernels, call(): pl.pallas_call(body, in_specs=specs, out_specs=[VMEM] * len(outs), out_sh...  6.87 us
    ppermute x4, waiting for transfers between devices, from_next(): return lax.ppermute(value, SECTION, [(i + 1, i) for i in range(length - 1)])  4.17 us
    ppermute x2, starting transfers between devices, to_partner(): return lax.ppermute(value, 'core', [(0, 1), (1, 0)])  3.83 us
  transfers between devices with their start and end apart: 11, of which 6 were waited for; matrix products, arithmetic and copies ran while one was open for 1% of the time, Pallas kernels for 4%

profile of v2, /device:TPU:6, one launch (start us, length us, event | category | flops | bytes accessed | tf_op | source)
XLA Modules:
  0.0 131.6 jit_solution(16261317398981325352)
XLA Ops:
  0.7 1.0 convert_bitcast_fusion
  1.7 27.9 %all_to_all.10.mine_ref = bf16[16,72,256]{2,1,0:T(8,128)(2,1)S(1)} all-to-all(bf16[16,72,256]{2,1,0:T(8,128)(2,1)S(1)} %broadcast_in_dim.5), channel_id=1, replica_groups=mesh['x_lo'=2,'z'=8,'x_hi'=2,'y'=8,'core'=2] {'x_hi','y'}, dimensions={0} | all-to-all | bytes 1179648 | tf_op jit(solution)/shard_map/all_to_all | solution.py:218
  29.6 1.9 %collective-permute-start = (bf16[16,72,256]{2,1,0:T(8,128)(2,1)S(1)}, bf16[16,72,256]{2,1,0:T(8,128)(2,1)S(1)}, u32[]{:S(2)}, u32[]{:S(2)}) collective-permute-start(bf16[16,72,256]{2,1,0:T(8,128)(2,1)S(1)} %all_to_all.10.mine_ref), channel_id=1, source_target_pairs={{0,1},{1,0},{2,3},{3,2},{4,5},{5,4},{6,7},{7,6},{8,9},{9,8},{10,11... | collective-permute-start | bytes 1769480 | tf_op jit(solution)/shard_map/ppermute | solution.py:207
  31.5 11.2 %collective-permute-start.4 = (bf16[3,256,256]{2,1,0:T(8,128)(2,1)S(1)}, bf16[3,256,256]{2,1,0:T(8,128)(2,1)S(1)}, u32[]{:S(2)}, u32[]{:S(2)}) collective-permute-start(bf16[3,256,256]{2,1,0:T(8,128)(2,1)S(1)} %bitcast.36), channel_id=1, source_target_pairs={{0,480},{32,448},{64,416},{96,384},{128,352},{160,320},{192,288},{... | collective-permute-start | bytes 1179656 | tf_op jit(solution)/shard_map/ppermute | solution.py:198
  42.7 1.9 %collective-permute-start.3 = (bf16[256,256]{1,0:T(8,128)(2,1)}, bf16[256,256]{1,0:T(8,128)(2,1)S(1)}, u32[]{:S(2)}, u32[]{:S(2)}) collective-permute-start(bf16[256,256]{1,0:T(8,128)(2,1)} %bitcast.8), channel_id=1, source_target_pairs={{0,480},{32,448},{64,416},{96,384},{128,352},{160,320},{192,288},{... | collective-permute-start | bytes 393224 | tf_op jit(solution)/shard_map/ppermute | solution.py:198
  44.7 0.6 shard_map.119
  45.3 18.4 %collective-permute-done.4.act_ref = bf16[3,256,256]{2,1,0:T(8,128)(2,1)S(1)} collective-permute-done((bf16[3,256,256]{2,1,0:T(8,128)(2,1)S(1)}, bf16[3,256,256]{2,1,0:T(8,128)(2,1)S(1)}, u32[]{:S(2)}, u32[]{:S(2)}) %collective-permute-start.4) | collective-permute-done | bytes 393248 | tf_op jit(solution)/shard_map/ppermute | solution.py:198
  63.7 0.7 copy-done.6
  64.5 1.0 copy-done.7
  65.4 0.6 shard_map.123
  66.1 0.8 copy-done
  66.9 1.1 copy-done.1
  68.6 6.2 %collective-permute-start.5 = (bf16[256,256]{1,0:T(8,128)(2,1)S(1)}, bf16[256,256]{1,0:T(8,128)(2,1)S(1)}, u32[]{:S(2)}, u32[]{:S(2)}) collective-permute-start(bf16[256,256]{1,0:T(8,128)(2,1)S(1)} %shard_map.124.refs_0_), channel_id=1, source_target_pairs={{32,0},{64,32},{96,64},{128,96},{160,128},{192,160},{224,192},{256... | collective-permute-start | bytes 393224 | tf_op jit(solution)/shard_map/ppermute | solution.py:203
  75.4 1.9 %collective-permute-start.1 = (bf16[256,256]{1,0:T(8,128)(2,1)S(1)}, bf16[256,256]{1,0:T(8,128)(2,1)S(1)}, u32[]{:S(2)}, u32[]{:S(2)}) collective-permute-start(bf16[256,256]{1,0:T(8,128)(2,1)S(1)} %shard_map.120), channel_id=1, source_target_pairs={{32,0},{64,32},{96,64},{128,96},{160,128},{192,160},{224,192},{256... | collective-permute-start | bytes 393224 | tf_op jit(solution)/shard_map/ppermute | solution.py:203
  77.3 0.7 collective-permute-done.5.front_ref.refs_3_
  78.6 6.5 %collective-permute-start.7 = (bf16[256,256]{1,0:T(8,128)(2,1)S(1)}, bf16[256,256]{1,0:T(8,128)(2,1)S(1)}, u32[]{:S(2)}, u32[]{:S(2)}) collective-permute-start(bf16[256,256]{1,0:T(8,128)(2,1)S(1)} %get-tuple-element.17), channel_id=1, source_target_pairs={{32,0},{64,32},{96,64},{128,96},{160,128},{192,160},{224,192},{256... | collective-permute-start | bytes 393224 | tf_op jit(solution)/shard_map/ppermute | solution.py:203
  85.6 1.9 %collective-permute-start.2 = (bf16[256,256]{1,0:T(8,128)(2,1)S(1)}, bf16[256,256]{1,0:T(8,128)(2,1)S(1)}, u32[]{:S(2)}, u32[]{:S(2)}) collective-permute-start(bf16[256,256]{1,0:T(8,128)(2,1)S(1)} %shard_map.121), channel_id=1, source_target_pairs={{32,0},{64,32},{96,64},{128,96},{160,128},{192,160},{224,192},{256... | collective-permute-start | bytes 393224 | tf_op jit(solution)/shard_map/ppermute | solution.py:203
  87.6 1.4 %shard_map.127.total_ref = f32[2304,256]{1,0:T(8,128)S(1)} custom-call(bf16[3,256,256]{2,1,0:T(8,128)(2,1)S(1)} %get-tuple-element.18.hid_down_ref, bf16[3,256,256]{2,1,0:T(8,128)(2,1)S(1)} %get-tuple-element.19.hid_up_ref, bf16[256,256]{1,0:T(8,128)(2,1)S(1)} %bitcast.29, bf16[256,256]{1,0:T(8,128)(2,1)S(1)} %collective-permute-done.1.front_ref.refs_1_, ...), custom_call_target="tpu_custom_call" | custom-call | tf_op jit(solution)/shard_map/pallas_call | solution.py:21
  89.0 3.5 %collective-permute-done.2.front_ref.refs_0_ = bf16[256,256]{1,0:T(8,128)(2,1)S(1)} collective-permute-done((bf16[256,256]{1,0:T(8,128)(2,1)S(1)}, bf16[256,256]{1,0:T(8,128)(2,1)S(1)}, u32[]{:S(2)}, u32[]{:S(2)}) %collective-permute-start.2) | collective-permute-done | bytes 131104 | tf_op jit(solution)/shard_map/ppermute | solution.py:203
  92.5 1.0 shard_map.128
  93.5 1.9 %collective-permute-start.9 = (bf16[16,72,256]{2,1,0:T(8,128)(2,1)S(1)}, bf16[16,72,256]{2,1,0:T(8,128)(2,1)S(1)}, u32[]{:S(2)}, u32[]{:S(2)}) collective-permute-start(bf16[16,72,256]{2,1,0:T(8,128)(2,1)S(1)} %get-tuple-element.21), channel_id=1, source_target_pairs={{0,1},{1,0},{2,3},{3,2},{4,5},{5,4},{6,7},{7,6},{8,9},{9,8},{10,11... | collective-permute-start | bytes 1769480 | tf_op jit(solution)/shard_map/ppermute | solution.py:207
  95.4 2.0 %collective-permute-done.9 = bf16[16,72,256]{2,1,0:T(8,128)(2,1)S(1)} collective-permute-done((bf16[16,72,256]{2,1,0:T(8,128)(2,1)S(1)}, bf16[16,72,256]{2,1,0:T(8,128)(2,1)S(1)}, u32[]{:S(2)}, u32[]{:S(2)}) %collective-permute-start.9) | collective-permute-done | bytes 589856 | tf_op jit(solution)/shard_map/ppermute | solution.py:207
  97.4 1.0 add_convert_fusion
  98.4 7.3 %all-to-all-start.1 = ((bf16[16,72,256]{2,1,0:T(8,128)(2,1)}), bf16[16,72,256]{2,1,0:T(8,128)(2,1)}, u32[]{:S(2)}, u32[]{:S(2)}) async-start(bf16[16,72,256]{2,1,0:T(8,128)(2,1)} %add_convert_fusion), calls=%async_computation.1 | async-start | bytes 1179648 | tf_op jit(solution)/shard_map/all_to_all | solution.py:241
  105.7 3.8 %collective-permute-start.6 = (bf16[2,256,256]{2,1,0:T(8,128)(2,1)S(1)}, bf16[2,256,256]{2,1,0:T(8,128)(2,1)S(1)}, u32[]{:S(2)}, u32[]{:S(2)}) collective-permute-start(bf16[2,256,256]{2,1,0:T(8,128)(2,1)S(1)} %copy-done.9), channel_id=1, source_target_pairs={{0,480},{32,448},{64,416},{96,384},{128,352},{160,320},{192,288},{... | collective-permute-start | bytes 786440 | tf_op jit(solution)/shard_map/ppermute | solution.py:198
  110.0 4.3 %collective-permute-start.8 = (bf16[256,256]{1,0:T(8,128)(2,1)S(1)}, bf16[256,256]{1,0:T(8,128)(2,1)S(1)}, u32[]{:S(2)}, u32[]{:S(2)}) collective-permute-start(bf16[256,256]{1,0:T(8,128)(2,1)S(1)} %shard_map.126), channel_id=1, source_target_pairs={{0,480},{32,448},{64,416},{96,384},{128,352},{160,320},{192,288},{... | collective-permute-start | bytes 393224 | tf_op jit(solution)/shard_map/ppermute | solution.py:198
  114.9 0.8 pad_maximum_fusion
  115.7 10.5 %collective-permute-done.6 = bf16[2,256,256]{2,1,0:T(8,128)(2,1)S(1)} collective-permute-done((bf16[2,256,256]{2,1,0:T(8,128)(2,1)S(1)}, bf16[2,256,256]{2,1,0:T(8,128)(2,1)S(1)}, u32[]{:S(2)}, u32[]{:S(2)}) %collective-permute-start.6) | collective-permute-done | bytes 262176 | tf_op jit(solution)/shard_map/ppermute | solution.py:198
  126.2 2.7 %collective-permute-done.8 = bf16[256,256]{1,0:T(8,128)(2,1)S(1)} collective-permute-done((bf16[256,256]{1,0:T(8,128)(2,1)S(1)}, bf16[256,256]{1,0:T(8,128)(2,1)S(1)}, u32[]{:S(2)}, u32[]{:S(2)}) %collective-permute-start.8) | collective-permute-done | bytes 131104 | tf_op jit(solution)/shard_map/ppermute | solution.py:198
  128.9 0.8 pad_maximum_fusion.1
  129.7 1.2 convert_reduce_fusion
  130.8 0.7 fusion.2
  (37 shorter events, 3.3 us)
Async XLA Ops:
  0.6 30.8 %copy-start.13 = (bf16[3,1,1,16,16,256]{5,4,3,2,1,0:T(8,128)(2,1)S(1)}, bf16[3,1,1,16,16,256]{5,4,3,2,1,0:T(8,128)(2,1)}, u32[]{:S(2)}) copy-start(bf16[3,1,1,16,16,256]{5,4,3,2,1,0:T(8,128)(2,1)} %param.8) | copy-start | bytes 1179652
  0.6 44.0 %copy-start.5 = (bf16[3,1,1,16,16,256]{5,4,3,2,1,0:T(8,128)(2,1)S(1)}, bf16[3,1,1,16,16,256]{5,4,3,2,1,0:T(8,128)(2,1)}, u32[]{:S(2)}) copy-start(bf16[3,1,1,16,16,256]{5,4,3,2,1,0:T(8,128)(2,1)} %param.7) | copy-start | bytes 1179652
  29.6 36.5 %collective-permute-start = (bf16[16,72,256]{2,1,0:T(8,128)(2,1)S(1)}, bf16[16,72,256]{2,1,0:T(8,128)(2,1)S(1)}, u32[]{:S(2)}, u32[]{:S(2)}) collective-permute-start(bf16[16,72,256]{2,1,0:T(8,128)(2,1)S(1)} %all_to_all.10.mine_ref), channel_id=1, source_target_pairs={{0,1},{1,0},{2,3},{3,2},{4,5},{5,4},{6,7},{7,6},{8,9},{9,8},{10,11... | collective-permute-start | bytes 1769480 | tf_op jit(solution)/shard_map/ppermute | solution.py:207
  31.5 32.2 %collective-permute-start.4 = (bf16[3,256,256]{2,1,0:T(8,128)(2,1)S(1)}, bf16[3,256,256]{2,1,0:T(8,128)(2,1)S(1)}, u32[]{:S(2)}, u32[]{:S(2)}) collective-permute-start(bf16[3,256,256]{2,1,0:T(8,128)(2,1)S(1)} %bitcast.36), channel_id=1, source_target_pairs={{0,480},{32,448},{64,416},{96,384},{128,352},{160,320},{192,288},{... | collective-permute-start | bytes 1179656 | tf_op jit(solution)/shard_map/ppermute | solution.py:198
  42.7 25.4 %collective-permute-start.3 = (bf16[256,256]{1,0:T(8,128)(2,1)}, bf16[256,256]{1,0:T(8,128)(2,1)S(1)}, u32[]{:S(2)}, u32[]{:S(2)}) collective-permute-start(bf16[256,256]{1,0:T(8,128)(2,1)} %bitcast.8), channel_id=1, source_target_pairs={{0,480},{32,448},{64,416},{96,384},{128,352},{160,320},{192,288},{... | collective-permute-start | bytes 393224 | tf_op jit(solution)/shard_map/ppermute | solution.py:198
  63.7 0.7 copy-start.6
  64.5 1.0 copy-start.7
  66.1 0.8 copy-start
  66.9 1.1 copy-start.1
  68.1 6.8 %copy-start.2 = (bf16[1,1,16,16,256]{4,3,2,1,0:T(8,128)(2,1)S(1)}, bf16[1,1,16,16,256]{4,3,2,1,0:T(8,128)(2,1)}, u32[]{:S(2)}) copy-start(bf16[1,1,16,16,256]{4,3,2,1,0:T(8,128)(2,1)} %param.9) | copy-start | bytes 393220
  68.6 9.4 %collective-permute-start.5 = (bf16[256,256]{1,0:T(8,128)(2,1)S(1)}, bf16[256,256]{1,0:T(8,128)(2,1)S(1)}, u32[]{:S(2)}, u32[]{:S(2)}) collective-permute-start(bf16[256,256]{1,0:T(8,128)(2,1)S(1)} %shard_map.124.refs_0_), channel_id=1, source_target_pairs={{32,0},{64,32},{96,64},{128,96},{160,128},{192,160},{224,192},{256... | collective-permute-start | bytes 393224 | tf_op jit(solution)/shard_map/ppermute | solution.py:203
  75.4 9.7 %copy-start.3 = (bf16[256,256]{1,0:T(8,128)(2,1)}, bf16[256,256]{1,0:T(8,128)(2,1)S(1)}, u32[]{:S(2)}) copy-start(bf16[256,256]{1,0:T(8,128)(2,1)S(1)} %shard_map.120) | copy-start | bytes 393220
  75.4 9.7 %collective-permute-start.1 = (bf16[256,256]{1,0:T(8,128)(2,1)S(1)}, bf16[256,256]{1,0:T(8,128)(2,1)S(1)}, u32[]{:S(2)}, u32[]{:S(2)}) collective-permute-start(bf16[256,256]{1,0:T(8,128)(2,1)S(1)} %shard_map.120), channel_id=1, source_target_pairs={{32,0},{64,32},{96,64},{128,96},{160,128},{192,160},{224,192},{256... | collective-permute-start | bytes 393224 | tf_op jit(solution)/shard_map/ppermute | solution.py:203
  78.6 10.4 %copy-start.8 = (bf16[2,256,256]{2,1,0:T(8,128)(2,1)}, bf16[2,256,256]{2,1,0:T(8,128)(2,1)S(1)}, u32[]{:S(2)}) copy-start(bf16[2,256,256]{2,1,0:T(8,128)(2,1)S(1)} %get-tuple-element.16) | copy-start | bytes 786436
  78.6 10.4 %collective-permute-start.7 = (bf16[256,256]{1,0:T(8,128)(2,1)S(1)}, bf16[256,256]{1,0:T(8,128)(2,1)S(1)}, u32[]{:S(2)}, u32[]{:S(2)}) collective-permute-start(bf16[256,256]{1,0:T(8,128)(2,1)S(1)} %get-tuple-element.17), channel_id=1, source_target_pairs={{32,0},{64,32},{96,64},{128,96},{160,128},{192,160},{224,192},{256... | collective-permute-start | bytes 393224 | tf_op jit(solution)/shard_map/ppermute | solution.py:203
  85.6 6.9 %collective-permute-start.2 = (bf16[256,256]{1,0:T(8,128)(2,1)S(1)}, bf16[256,256]{1,0:T(8,128)(2,1)S(1)}, u32[]{:S(2)}, u32[]{:S(2)}) collective-permute-start(bf16[256,256]{1,0:T(8,128)(2,1)S(1)} %shard_map.121), channel_id=1, source_target_pairs={{32,0},{64,32},{96,64},{128,96},{160,128},{192,160},{224,192},{256... | collective-permute-start | bytes 393224 | tf_op jit(solution)/shard_map/ppermute | solution.py:203
  93.5 3.9 %collective-permute-start.9 = (bf16[16,72,256]{2,1,0:T(8,128)(2,1)S(1)}, bf16[16,72,256]{2,1,0:T(8,128)(2,1)S(1)}, u32[]{:S(2)}, u32[]{:S(2)}) collective-permute-start(bf16[16,72,256]{2,1,0:T(8,128)(2,1)S(1)} %get-tuple-element.21), channel_id=1, source_target_pairs={{0,1},{1,0},{2,3},{3,2},{4,5},{5,4},{6,7},{7,6},{8,9},{9,8},{10,11... | collective-permute-start | bytes 1769480 | tf_op jit(solution)/shard_map/ppermute | solution.py:207
  97.4 8.3 %copy-start.9 = (bf16[2,256,256]{2,1,0:T(8,128)(2,1)S(1)}, bf16[2,256,256]{2,1,0:T(8,128)(2,1)}, u32[]{:S(2)}) copy-start(bf16[2,256,256]{2,1,0:T(8,128)(2,1)} %copy-done.8) | copy-start | bytes 786436
  98.4 31.3 %all-to-all-start.1 = ((bf16[16,72,256]{2,1,0:T(8,128)(2,1)}), bf16[16,72,256]{2,1,0:T(8,128)(2,1)}, u32[]{:S(2)}, u32[]{:S(2)}) async-start(bf16[16,72,256]{2,1,0:T(8,128)(2,1)} %add_convert_fusion), calls=%async_computation.1 | async-start | bytes 1179648 | tf_op jit(solution)/shard_map/all_to_all | solution.py:241
  105.7 20.5 %collective-permute-start.6 = (bf16[2,256,256]{2,1,0:T(8,128)(2,1)S(1)}, bf16[2,256,256]{2,1,0:T(8,128)(2,1)S(1)}, u32[]{:S(2)}, u32[]{:S(2)}) collective-permute-start(bf16[2,256,256]{2,1,0:T(8,128)(2,1)S(1)} %copy-done.9), channel_id=1, source_target_pairs={{0,480},{32,448},{64,416},{96,384},{128,352},{160,320},{192,288},{... | collective-permute-start | bytes 786440 | tf_op jit(solution)/shard_map/ppermute | solution.py:198
  110.0 4.9 %copy-start.4 = (bf16[256,256]{1,0:T(8,128)(2,1)S(1)}, bf16[256,256]{1,0:T(8,128)(2,1)}, u32[]{:S(2)}) copy-start(bf16[256,256]{1,0:T(8,128)(2,1)} %copy-done.3) | copy-start | bytes 393220
  110.0 18.9 %collective-permute-start.8 = (bf16[256,256]{1,0:T(8,128)(2,1)S(1)}, bf16[256,256]{1,0:T(8,128)(2,1)S(1)}, u32[]{:S(2)}, u32[]{:S(2)}) collective-permute-start(bf16[256,256]{1,0:T(8,128)(2,1)S(1)} %shard_map.126), channel_id=1, source_target_pairs={{0,480},{32,448},{64,416},{96,384},{128,352},{160,320},{192,288},{... | collective-permute-start | bytes 393224 | tf_op jit(solution)/shard_map/ppermute | solution.py:198
  114.8 16.0 %copy-start.10 = (f32[1,72,256]{2,1,0:T(8,128)S(1)}, f32[1,72,256]{2,1,0:T(8,128)}, u32[]{:S(2)}) copy-start(f32[1,72,256]{2,1,0:T(8,128)} %param.11) | copy-start | bytes 221188
  114.9 16.0 %copy-start.11 = (f32[1,72,256]{2,1,0:T(8,128)S(1)}, f32[1,72,256]{2,1,0:T(8,128)}, u32[]{:S(2)}) copy-start(f32[1,72,256]{2,1,0:T(8,128)} %param.13) | copy-start | bytes 221188
  114.9 16.0 %copy-start.12 = (f32[1,72,256]{2,1,0:T(8,128)S(1)}, f32[1,72,256]{2,1,0:T(8,128)}, u32[]{:S(2)}) copy-start(f32[1,72,256]{2,1,0:T(8,128)} %param.12) | copy-start | bytes 221188

commit v3 on v2

--- a/solution.py
+++ b/solution.py
@@ -15,36 +15,54 @@
     return pltpu.with_memory_space_constraint(value, pltpu.VMEM)
 
 
-def call(body, outs, args, scratch=(), scalars=0, alias=None):
+def call(body, outs, args, scratch=(), scalars=0, off_chip=False):
     specs = [SMEM] * scalars + [VMEM] * (len(args) - scalars)
     args = [*args[:scalars], *map(on_chip, args[scalars:])]
     return pl.pallas_call(
         body,
         in_specs=specs,
         out_specs=[VMEM] * len(outs),
-        out_shape=[pltpu.VMEM(shape, dtype) for shape, dtype in outs],
+        out_shape=[(jax.ShapeDtypeStruct if off_chip else pltpu.VMEM)(*out) for out in outs],
         scratch_shapes=list(scratch),
-        input_output_aliases=alias or {},
         compiler_params=pltpu.CompilerParams(vmem_limit_bytes=16 << 20),
     )(*args)
 
 
-def gelu_kernel(act_ref, hid_ref, slope_ref):
-    for t in range(act_ref.shape[0]):
-        x = act_ref[t].astype(jnp.float32)
-        cube = 0.044715 * x * x * x
-        bent = jnp.tanh(0.7978845608028654 * (x + cube))
-        half = 0.5 * (1.0 + bent)
-        hidden = (x * half).astype(jnp.bfloat16)
-        hid_ref[t] = hidden.astype(jnp.float32).T.astype(jnp.bfloat16)
-        inner = 0.7978845608028654 * (1.0 + 3.0 * 0.044715 * x * x)
-        slope_ref[t] = half + 0.5 * x * (1.0 - bent * bent) * inner
-
-
-def gelu_parts(acts):
-    n, pixels, channels = acts.shape
-    outs = [((n, channels, pixels), jnp.bfloat16), ((n, pixels, channels), jnp.float32)]
-    return call(gelu_kernel, outs, [acts])
+def spread_kernel(rows_ref, out_ref):
+    rows = rows_ref[...].astype(jnp.bfloat16)
+    for i in range(out_ref.shape[0]):
+        out_ref[i] = rows
+
+
+def spread(rows, count):
+    return call(spread_kernel, [((count, *rows.shape), jnp.bfloat16)], [rows])[0]
+
+
+def add_kernel(one_ref, two_ref, out_ref):
+    total = one_ref[...].astype(jnp.float32) + two_ref[...].astype(jnp.float32)
+    out_ref[...] = total.astype(jnp.bfloat16)
+
+
+def pair_add(one, two):
+    return call(add_kernel, [(one.shape, jnp.bfloat16)], [one, two])[0]
+
+
+def bend(x):
+    bent = jnp.tanh(0.7978845608028654 * (x + 0.044715 * x * x * x))
+    return bent, 0.5 * (1.0 + bent)
+
+
+def hidden_kernel(*refs):
+    acts, outs = refs[: len(refs) // 2], refs[len(refs) // 2 :]
+    for act_ref, out_ref in zip(acts, outs):
+        x = act_ref[...].astype(jnp.float32)
+        hidden = (x * bend(x)[1]).astype(jnp.bfloat16)
+        out_ref[...] = hidden.astype(jnp.float32).T.astype(jnp.bfloat16)
+
+
+def hidden_parts(acts):
+    outs = [(act.shape[::-1], jnp.bfloat16) for act in acts]
+    return call(hidden_kernel, outs, acts, off_chip=True)
 
 
 def fill_taps(front, pad_ref, width):
@@ -64,7 +82,7 @@
     return pltpu.VMEM((count, 3, pixels + 2 * width, channels), jnp.bfloat16)
 
 
-def tick_kernel(t, width, factor, front_ref, weight_ref, slope_ref, *refs):
+def tick_kernel(width, factor, front_ref, weight_ref, act_ref, *refs):
     earlier, (out_ref, *pair, pad_ref) = refs[: len(refs) // 2 - 1], refs[len(refs) // 2 - 1 :]
     front = front_ref[...]
     pixels, channels = front.shape
@@ -79,23 +97,27 @@
                 (((1,), (1,)), ((), ())),
                 preferred_element_type=jnp.float32,
             )
-    out = (front.astype(jnp.float32) + slope_ref[t] * (factor * total)).astype(jnp.bfloat16)
+    x = act_ref[...].astype(jnp.float32)
+    bent, half = bend(x)
+    inner = 0.7978845608028654 * (1.0 + 3.0 * 0.044715 * x * x)
+    slope = half + 0.5 * x * (1.0 - bent * bent) * inner
+    out = (front.astype(jnp.float32) + slope * (factor * total)).astype(jnp.bfloat16)
     out_ref[...] = out
     if pair:
         pair[0][0] = earlier[0][...]
         pair[0][1] = out
 
 
-def tick(front, weight, slopes, t, width, earlier=None):
+def tick(front, weight, act, width, earlier=None):
     pixels, channels = front.shape
     factor = (9 * channels) ** -0.5
     outs = [(front.shape, jnp.bfloat16)]
-    args = [front, weight, slopes]
+    args = [front, weight, act]
     if earlier is not None:
         outs.append(((2, *front.shape), jnp.bfloat16))
         args.append(earlier)
     return call(
-        functools.partial(tick_kernel, t, width, factor),
+        functools.partial(tick_kernel, width, factor),
         outs,
         args,
         [pads(1, pixels, width, channels)],
@@ -119,35 +141,37 @@
             write((3 * a + b) * channels, total)
 
 
-def early_kernel(ticks, width, hid_down_ref, hid_up_ref, *refs):
-    front_refs, (out_ref, pad_ref) = refs[:-2], refs[-2:]
-    hiddens = [hid_down_ref.at[t] for t in ticks] + [hid_up_ref.at[t] for t in ticks]
+def early_kernel(width, *refs):
+    count = len(refs) // 2 - 1
+    hid_refs, front_refs, (out_ref, pad_ref) = refs[:count], refs[count:-2], refs[-2:]
 
     def write(row, total):
         out_ref[row : row + total.shape[0]] = total
 
-    add_terms(hiddens, front_refs, pad_ref, width, write)
-
-
-def early_terms(hid_down, hid_up, fronts, ticks, width):
-    channels, pixels = hid_down.shape[1:]
+    add_terms(hid_refs, front_refs, pad_ref, width, write)
+
+
+def early_terms(hiddens, fronts, width):
+    channels, pixels = hiddens[0].shape
     return call(
-        functools.partial(early_kernel, ticks, width),
+        functools.partial(early_kernel, width),
         [((9 * channels, channels), jnp.float32)],
-        [hid_down, hid_up, *fronts],
+        [*hiddens, *fronts],
         [pads(len(fronts), pixels, width, channels)],
     )[0]
 
 
-def last_kernel(t, width, factor, core_ref, hid_down_ref, hid_up_ref, total_ref, *refs):
-    front_refs, (kept_ref, given_ref, sum_ref, pad_ref) = refs[:-4], refs[-4:]
+def last_kernel(width, factor, core_ref, total_ref, *refs):
+    count = len(refs) // 2 - 2
+    hid_refs, front_refs = refs[:count], refs[count:-4]
+    kept_ref, given_ref, sum_ref, pad_ref = refs[-4:]
     rows = kept_ref.shape[1]
 
     def write(row, total):
         at = slice(row, row + total.shape[0])
         sum_ref[at] = factor * (total_ref[at] + total)
 
-    add_terms([hid_down_ref.at[t], hid_up_ref.at[t]], front_refs, pad_ref, width, write)
+    add_terms(hid_refs, front_refs, pad_ref, width, write)
     for core, places in enumerate(((kept_ref, given_ref), (given_ref, kept_ref))):
 
         @pl.when(core_ref[0] == core)
@@ -156,14 +180,17 @@
                 places[i % 2][i // 2] = sum_ref[i * rows : (i + 1) * rows].astype(jnp.bfloat16)
 
 
-def last_terms(core, hid_down, hid_up, total, fronts, t, chips, width):
-    channels, pixels = hid_down.shape[1:]
+def last_terms(core, total, hiddens, fronts, chips, width):
+    channels, pixels = hiddens[0].shape
     half = (chips, 9 * channels // (2 * chips), channels)
     return call(
-        functools.partial(last_kernel, t, width, (9 * channels) ** -0.5),
+        functools.partial(last_kernel, width, (9 * channels) ** -0.5),
         [(half, jnp.bfloat16), (half, jnp.bfloat16)],
-        [core, hid_down, hid_up, total, *fronts],
-        [pltpu.VMEM((9 * channels, channels), jnp.float32), pads(len(fronts), pixels, width, channels)],
+        [core, total, *hiddens, *fronts],
+        [
+            pltpu.VMEM((9 * channels, channels), jnp.float32),
+            pads(len(fronts), pixels, width, channels),
+        ],
         scalars=1,
     )
 
@@ -212,34 +239,38 @@
     flat = (height * width, channels)
     chips = lax.axis_size(CHIPS)
     core = lax.axis_index("core").astype(jnp.int32).reshape(1)
+    acts_down = [acts_down[t].reshape(flat) for t in range(ticks)]
+    acts_up = acts_up.reshape(ticks, *flat)
+    mine = lax.all_to_all(spread(master[0], chips), CHIPS, 0, 0, tiled=True)
     front_up = to_mirror(front_up.reshape(flat))
-    acts_up = to_mirror(acts_up.reshape(ticks, *flat))
-    rows = master[0].astype(jnp.bfloat16)
-    mine = lax.all_to_all(jnp.broadcast_to(rows[None], (chips, *rows.shape)), CHIPS, 0, 0, tiled=True)
-    hid_down, slope_down = gelu_parts(acts_down.reshape(ticks, *flat))
-    hid_up, slope_up = gelu_parts(acts_up)
+    far_act = to_mirror(acts_up[0])
+    far_rest = to_mirror(acts_up[1:])
+    hid_down = hidden_parts(acts_down)
+    hid_up = hidden_parts([far_act])
+    acts_up = [far_act, *far_rest]
     other = to_partner(mine)
     weight = weave(core, mine, other)
     down, up = [front_down.reshape(flat)], [front_up]
     outs_down, outs_up = [], []
     for t in range(ticks):
-        next_down = tick(down[t], weight, slope_down, t, width)[0]
-        if t == 1:
-            next_up, pair = tick(up[t], weight, slope_up, t, width, outs_up[0])
+        next_down = tick(down[t], weight, acts_down[t], width)[0]
+        if t + 1 < ticks:
+            next_up = tick(up[t], weight, acts_up[t], width)[0]
         else:
-            next_up = tick(up[t], weight, slope_up, t, width)[0]
+            next_up, pair = tick(up[t], weight, acts_up[t], width, outs_up[1])
         outs_down.append(next_down)
         outs_up.append(next_up)
         if t + 1 < ticks:
             down.append(from_next(next_down))
             up.append(from_next(next_up))
-    total = early_terms(hid_down, hid_up, down[:2] + up[:2], (0, 1), width)
+    first = to_mirror(outs_up[0])
+    hid_up = hid_up + hidden_parts(acts_up[1:])
+    total = early_terms([*hid_down[:2], *hid_up[:2]], down[:2] + up[:2], width)
+    kept, given = last_terms(core, total, [hid_down[2], hid_up[2]], [down[2], up[2]], chips, width)
+    taken = to_partner(given)
+    both = pair_add(kept, taken)
+    pieces = lax.all_to_all(both, CHIPS, 0, 0, tiled=True)
     pair = to_mirror(pair)
-    kept, given = last_terms(core, hid_down, hid_up, total, [down[2], up[2]], 2, chips, width)
-    taken = to_partner(given)
-    both = (kept.astype(jnp.float32) + taken.astype(jnp.float32)).astype(jnp.bfloat16)
-    pieces = lax.all_to_all(both, CHIPS, 0, 0, tiled=True)
-    last = to_mirror(outs_up[2])
     gradient = jnp.sum(pieces.astype(jnp.float32), axis=0)
     old_master = master[0]
     new_first = beta_first * moment_first[0] + (1.0 - beta_first) * gradient
@@ -250,7 +281,7 @@
     shape = (ticks, 1, 1, height, width, channels)
     return (
         jnp.stack(outs_down).reshape(shape),
-        jnp.concatenate([pair, last[None]]).reshape(shape),
+        jnp.concatenate([first[None], pair]).reshape(shape),
         new_master.astype(jnp.bfloat16)[None],
         new_master[None],
         new_first[None],

time: 132 us -> 125 us (0.947)
  waiting for transfers between devices: 37.8 us -> 28.6 us
  starting transfers between devices: 48.9 us -> 54.2 us
  other arithmetic: 5.38 us -> 2.38 us
  local copies, waits for them, and re-layouts: 3.74 us -> 1.79 us
  Pallas kernels: 6.87 us -> 8.68 us
    ppermute x4 -> x5, starting transfers between devices: 21.2 us -> 27.1 us  [to_mirror(): lax.ppermute(value, SECTION, [(i, length - 1 - i) for i in range(length)])]
    ppermute x4 -> x5, waiting for transfers between devices: 31.6 us -> 26.1 us  [to_mirror(): lax.ppermute(value, SECTION, [(i, length - 1 - i) for i in range(length)])]
    ppermute x4, waiting for transfers between devices: 4.17 us -> 0.52 us  [from_next(): return lax.ppermute(value, SECTION, [(i + 1, i) for i in range(length - 1)])]
    unnamed x28 -> x16, local copies, waits for them, and re-layouts: 3.7 us -> 1.71 us
    pallas_call x11 -> x14, Pallas kernels: 6.87 us -> 8.68 us  [call(): pl.pallas_call(body, in_specs=specs, out_specs=[VMEM] * len(outs), out_sh...]
  transfers between devices with their start and end apart: 11 -> 12, of which waited for: 6 -> 6; matrix products, arithmetic and copies ran while one was open for 1% -> 1% of each run, Pallas kernels for 4% -> 5%
where the time goes in v3:
time: 125 us
  starting transfers between devices  54.2 us (43%)
  waiting for transfers between devices  28.6 us (23%)
  blocking collectives  28 us (22%)
  Pallas kernels  8.68 us (7%)
  other arithmetic  2.38 us (2%)
  local copies, waits for them, and re-layouts  1.79 us (1%)
    all_to_all x1, blocking collectives, step(): mine = lax.all_to_all(spread(master[0], chips), CHIPS, 0, 0, tiled=True)  28 us
    ppermute x5, starting transfers between devices, to_mirror(): lax.ppermute(value, SECTION, [(i, length - 1 - i) for i in range(length)])  27.1 us
    ppermute x5, waiting for transfers between devices, to_mirror(): lax.ppermute(value, SECTION, [(i, length - 1 - i) for i in range(length)])  26.1 us
    ppermute x4, starting transfers between devices, from_next(): return lax.ppermute(value, SECTION, [(i + 1, i) for i in range(length - 1)])  16.6 us
    pallas_call x14, Pallas kernels, call(): pl.pallas_call(body, in_specs=specs, out_specs=[VMEM] * len(outs), out_sh...  8.68 us
    all_to_all x1, starting transfers between devices, step(): pieces = lax.all_to_all(both, CHIPS, 0, 0, tiled=True)  6.68 us
    ppermute x2, starting transfers between devices, to_partner(): return lax.ppermute(value, 'core', [(0, 1), (1, 0)])  3.83 us
  transfers between devices with their start and end apart: 12, of which 6 were waited for; matrix products, arithmetic and copies ran while one was open for 1% of the time, Pallas kernels for 5%

profile of v3, /device:TPU:6, one launch (start us, length us, event | category | flops | bytes accessed | tf_op | source)
XLA Modules:
  0.0 124.6 jit_solution(12793069511325896597)
XLA Ops:
  0.6 0.9 copy-done.1
  1.6 28.0 %all_to_all.10.mine_ref = bf16[16,72,256]{2,1,0:T(8,128)(2,1)S(1)} all-to-all(bf16[16,72,256]{2,1,0:T(8,128)(2,1)S(1)} %shard_map.118), channel_id=1, replica_groups=mesh['x_lo'=2,'z'=8,'x_hi'=2,'y'=8,'core'=2] {'x_hi','y'}, dimensions={0} | all-to-all | bytes 1179648 | tf_op jit(solution)/shard_map/all_to_all | solution.py:244
  29.6 1.9 %collective-permute-start = (bf16[16,72,256]{2,1,0:T(8,128)(2,1)S(1)}, bf16[16,72,256]{2,1,0:T(8,128)(2,1)S(1)}, u32[]{:S(2)}, u32[]{:S(2)}) collective-permute-start(bf16[16,72,256]{2,1,0:T(8,128)(2,1)S(1)} %all_to_all.10.mine_ref), channel_id=1, source_target_pairs={{0,1},{1,0},{2,3},{3,2},{4,5},{5,4},{6,7},{7,6},{8,9},{9,8},{10,11... | collective-permute-start | bytes 1769480 | tf_op jit(solution)/shard_map/ppermute | solution.py:234
  31.6 11.2 %collective-permute-start.7 = (bf16[2,256,256]{2,1,0:T(8,128)(2,1)S(1)}, bf16[2,256,256]{2,1,0:T(8,128)(2,1)S(1)}, u32[]{:S(2)}, u32[]{:S(2)}) collective-permute-start(bf16[2,256,256]{2,1,0:T(8,128)(2,1)S(1)} %bitcast.47), channel_id=1, source_target_pairs={{0,480},{32,448},{64,416},{96,384},{128,352},{160,320},{192,288},{... | collective-permute-start | bytes 786440 | tf_op jit(solution)/shard_map/ppermute | solution.py:225
  42.8 1.9 %collective-permute-start.4 = (bf16[256,256]{1,0:T(8,128)(2,1)S(1)}, bf16[256,256]{1,0:T(8,128)(2,1)S(1)}, u32[]{:S(2)}, u32[]{:S(2)}) collective-permute-start(bf16[256,256]{1,0:T(8,128)(2,1)S(1)} %bitcast.48), channel_id=1, source_target_pairs={{0,480},{32,448},{64,416},{96,384},{128,352},{160,320},{192,288},{... | collective-permute-start | bytes 393224 | tf_op jit(solution)/shard_map/ppermute | solution.py:225
  44.7 6.0 %collective-permute-start.3 = (bf16[256,256]{1,0:T(8,128)(2,1)S(1)}, bf16[256,256]{1,0:T(8,128)(2,1)S(1)}, u32[]{:S(2)}, u32[]{:S(2)}) collective-permute-start(bf16[256,256]{1,0:T(8,128)(2,1)S(1)} %bitcast.50), channel_id=1, source_target_pairs={{0,480},{32,448},{64,416},{96,384},{128,352},{160,320},{192,288},{... | collective-permute-start | bytes 393224 | tf_op jit(solution)/shard_map/ppermute | solution.py:225
  50.9 0.8 copy-done
  51.7 0.6 shard_map.120
  52.4 1.9 %collective-permute-start.1 = (bf16[256,256]{1,0:T(8,128)(2,1)S(1)}, bf16[256,256]{1,0:T(8,128)(2,1)S(1)}, u32[]{:S(2)}, u32[]{:S(2)}) collective-permute-start(bf16[256,256]{1,0:T(8,128)(2,1)S(1)} %shard_map.120), channel_id=1, source_target_pairs={{32,0},{64,32},{96,64},{128,96},{160,128},{192,160},{224,192},{256... | collective-permute-start | bytes 393224 | tf_op jit(solution)/shard_map/ppermute | solution.py:230
  54.3 9.5 %collective-permute-done.4.act_ref.refs_0_ = bf16[256,256]{1,0:T(8,128)(2,1)S(1)} collective-permute-done((bf16[256,256]{1,0:T(8,128)(2,1)S(1)}, bf16[256,256]{1,0:T(8,128)(2,1)S(1)}, u32[]{:S(2)}, u32[]{:S(2)}) %collective-permute-start.4) | collective-permute-done | bytes 131104 | tf_op jit(solution)/shard_map/ppermute | solution.py:225
  63.8 2.8 %collective-permute-done.3.front_ref.refs_6_ = bf16[256,256]{1,0:T(8,128)(2,1)S(1)} collective-permute-done((bf16[256,256]{1,0:T(8,128)(2,1)S(1)}, bf16[256,256]{1,0:T(8,128)(2,1)S(1)}, u32[]{:S(2)}, u32[]{:S(2)}) %collective-permute-start.3) | collective-permute-done | bytes 131104 | tf_op jit(solution)/shard_map/ppermute | solution.py:225
  66.6 0.6 shard_map.123
  67.2 6.2 %collective-permute-start.6 = (bf16[256,256]{1,0:T(8,128)(2,1)S(1)}, bf16[256,256]{1,0:T(8,128)(2,1)S(1)}, u32[]{:S(2)}, u32[]{:S(2)}) collective-permute-start(bf16[256,256]{1,0:T(8,128)(2,1)S(1)} %shard_map.123), channel_id=1, source_target_pairs={{32,0},{64,32},{96,64},{128,96},{160,128},{192,160},{224,192},{256... | collective-permute-start | bytes 393224 | tf_op jit(solution)/shard_map/ppermute | solution.py:230
  73.5 0.6 shard_map.121
  74.1 1.9 %collective-permute-start.2 = (bf16[256,256]{1,0:T(8,128)(2,1)S(1)}, bf16[256,256]{1,0:T(8,128)(2,1)S(1)}, u32[]{:S(2)}, u32[]{:S(2)}) collective-permute-start(bf16[256,256]{1,0:T(8,128)(2,1)S(1)} %shard_map.121), channel_id=1, source_target_pairs={{32,0},{64,32},{96,64},{128,96},{160,128},{192,160},{224,192},{256... | collective-permute-start | bytes 393224 | tf_op jit(solution)/shard_map/ppermute | solution.py:230
  76.3 0.6 shard_map.124.refs_0_
  76.9 6.5 %collective-permute-start.8 = (bf16[256,256]{1,0:T(8,128)(2,1)S(1)}, bf16[256,256]{1,0:T(8,128)(2,1)S(1)}, u32[]{:S(2)}, u32[]{:S(2)}) collective-permute-start(bf16[256,256]{1,0:T(8,128)(2,1)S(1)} %shard_map.124.refs_0_), channel_id=1, source_target_pairs={{32,0},{64,32},{96,64},{128,96},{160,128},{192,160},{224,192},{256... | collective-permute-start | bytes 393224 | tf_op jit(solution)/shard_map/ppermute | solution.py:230
  83.4 0.4 shard_map.126
  84.2 1.4 %shard_map.129.total_ref = f32[2304,256]{1,0:T(8,128)S(1)} custom-call(bf16[256,256]{1,0:T(8,128)(2,1)S(1)} %get-tuple-element.15.refs_0_, bf16[256,256]{1,0:T(8,128)(2,1)S(1)} %get-tuple-element.16.refs_1_, bf16[256,256]{1,0:T(8,128)(2,1)S(1)} %shard_map.127.refs_2_, bf16[256,256]{1,0:T(8,128)(2,1)S(1)} %get-tuple-element.17.refs_3_, ...), custom_call_target="tpu_custom_call" | custom-call | tf_op jit(solution)/shard_map/pallas_call | solution.py:21
  85.9 1.0 shard_map.130
  86.9 1.9 %collective-permute-start.10 = (bf16[16,72,256]{2,1,0:T(8,128)(2,1)S(1)}, bf16[16,72,256]{2,1,0:T(8,128)(2,1)S(1)}, u32[]{:S(2)}, u32[]{:S(2)}) collective-permute-start(bf16[16,72,256]{2,1,0:T(8,128)(2,1)S(1)} %get-tuple-element.21), channel_id=1, source_target_pairs={{0,1},{1,0},{2,3},{3,2},{4,5},{5,4},{6,7},{7,6},{8,9},{9,8},{10,11... | collective-permute-start | bytes 1769480 | tf_op jit(solution)/shard_map/ppermute | solution.py:234
  88.8 2.0 %collective-permute-done.10.two_ref = bf16[16,72,256]{2,1,0:T(8,128)(2,1)S(1)} collective-permute-done((bf16[16,72,256]{2,1,0:T(8,128)(2,1)S(1)}, bf16[16,72,256]{2,1,0:T(8,128)(2,1)S(1)}, u32[]{:S(2)}, u32[]{:S(2)}) %collective-permute-start.10) | collective-permute-done | bytes 589856 | tf_op jit(solution)/shard_map/ppermute | solution.py:234
  90.8 1.0 shard_map.131
  91.8 6.7 %all-to-all-start.1 = ((bf16[16,72,256]{2,1,0:T(8,128)(2,1)}), bf16[16,72,256]{2,1,0:T(8,128)(2,1)S(1)}, u32[]{:S(2)}, u32[]{:S(2)}) async-start(bf16[16,72,256]{2,1,0:T(8,128)(2,1)} %shard_map.131), calls=%async_computation.1 | async-start | bytes 1179648 | tf_op jit(solution)/shard_map/all_to_all | solution.py:272
  98.5 1.3 %shard_map.125 = (bf16[256,256]{1,0:T(8,128)(2,1)}, bf16[2,256,256]{2,1,0:T(8,128)(2,1)S(1)}) custom-call(bf16[256,256]{1,0:T(8,128)(2,1)S(1)} %collective-permute-done.8.front_ref.refs_3_, bf16[2304,256]{1,0:T(8,128)(2,1)S(1)} %bitcast.32, bf16[256,256]{1,0:T(8,128)(2,1)S(1)} %get-tuple-element.29.act_ref.refs_1_, bf16[256,256]{1,0:T(8,128)(2,1)S(1)} %shard_map.124.refs_0_), custom_call_target="tpu_custom_call" | custom-call | tf_op jit(solution)/shard_map/pallas_call | solution.py:21
  99.8 5.8 %collective-permute-start.9 = (bf16[2,256,256]{2,1,0:T(8,128)(2,1)S(1)}, bf16[2,256,256]{2,1,0:T(8,128)(2,1)S(1)}, u32[]{:S(2)}, u32[]{:S(2)}) collective-permute-start(bf16[2,256,256]{2,1,0:T(8,128)(2,1)S(1)} %get-tuple-element.14), channel_id=1, source_target_pairs={{0,480},{32,448},{64,416},{96,384},{128,352},{160,320},{192,288},{... | collective-permute-start | bytes 786440 | tf_op jit(solution)/shard_map/ppermute | solution.py:225
  105.6 2.1 %collective-permute-start.5 = (bf16[256,256]{1,0:T(8,128)(2,1)S(1)}, bf16[256,256]{1,0:T(8,128)(2,1)S(1)}, u32[]{:S(2)}, u32[]{:S(2)}) collective-permute-start(bf16[256,256]{1,0:T(8,128)(2,1)S(1)} %shard_map.123), channel_id=1, source_target_pairs={{0,480},{32,448},{64,416},{96,384},{128,352},{160,320},{192,288},{... | collective-permute-start | bytes 393224 | tf_op jit(solution)/shard_map/ppermute | solution.py:225
  107.7 0.6 shard_map.122
  108.4 0.8 pad_maximum_fusion
  109.2 13.8 %collective-permute-done.5 = bf16[256,256]{1,0:T(8,128)(2,1)S(1)} collective-permute-done((bf16[256,256]{1,0:T(8,128)(2,1)S(1)}, bf16[256,256]{1,0:T(8,128)(2,1)S(1)}, u32[]{:S(2)}, u32[]{:S(2)}) %collective-permute-start.5) | collective-permute-done | bytes 131104 | tf_op jit(solution)/shard_map/ppermute | solution.py:225
  123.0 0.8 pad_maximum_fusion.1
  123.9 0.7 fusion.2
  (31 shorter events, 1.3 us)
Async XLA Ops:
  0.6 0.9 copy-start.1
  1.5 30.0 %copy-start.4 = (bf16[3,1,1,16,16,256]{5,4,3,2,1,0:T(8,128)(2,1)S(1)}, bf16[3,1,1,16,16,256]{5,4,3,2,1,0:T(8,128)(2,1)}, u32[]{:S(2)}) copy-start(bf16[3,1,1,16,16,256]{5,4,3,2,1,0:T(8,128)(2,1)} %param.8) | copy-start | bytes 1179652
  1.5 43.2 %copy-start.7 = (bf16[1,1,16,16,256]{4,3,2,1,0:T(8,128)(2,1)S(1)}, bf16[1,1,16,16,256]{4,3,2,1,0:T(8,128)(2,1)}, u32[]{:S(2)}) copy-start(bf16[1,1,16,16,256]{4,3,2,1,0:T(8,128)(2,1)} %param.10) | copy-start | bytes 393220
  1.5 49.3 %copy-start.3 = (bf16[3,1,1,16,16,256]{5,4,3,2,1,0:T(8,128)(2,1)S(1)}, bf16[3,1,1,16,16,256]{5,4,3,2,1,0:T(8,128)(2,1)}, u32[]{:S(2)}) copy-start(bf16[3,1,1,16,16,256]{5,4,3,2,1,0:T(8,128)(2,1)} %param.7) | copy-start | bytes 1179652
  29.6 21.2 %collective-permute-start = (bf16[16,72,256]{2,1,0:T(8,128)(2,1)S(1)}, bf16[16,72,256]{2,1,0:T(8,128)(2,1)S(1)}, u32[]{:S(2)}, u32[]{:S(2)}) collective-permute-start(bf16[16,72,256]{2,1,0:T(8,128)(2,1)S(1)} %all_to_all.10.mine_ref), channel_id=1, source_target_pairs={{0,1},{1,0},{2,3},{3,2},{4,5},{5,4},{6,7},{7,6},{8,9},{9,8},{10,11... | collective-permute-start | bytes 1769480 | tf_op jit(solution)/shard_map/ppermute | solution.py:234
  31.6 41.9 %collective-permute-start.7 = (bf16[2,256,256]{2,1,0:T(8,128)(2,1)S(1)}, bf16[2,256,256]{2,1,0:T(8,128)(2,1)S(1)}, u32[]{:S(2)}, u32[]{:S(2)}) collective-permute-start(bf16[2,256,256]{2,1,0:T(8,128)(2,1)S(1)} %bitcast.47), channel_id=1, source_target_pairs={{0,480},{32,448},{64,416},{96,384},{128,352},{160,320},{192,288},{... | collective-permute-start | bytes 786440 | tf_op jit(solution)/shard_map/ppermute | solution.py:225
  42.8 21.0 %collective-permute-start.4 = (bf16[256,256]{1,0:T(8,128)(2,1)S(1)}, bf16[256,256]{1,0:T(8,128)(2,1)S(1)}, u32[]{:S(2)}, u32[]{:S(2)}) collective-permute-start(bf16[256,256]{1,0:T(8,128)(2,1)S(1)} %bitcast.48), channel_id=1, source_target_pairs={{0,480},{32,448},{64,416},{96,384},{128,352},{160,320},{192,288},{... | collective-permute-start | bytes 393224 | tf_op jit(solution)/shard_map/ppermute | solution.py:225
  44.7 21.8 %collective-permute-start.3 = (bf16[256,256]{1,0:T(8,128)(2,1)S(1)}, bf16[256,256]{1,0:T(8,128)(2,1)S(1)}, u32[]{:S(2)}, u32[]{:S(2)}) collective-permute-start(bf16[256,256]{1,0:T(8,128)(2,1)S(1)} %bitcast.50), channel_id=1, source_target_pairs={{0,480},{32,448},{64,416},{96,384},{128,352},{160,320},{192,288},{... | collective-permute-start | bytes 393224 | tf_op jit(solution)/shard_map/ppermute | solution.py:225
  50.8 0.9 copy-start
  52.4 21.1 %collective-permute-start.1 = (bf16[256,256]{1,0:T(8,128)(2,1)S(1)}, bf16[256,256]{1,0:T(8,128)(2,1)S(1)}, u32[]{:S(2)}, u32[]{:S(2)}) collective-permute-start(bf16[256,256]{1,0:T(8,128)(2,1)S(1)} %shard_map.120), channel_id=1, source_target_pairs={{32,0},{64,32},{96,64},{128,96},{160,128},{192,160},{224,192},{256... | collective-permute-start | bytes 393224 | tf_op jit(solution)/shard_map/ppermute | solution.py:230
  67.2 9.1 %collective-permute-start.6 = (bf16[256,256]{1,0:T(8,128)(2,1)S(1)}, bf16[256,256]{1,0:T(8,128)(2,1)S(1)}, u32[]{:S(2)}, u32[]{:S(2)}) collective-permute-start(bf16[256,256]{1,0:T(8,128)(2,1)S(1)} %shard_map.123), channel_id=1, source_target_pairs={{32,0},{64,32},{96,64},{128,96},{160,128},{192,160},{224,192},{256... | collective-permute-start | bytes 393224 | tf_op jit(solution)/shard_map/ppermute | solution.py:230
  74.1 11.6 %collective-permute-start.2 = (bf16[256,256]{1,0:T(8,128)(2,1)S(1)}, bf16[256,256]{1,0:T(8,128)(2,1)S(1)}, u32[]{:S(2)}, u32[]{:S(2)}) collective-permute-start(bf16[256,256]{1,0:T(8,128)(2,1)S(1)} %shard_map.121), channel_id=1, source_target_pairs={{32,0},{64,32},{96,64},{128,96},{160,128},{192,160},{224,192},{256... | collective-permute-start | bytes 393224 | tf_op jit(solution)/shard_map/ppermute | solution.py:230
  76.9 9.0 %collective-permute-start.8 = (bf16[256,256]{1,0:T(8,128)(2,1)S(1)}, bf16[256,256]{1,0:T(8,128)(2,1)S(1)}, u32[]{:S(2)}, u32[]{:S(2)}) collective-permute-start(bf16[256,256]{1,0:T(8,128)(2,1)S(1)} %shard_map.124.refs_0_), channel_id=1, source_target_pairs={{32,0},{64,32},{96,64},{128,96},{160,128},{192,160},{224,192},{256... | collective-permute-start | bytes 393224 | tf_op jit(solution)/shard_map/ppermute | solution.py:230
  86.9 3.9 %collective-permute-start.10 = (bf16[16,72,256]{2,1,0:T(8,128)(2,1)S(1)}, bf16[16,72,256]{2,1,0:T(8,128)(2,1)S(1)}, u32[]{:S(2)}, u32[]{:S(2)}) collective-permute-start(bf16[16,72,256]{2,1,0:T(8,128)(2,1)S(1)} %get-tuple-element.21), channel_id=1, source_target_pairs={{0,1},{1,0},{2,3},{3,2},{4,5},{5,4},{6,7},{7,6},{8,9},{9,8},{10,11... | collective-permute-start | bytes 1769480 | tf_op jit(solution)/shard_map/ppermute | solution.py:234
  91.8 32.0 %all-to-all-start.1 = ((bf16[16,72,256]{2,1,0:T(8,128)(2,1)}), bf16[16,72,256]{2,1,0:T(8,128)(2,1)S(1)}, u32[]{:S(2)}, u32[]{:S(2)}) async-start(bf16[16,72,256]{2,1,0:T(8,128)(2,1)} %shard_map.131), calls=%async_computation.1 | async-start | bytes 1179648 | tf_op jit(solution)/shard_map/all_to_all | solution.py:272
  99.8 23.2 %collective-permute-start.9 = (bf16[2,256,256]{2,1,0:T(8,128)(2,1)S(1)}, bf16[2,256,256]{2,1,0:T(8,128)(2,1)S(1)}, u32[]{:S(2)}, u32[]{:S(2)}) collective-permute-start(bf16[2,256,256]{2,1,0:T(8,128)(2,1)S(1)} %get-tuple-element.14), channel_id=1, source_target_pairs={{0,480},{32,448},{64,416},{96,384},{128,352},{160,320},{192,288},{... | collective-permute-start | bytes 786440 | tf_op jit(solution)/shard_map/ppermute | solution.py:225
  105.6 17.4 %collective-permute-start.5 = (bf16[256,256]{1,0:T(8,128)(2,1)S(1)}, bf16[256,256]{1,0:T(8,128)(2,1)S(1)}, u32[]{:S(2)}, u32[]{:S(2)}) collective-permute-start(bf16[256,256]{1,0:T(8,128)(2,1)S(1)} %shard_map.123), channel_id=1, source_target_pairs={{0,480},{32,448},{64,416},{96,384},{128,352},{160,320},{192,288},{... | collective-permute-start | bytes 393224 | tf_op jit(solution)/shard_map/ppermute | solution.py:225
  108.3 15.5 %copy-start.2 = (f32[1,72,256]{2,1,0:T(8,128)S(1)}, f32[1,72,256]{2,1,0:T(8,128)}, u32[]{:S(2)}) copy-start(f32[1,72,256]{2,1,0:T(8,128)} %param.11) | copy-start | bytes 221188
  108.3 15.5 %copy-start.5 = (f32[1,72,256]{2,1,0:T(8,128)S(1)}, f32[1,72,256]{2,1,0:T(8,128)}, u32[]{:S(2)}) copy-start(f32[1,72,256]{2,1,0:T(8,128)} %param.13) | copy-start | bytes 221188
  108.4 15.5 %copy-start.6 = (f32[1,72,256]{2,1,0:T(8,128)S(1)}, f32[1,72,256]{2,1,0:T(8,128)}, u32[]{:S(2)}) copy-start(f32[1,72,256]{2,1,0:T(8,128)} %param.12) | copy-start | bytes 221188

commit v4 on v3

--- a/solution.py
+++ b/solution.py
@@ -52,17 +52,35 @@
     return bent, 0.5 * (1.0 + bent)
 
 
-def hidden_kernel(*refs):
-    acts, outs = refs[: len(refs) // 2], refs[len(refs) // 2 :]
-    for act_ref, out_ref in zip(acts, outs):
-        x = act_ref[...].astype(jnp.float32)
+def split(pieces):
+    arrays = [array for array, _ in pieces]
+
+    def read(refs):
+        return [ref[index] for ref, (_, index) in zip(refs, pieces)]
+
+    return arrays, read
+
+
+def hidden_kernel(read, count, *refs):
+    for act, out_ref in zip(read(refs[:count]), refs[count:]):
+        x = act.astype(jnp.float32)
         hidden = (x * bend(x)[1]).astype(jnp.bfloat16)
         out_ref[...] = hidden.astype(jnp.float32).T.astype(jnp.bfloat16)
 
 
 def hidden_parts(acts):
-    outs = [(act.shape[::-1], jnp.bfloat16) for act in acts]
-    return call(hidden_kernel, outs, acts, off_chip=True)
+    arrays, read = split(acts)
+    outs = [(arrays[0].shape[:0:-1], jnp.bfloat16)] * len(arrays)
+    body = functools.partial(hidden_kernel, read, len(arrays))
+    return call(body, outs, arrays, off_chip=True)
+
+
+def keep_kernel(front_ref, out_ref):
+    out_ref[...] = front_ref[...]
+
+
+def keep(front):
+    return call(keep_kernel, [(front.shape, front.dtype)], [front])[0]
 
 
 def fill_taps(front, pad_ref, width):
@@ -82,9 +100,10 @@
     return pltpu.VMEM((count, 3, pixels + 2 * width, channels), jnp.bfloat16)
 
 
-def tick_kernel(width, factor, front_ref, weight_ref, act_ref, *refs):
-    earlier, (out_ref, *pair, pad_ref) = refs[: len(refs) // 2 - 1], refs[len(refs) // 2 - 1 :]
-    front = front_ref[...]
+def tick_kernel(read, width, factor, *refs):
+    front_ref, act_ref, weight_ref, *earlier = refs[: len(refs) // 2 + 1]
+    out_ref, *pair, pad_ref = refs[len(refs) // 2 + 1 :]
+    front, act = read((front_ref, act_ref))
     pixels, channels = front.shape
     fill_taps(front, pad_ref.at[0], width)
     total = jnp.zeros((pixels, channels), jnp.float32)
@@ -97,7 +116,7 @@
                 (((1,), (1,)), ((), ())),
                 preferred_element_type=jnp.float32,
             )
-    x = act_ref[...].astype(jnp.float32)
+    x = act.astype(jnp.float32)
     bent, half = bend(x)
     inner = 0.7978845608028654 * (1.0 + 3.0 * 0.044715 * x * x)
     slope = half + 0.5 * x * (1.0 - bent * bent) * inner
@@ -108,25 +127,26 @@
         pair[0][1] = out
 
 
-def tick(front, weight, act, width, earlier=None):
-    pixels, channels = front.shape
-    factor = (9 * channels) ** -0.5
-    outs = [(front.shape, jnp.bfloat16)]
-    args = [front, weight, act]
+def tick(front, act, weight, width, earlier=None):
+    arrays, read = split([front, act])
+    channels = weight.shape[1]
+    pixels = act[0].shape[-2]
+    outs = [((pixels, channels), jnp.bfloat16)]
+    args = [*arrays, weight]
     if earlier is not None:
-        outs.append(((2, *front.shape), jnp.bfloat16))
+        outs.append(((2, pixels, channels), jnp.bfloat16))
         args.append(earlier)
     return call(
-        functools.partial(tick_kernel, width, factor),
+        functools.partial(tick_kernel, read, width, (9 * channels) ** -0.5),
         outs,
         args,
         [pads(1, pixels, width, channels)],
     )
 
 
-def add_terms(hiddens, front_refs, pad_ref, width, write):
-    for j, front_ref in enumerate(front_refs):
-        fill_taps(front_ref[...], pad_ref.at[j], width)
+def add_terms(hiddens, fronts, pad_ref, width, write):
+    for j, front in enumerate(fronts):
+        fill_taps(front, pad_ref.at[j], width)
     channels, pixels = hiddens[0].shape
     for a in range(3):
         for b in range(3):
@@ -141,27 +161,28 @@
             write((3 * a + b) * channels, total)
 
 
-def early_kernel(width, *refs):
+def early_kernel(read, width, *refs):
     count = len(refs) // 2 - 1
     hid_refs, front_refs, (out_ref, pad_ref) = refs[:count], refs[count:-2], refs[-2:]
 
     def write(row, total):
         out_ref[row : row + total.shape[0]] = total
 
-    add_terms(hid_refs, front_refs, pad_ref, width, write)
+    add_terms(hid_refs, read(front_refs), pad_ref, width, write)
 
 
 def early_terms(hiddens, fronts, width):
     channels, pixels = hiddens[0].shape
+    arrays, read = split(fronts)
     return call(
-        functools.partial(early_kernel, width),
+        functools.partial(early_kernel, read, width),
         [((9 * channels, channels), jnp.float32)],
-        [*hiddens, *fronts],
+        [*hiddens, *arrays],
         [pads(len(fronts), pixels, width, channels)],
     )[0]
 
 
-def last_kernel(width, factor, core_ref, total_ref, *refs):
+def last_kernel(read, width, factor, core_ref, total_ref, *refs):
     count = len(refs) // 2 - 2
     hid_refs, front_refs = refs[:count], refs[count:-4]
     kept_ref, given_ref, sum_ref, pad_ref = refs[-4:]
@@ -171,7 +192,7 @@
         at = slice(row, row + total.shape[0])
         sum_ref[at] = factor * (total_ref[at] + total)
 
-    add_terms(hid_refs, front_refs, pad_ref, width, write)
+    add_terms(hid_refs, read(front_refs), pad_ref, width, write)
     for core, places in enumerate(((kept_ref, given_ref), (given_ref, kept_ref))):
 
         @pl.when(core_ref[0] == core)
@@ -183,10 +204,11 @@
 def last_terms(core, total, hiddens, fronts, chips, width):
     channels, pixels = hiddens[0].shape
     half = (chips, 9 * channels // (2 * chips), channels)
+    arrays, read = split(fronts)
     return call(
-        functools.partial(last_kernel, width, (9 * channels) ** -0.5),
+        functools.partial(last_kernel, read, width, (9 * channels) ** -0.5),
         [(half, jnp.bfloat16), (half, jnp.bfloat16)],
-        [core, total, *hiddens, *fronts],
+        [core, total, *hiddens, *arrays],
         [
             pltpu.VMEM((9 * channels, channels), jnp.float32),
             pads(len(fronts), pixels, width, channels),
@@ -239,33 +261,34 @@
     flat = (height * width, channels)
     chips = lax.axis_size(CHIPS)
     core = lax.axis_index("core").astype(jnp.int32).reshape(1)
-    acts_down = [acts_down[t].reshape(flat) for t in range(ticks)]
+    whole = slice(None)
+    acts_down = acts_down.reshape(ticks, *flat)
     acts_up = acts_up.reshape(ticks, *flat)
     mine = lax.all_to_all(spread(master[0], chips), CHIPS, 0, 0, tiled=True)
-    front_up = to_mirror(front_up.reshape(flat))
-    far_act = to_mirror(acts_up[0])
+    far_first = to_mirror(jnp.stack([front_up.reshape(flat), acts_up[0]]))
     far_rest = to_mirror(acts_up[1:])
+    front_down = keep(front_down.reshape(flat))
+    acts_down = [(acts_down, t) for t in range(ticks)]
+    acts_up = [(far_first, 1)] + [(far_rest, t) for t in range(ticks - 1)]
     hid_down = hidden_parts(acts_down)
-    hid_up = hidden_parts([far_act])
-    acts_up = [far_act, *far_rest]
     other = to_partner(mine)
     weight = weave(core, mine, other)
-    down, up = [front_down.reshape(flat)], [front_up]
+    down, up = [(front_down, whole)], [(far_first, 0)]
     outs_down, outs_up = [], []
     for t in range(ticks):
-        next_down = tick(down[t], weight, acts_down[t], width)[0]
+        next_down = tick(down[t], acts_down[t], weight, width)[0]
         if t + 1 < ticks:
-            next_up = tick(up[t], weight, acts_up[t], width)[0]
+            next_up = tick(up[t], acts_up[t], weight, width)[0]
         else:
-            next_up, pair = tick(up[t], weight, acts_up[t], width, outs_up[1])
+            next_up, pair = tick(up[t], acts_up[t], weight, width, outs_up[1])
         outs_down.append(next_down)
         outs_up.append(next_up)
         if t + 1 < ticks:
-            down.append(from_next(next_down))
-            up.append(from_next(next_up))
+            down.append((from_next(next_down), whole))
+            up.append((from_next(next_up), whole))
+    hid_up = hidden_parts(acts_up)
+    total = early_terms([*hid_down[:2], *hid_up[:2]], down[:2] + up[:2], width)
     first = to_mirror(outs_up[0])
-    hid_up = hid_up + hidden_parts(acts_up[1:])
-    total = early_terms([*hid_down[:2], *hid_up[:2]], down[:2] + up[:2], width)
     kept, given = last_terms(core, total, [hid_down[2], hid_up[2]], [down[2], up[2]], chips, width)
     taken = to_partner(given)
     both = pair_add(kept, taken)

time: 125 us -> 124 us (level)
  starting transfers between devices: 54.2 us -> 52.3 us
    ppermute x5 -> x4, starting transfers between devices: 27.1 us -> 21.1 us  [to_mirror(): lax.ppermute(value, SECTION, [(i, length - 1 - i) for i in range(length)])]
    ppermute x4, starting transfers between devices: 16.6 us -> 20.7 us  [from_next(): return lax.ppermute(value, SECTION, [(i + 1, i) for i in range(length - 1)])]
    ppermute x5 -> x4, waiting for transfers between devices: 26.1 us -> 22.6 us  [to_mirror(): lax.ppermute(value, SECTION, [(i, length - 1 - i) for i in range(length)])]
    ppermute x4, waiting for transfers between devices: 0.52 us -> 4.04 us  [from_next(): return lax.ppermute(value, SECTION, [(i + 1, i) for i in range(length - 1)])]
  transfers between devices with their start and end apart: 12 -> 11, of which waited for: 6 -> 5; matrix products, arithmetic and copies ran while one was open for 1% -> 2% of each run, Pallas kernels for 5% -> 5%
where the time goes in v4:
time: 124 us; the launch traced here: 123 us
  starting transfers between devices  52.3 us (42%)
  waiting for transfers between devices  28.6 us (23%)
  blocking collectives  28 us (23%)
  Pallas kernels  8.58 us (7%)
  other arithmetic  3.1 us (2%)
  local copies, waits for them, and re-layouts  1.83 us (1%)
    all_to_all x1, blocking collectives, step(): mine = lax.all_to_all(spread(master[0], chips), CHIPS, 0, 0, tiled=True)  28 us
    ppermute x4, waiting for transfers between devices, to_mirror(): lax.ppermute(value, SECTION, [(i, length - 1 - i) for i in range(length)])  22.6 us
    ppermute x4, starting transfers between devices, to_mirror(): lax.ppermute(value, SECTION, [(i, length - 1 - i) for i in range(length)])  21.1 us
    ppermute x4, starting transfers between devices, from_next(): return lax.ppermute(value, SECTION, [(i + 1, i) for i in range(length - 1)])  20.7 us
    pallas_call x14, Pallas kernels, call(): pl.pallas_call(body, in_specs=specs, out_specs=[VMEM] * len(outs), out_sh...  8.58 us
    all_to_all x1, starting transfers between devices, step(): pieces = lax.all_to_all(both, CHIPS, 0, 0, tiled=True)  6.68 us
    ppermute x4, waiting for transfers between devices, from_next(): return lax.ppermute(value, SECTION, [(i + 1, i) for i in range(length - 1)])  4.04 us
    ppermute x2, starting transfers between devices, to_partner(): return lax.ppermute(value, 'core', [(0, 1), (1, 0)])  3.83 us
  transfers between devices with their start and end apart: 11, of which 5 were waited for; matrix products, arithmetic and copies ran while one was open for 2% of the time, Pallas kernels for 5%

profile of v4, /device:TPU:6, one launch (start us, length us, event | category | flops | bytes accessed | tf_op | source)
XLA Modules:
  0.0 123.3 jit_solution(10395877794347554133)
XLA Ops:
  0.6 0.9 copy-done.1
  1.6 28.0 %all_to_all.10.mine_ref = bf16[16,72,256]{2,1,0:T(8,128)(2,1)S(1)} all-to-all(bf16[16,72,256]{2,1,0:T(8,128)(2,1)S(1)} %shard_map.119), channel_id=1, replica_groups=mesh['x_lo'=2,'z'=8,'x_hi'=2,'y'=8,'core'=2] {'x_hi','y'}, dimensions={0} | all-to-all | bytes 1179648 | tf_op jit(solution)/shard_map/all_to_all | solution.py:267
  29.6 1.9 %collective-permute-start = (bf16[16,72,256]{2,1,0:T(8,128)(2,1)S(1)}, bf16[16,72,256]{2,1,0:T(8,128)(2,1)S(1)}, u32[]{:S(2)}, u32[]{:S(2)}) collective-permute-start(bf16[16,72,256]{2,1,0:T(8,128)(2,1)S(1)} %all_to_all.10.mine_ref), channel_id=1, source_target_pairs={{0,1},{1,0},{2,3},{3,2},{4,5},{5,4},{6,7},{7,6},{8,9},{9,8},{10,11... | collective-permute-start | bytes 1769480 | tf_op jit(solution)/shard_map/ppermute | solution.py:256
  31.6 0.7 pad_maximum_fusion.2
  32.3 11.2 %collective-permute-start.3 = (bf16[2,256,256]{2,1,0:T(8,128)(2,1)}, bf16[2,256,256]{2,1,0:T(8,128)(2,1)S(1)}, u32[]{:S(2)}, u32[]{:S(2)}) collective-permute-start(bf16[2,256,256]{2,1,0:T(8,128)(2,1)} %pad_maximum_fusion.2), channel_id=1, source_target_pairs={{0,480},{32,448},{64,416},{96,384},{128,352},{160,320},{192,288},{... | collective-permute-start | bytes 786440 | tf_op jit(solution)/shard_map/ppermute | solution.py:247
  43.5 1.9 %collective-permute-start.6 = (bf16[2,256,256]{2,1,0:T(8,128)(2,1)S(1)}, bf16[2,256,256]{2,1,0:T(8,128)(2,1)S(1)}, u32[]{:S(2)}, u32[]{:S(2)}) collective-permute-start(bf16[2,256,256]{2,1,0:T(8,128)(2,1)S(1)} %bitcast.41), channel_id=1, source_target_pairs={{0,480},{32,448},{64,416},{96,384},{128,352},{160,320},{192,288},{... | collective-permute-start | bytes 786440 | tf_op jit(solution)/shard_map/ppermute | solution.py:247
  45.6 0.9 copy-done
  46.5 0.6 shard_map.121
  47.1 6.0 %collective-permute-start.1 = (bf16[256,256]{1,0:T(8,128)(2,1)S(1)}, bf16[256,256]{1,0:T(8,128)(2,1)S(1)}, u32[]{:S(2)}, u32[]{:S(2)}) collective-permute-start(bf16[256,256]{1,0:T(8,128)(2,1)S(1)} %shard_map.121), channel_id=1, source_target_pairs={{32,0},{64,32},{96,64},{128,96},{160,128},{192,160},{224,192},{256... | collective-permute-start | bytes 393224 | tf_op jit(solution)/shard_map/ppermute | solution.py:252
  53.2 8.7 %collective-permute-done.3.refs_0_.refs_1_.refs_6_ = bf16[2,256,256]{2,1,0:T(8,128)(2,1)S(1)} collective-permute-done((bf16[2,256,256]{2,1,0:T(8,128)(2,1)}, bf16[2,256,256]{2,1,0:T(8,128)(2,1)S(1)}, u32[]{:S(2)}, u32[]{:S(2)}) %collective-permute-start.3) | collective-permute-done | bytes 262176 | tf_op jit(solution)/shard_map/ppermute | solution.py:247
  61.9 0.6 shard_map.124
  62.5 6.2 %collective-permute-start.5 = (bf16[256,256]{1,0:T(8,128)(2,1)S(1)}, bf16[256,256]{1,0:T(8,128)(2,1)S(1)}, u32[]{:S(2)}, u32[]{:S(2)}) collective-permute-start(bf16[256,256]{1,0:T(8,128)(2,1)S(1)} %shard_map.124), channel_id=1, source_target_pairs={{32,0},{64,32},{96,64},{128,96},{160,128},{192,160},{224,192},{256... | collective-permute-start | bytes 393224 | tf_op jit(solution)/shard_map/ppermute | solution.py:252
  68.8 1.3 %collective-permute-done.1.refs_0_.refs_5_ = bf16[256,256]{1,0:T(8,128)(2,1)S(1)} collective-permute-done((bf16[256,256]{1,0:T(8,128)(2,1)S(1)}, bf16[256,256]{1,0:T(8,128)(2,1)S(1)}, u32[]{:S(2)}, u32[]{:S(2)}) %collective-permute-start.1) | collective-permute-done | bytes 131104 | tf_op jit(solution)/shard_map/ppermute | solution.py:252
  70.1 0.6 shard_map.122
  70.7 6.5 %collective-permute-start.2 = (bf16[256,256]{1,0:T(8,128)(2,1)S(1)}, bf16[256,256]{1,0:T(8,128)(2,1)S(1)}, u32[]{:S(2)}, u32[]{:S(2)}) collective-permute-start(bf16[256,256]{1,0:T(8,128)(2,1)S(1)} %shard_map.122), channel_id=1, source_target_pairs={{32,0},{64,32},{96,64},{128,96},{160,128},{192,160},{224,192},{256... | collective-permute-start | bytes 393224 | tf_op jit(solution)/shard_map/ppermute | solution.py:252
  77.2 0.6 shard_map.125.refs_3_
  77.8 1.9 %collective-permute-start.7 = (bf16[256,256]{1,0:T(8,128)(2,1)S(1)}, bf16[256,256]{1,0:T(8,128)(2,1)S(1)}, u32[]{:S(2)}, u32[]{:S(2)}) collective-permute-start(bf16[256,256]{1,0:T(8,128)(2,1)S(1)} %shard_map.125.refs_3_), channel_id=1, source_target_pairs={{32,0},{64,32},{96,64},{128,96},{160,128},{192,160},{224,192},{256... | collective-permute-start | bytes 393224 | tf_op jit(solution)/shard_map/ppermute | solution.py:252
  80.5 1.4 %shard_map.129.total_ref = f32[2304,256]{1,0:T(8,128)S(1)} custom-call(bf16[256,256]{1,0:T(8,128)(2,1)S(1)} %get-tuple-element.16.refs_0_, bf16[256,256]{1,0:T(8,128)(2,1)S(1)} %get-tuple-element.17.refs_1_, bf16[256,256]{1,0:T(8,128)(2,1)S(1)} %get-tuple-element.18.refs_2_, bf16[256,256]{1,0:T(8,128)(2,1)S(1)} %get-tuple-element.19.refs_3_, ...), custom_call_target="tpu_custom_call" | custom-call | tf_op jit(solution)/shard_map/pallas_call | solution.py:21
  81.9 2.7 %collective-permute-done.7.refs_0_.refs_3_ = bf16[256,256]{1,0:T(8,128)(2,1)S(1)} collective-permute-done((bf16[256,256]{1,0:T(8,128)(2,1)S(1)}, bf16[256,256]{1,0:T(8,128)(2,1)S(1)}, u32[]{:S(2)}, u32[]{:S(2)}) %collective-permute-start.7) | collective-permute-done | bytes 131104 | tf_op jit(solution)/shard_map/ppermute | solution.py:252
  84.7 1.0 shard_map.130
  85.7 1.9 %collective-permute-start.9 = (bf16[16,72,256]{2,1,0:T(8,128)(2,1)S(1)}, bf16[16,72,256]{2,1,0:T(8,128)(2,1)S(1)}, u32[]{:S(2)}, u32[]{:S(2)}) collective-permute-start(bf16[16,72,256]{2,1,0:T(8,128)(2,1)S(1)} %get-tuple-element.23), channel_id=1, source_target_pairs={{0,1},{1,0},{2,3},{3,2},{4,5},{5,4},{6,7},{7,6},{8,9},{9,8},{10,11... | collective-permute-start | bytes 1769480 | tf_op jit(solution)/shard_map/ppermute | solution.py:256
  87.6 2.0 %collective-permute-done.9.two_ref = bf16[16,72,256]{2,1,0:T(8,128)(2,1)S(1)} collective-permute-done((bf16[16,72,256]{2,1,0:T(8,128)(2,1)S(1)}, bf16[16,72,256]{2,1,0:T(8,128)(2,1)S(1)}, u32[]{:S(2)}, u32[]{:S(2)}) %collective-permute-start.9) | collective-permute-done | bytes 589856 | tf_op jit(solution)/shard_map/ppermute | solution.py:256
  89.6 1.0 shard_map.131
  90.5 6.7 %all-to-all-start.1 = ((bf16[16,72,256]{2,1,0:T(8,128)(2,1)}), bf16[16,72,256]{2,1,0:T(8,128)(2,1)S(1)}, u32[]{:S(2)}, u32[]{:S(2)}) async-start(bf16[16,72,256]{2,1,0:T(8,128)(2,1)} %shard_map.131), calls=%async_computation.1 | async-start | bytes 1179648 | tf_op jit(solution)/shard_map/all_to_all | solution.py:295
  97.2 1.3 %shard_map.126 = (bf16[256,256]{1,0:T(8,128)(2,1)}, bf16[2,256,256]{2,1,0:T(8,128)(2,1)S(1)}) custom-call(bf16[256,256]{1,0:T(8,128)(2,1)S(1)} %collective-permute-done.7.refs_0_.refs_3_, bf16[2,256,256]{2,1,0:T(8,128)(2,1)S(1)} %collective-permute-done.6.refs_1_.refs_2_, bf16[2304,256]{1,0:T(8,128)(2,1)S(1)} %bitcast.26, ...), custom_call_target="tpu_custom_call" | custom-call | tf_op jit(solution)/shard_map/pallas_call | solution.py:21
  98.5 3.7 %collective-permute-start.8 = (bf16[2,256,256]{2,1,0:T(8,128)(2,1)S(1)}, bf16[2,256,256]{2,1,0:T(8,128)(2,1)S(1)}, u32[]{:S(2)}, u32[]{:S(2)}) collective-permute-start(bf16[2,256,256]{2,1,0:T(8,128)(2,1)S(1)} %get-tuple-element.15), channel_id=1, source_target_pairs={{0,480},{32,448},{64,416},{96,384},{128,352},{160,320},{192,288},{... | collective-permute-start | bytes 786440 | tf_op jit(solution)/shard_map/ppermute | solution.py:247
  102.1 4.3 %collective-permute-start.4 = (bf16[256,256]{1,0:T(8,128)(2,1)S(1)}, bf16[256,256]{1,0:T(8,128)(2,1)S(1)}, u32[]{:S(2)}, u32[]{:S(2)}) collective-permute-start(bf16[256,256]{1,0:T(8,128)(2,1)S(1)} %shard_map.124), channel_id=1, source_target_pairs={{0,480},{32,448},{64,416},{96,384},{128,352},{160,320},{192,288},{... | collective-permute-start | bytes 393224 | tf_op jit(solution)/shard_map/ppermute | solution.py:247
  106.4 0.6 shard_map.123
  107.1 0.8 pad_maximum_fusion
  107.9 13.8 %collective-permute-done.4 = bf16[256,256]{1,0:T(8,128)(2,1)S(1)} collective-permute-done((bf16[256,256]{1,0:T(8,128)(2,1)S(1)}, bf16[256,256]{1,0:T(8,128)(2,1)S(1)}, u32[]{:S(2)}, u32[]{:S(2)}) %collective-permute-start.4) | collective-permute-done | bytes 131104 | tf_op jit(solution)/shard_map/ppermute | solution.py:247
  121.7 0.8 pad_maximum_fusion.1
  122.6 0.7 fusion.2
  (28 shorter events, 1.0 us)
Async XLA Ops:
  0.6 0.9 copy-start.1
  1.5 30.0 %copy-start.4 = (bf16[3,1,1,16,16,256]{5,4,3,2,1,0:T(8,128)(2,1)S(1)}, bf16[3,1,1,16,16,256]{5,4,3,2,1,0:T(8,128)(2,1)}, u32[]{:S(2)}) copy-start(bf16[3,1,1,16,16,256]{5,4,3,2,1,0:T(8,128)(2,1)} %param.8) | copy-start | bytes 1179652
  1.5 30.0 %copy-start.5 = (bf16[1,1,16,16,256]{4,3,2,1,0:T(8,128)(2,1)S(1)}, bf16[1,1,16,16,256]{4,3,2,1,0:T(8,128)(2,1)}, u32[]{:S(2)}) copy-start(bf16[1,1,16,16,256]{4,3,2,1,0:T(8,128)(2,1)} %param.10) | copy-start | bytes 393220
  1.6 43.9 %copy-start.3 = (bf16[1,1,16,16,256]{4,3,2,1,0:T(8,128)(2,1)S(1)}, bf16[1,1,16,16,256]{4,3,2,1,0:T(8,128)(2,1)}, u32[]{:S(2)}) copy-start(bf16[1,1,16,16,256]{4,3,2,1,0:T(8,128)(2,1)} %param.9) | copy-start | bytes 393220
  29.6 15.9 %collective-permute-start = (bf16[16,72,256]{2,1,0:T(8,128)(2,1)S(1)}, bf16[16,72,256]{2,1,0:T(8,128)(2,1)S(1)}, u32[]{:S(2)}, u32[]{:S(2)}) collective-permute-start(bf16[16,72,256]{2,1,0:T(8,128)(2,1)S(1)} %all_to_all.10.mine_ref), channel_id=1, source_target_pairs={{0,1},{1,0},{2,3},{3,2},{4,5},{5,4},{6,7},{7,6},{8,9},{9,8},{10,11... | collective-permute-start | bytes 1769480 | tf_op jit(solution)/shard_map/ppermute | solution.py:256
  32.3 29.6 %collective-permute-start.3 = (bf16[2,256,256]{2,1,0:T(8,128)(2,1)}, bf16[2,256,256]{2,1,0:T(8,128)(2,1)S(1)}, u32[]{:S(2)}, u32[]{:S(2)}) collective-permute-start(bf16[2,256,256]{2,1,0:T(8,128)(2,1)} %pad_maximum_fusion.2), channel_id=1, source_target_pairs={{0,480},{32,448},{64,416},{96,384},{128,352},{160,320},{192,288},{... | collective-permute-start | bytes 786440 | tf_op jit(solution)/shard_map/ppermute | solution.py:247
  43.5 33.6 %collective-permute-start.6 = (bf16[2,256,256]{2,1,0:T(8,128)(2,1)S(1)}, bf16[2,256,256]{2,1,0:T(8,128)(2,1)S(1)}, u32[]{:S(2)}, u32[]{:S(2)}) collective-permute-start(bf16[2,256,256]{2,1,0:T(8,128)(2,1)S(1)} %bitcast.41), channel_id=1, source_target_pairs={{0,480},{32,448},{64,416},{96,384},{128,352},{160,320},{192,288},{... | collective-permute-start | bytes 786440 | tf_op jit(solution)/shard_map/ppermute | solution.py:247
  45.5 1.0 copy-start
  47.1 22.9 %collective-permute-start.1 = (bf16[256,256]{1,0:T(8,128)(2,1)S(1)}, bf16[256,256]{1,0:T(8,128)(2,1)S(1)}, u32[]{:S(2)}, u32[]{:S(2)}) collective-permute-start(bf16[256,256]{1,0:T(8,128)(2,1)S(1)} %shard_map.121), channel_id=1, source_target_pairs={{32,0},{64,32},{96,64},{128,96},{160,128},{192,160},{224,192},{256... | collective-permute-start | bytes 393224 | tf_op jit(solution)/shard_map/ppermute | solution.py:252
  62.5 14.7 %collective-permute-start.5 = (bf16[256,256]{1,0:T(8,128)(2,1)S(1)}, bf16[256,256]{1,0:T(8,128)(2,1)S(1)}, u32[]{:S(2)}, u32[]{:S(2)}) collective-permute-start(bf16[256,256]{1,0:T(8,128)(2,1)S(1)} %shard_map.124), channel_id=1, source_target_pairs={{32,0},{64,32},{96,64},{128,96},{160,128},{192,160},{224,192},{256... | collective-permute-start | bytes 393224 | tf_op jit(solution)/shard_map/ppermute | solution.py:252
  70.7 11.3 %collective-permute-start.2 = (bf16[256,256]{1,0:T(8,128)(2,1)S(1)}, bf16[256,256]{1,0:T(8,128)(2,1)S(1)}, u32[]{:S(2)}, u32[]{:S(2)}) collective-permute-start(bf16[256,256]{1,0:T(8,128)(2,1)S(1)} %shard_map.122), channel_id=1, source_target_pairs={{32,0},{64,32},{96,64},{128,96},{160,128},{192,160},{224,192},{256... | collective-permute-start | bytes 393224 | tf_op jit(solution)/shard_map/ppermute | solution.py:252
  77.8 6.9 %collective-permute-start.7 = (bf16[256,256]{1,0:T(8,128)(2,1)S(1)}, bf16[256,256]{1,0:T(8,128)(2,1)S(1)}, u32[]{:S(2)}, u32[]{:S(2)}) collective-permute-start(bf16[256,256]{1,0:T(8,128)(2,1)S(1)} %shard_map.125.refs_3_), channel_id=1, source_target_pairs={{32,0},{64,32},{96,64},{128,96},{160,128},{192,160},{224,192},{256... | collective-permute-start | bytes 393224 | tf_op jit(solution)/shard_map/ppermute | solution.py:252
  85.7 3.9 %collective-permute-start.9 = (bf16[16,72,256]{2,1,0:T(8,128)(2,1)S(1)}, bf16[16,72,256]{2,1,0:T(8,128)(2,1)S(1)}, u32[]{:S(2)}, u32[]{:S(2)}) collective-permute-start(bf16[16,72,256]{2,1,0:T(8,128)(2,1)S(1)} %get-tuple-element.23), channel_id=1, source_target_pairs={{0,1},{1,0},{2,3},{3,2},{4,5},{5,4},{6,7},{7,6},{8,9},{9,8},{10,11... | collective-permute-start | bytes 1769480 | tf_op jit(solution)/shard_map/ppermute | solution.py:256
  90.5 31.9 %all-to-all-start.1 = ((bf16[16,72,256]{2,1,0:T(8,128)(2,1)}), bf16[16,72,256]{2,1,0:T(8,128)(2,1)S(1)}, u32[]{:S(2)}, u32[]{:S(2)}) async-start(bf16[16,72,256]{2,1,0:T(8,128)(2,1)} %shard_map.131), calls=%async_computation.1 | async-start | bytes 1179648 | tf_op jit(solution)/shard_map/all_to_all | solution.py:295
  98.5 23.2 %collective-permute-start.8 = (bf16[2,256,256]{2,1,0:T(8,128)(2,1)S(1)}, bf16[2,256,256]{2,1,0:T(8,128)(2,1)S(1)}, u32[]{:S(2)}, u32[]{:S(2)}) collective-permute-start(bf16[2,256,256]{2,1,0:T(8,128)(2,1)S(1)} %get-tuple-element.15), channel_id=1, source_target_pairs={{0,480},{32,448},{64,416},{96,384},{128,352},{160,320},{192,288},{... | collective-permute-start | bytes 786440 | tf_op jit(solution)/shard_map/ppermute | solution.py:247
  102.1 19.5 %collective-permute-start.4 = (bf16[256,256]{1,0:T(8,128)(2,1)S(1)}, bf16[256,256]{1,0:T(8,128)(2,1)S(1)}, u32[]{:S(2)}, u32[]{:S(2)}) collective-permute-start(bf16[256,256]{1,0:T(8,128)(2,1)S(1)} %shard_map.124), channel_id=1, source_target_pairs={{0,480},{32,448},{64,416},{96,384},{128,352},{160,320},{192,288},{... | collective-permute-start | bytes 393224 | tf_op jit(solution)/shard_map/ppermute | solution.py:247
  107.1 15.5 %copy-start.2 = (f32[1,72,256]{2,1,0:T(8,128)S(1)}, f32[1,72,256]{2,1,0:T(8,128)}, u32[]{:S(2)}) copy-start(f32[1,72,256]{2,1,0:T(8,128)} %param.11) | copy-start | bytes 221188
  107.1 15.5 %copy-start.6 = (f32[1,72,256]{2,1,0:T(8,128)S(1)}, f32[1,72,256]{2,1,0:T(8,128)}, u32[]{:S(2)}) copy-start(f32[1,72,256]{2,1,0:T(8,128)} %param.13) | copy-start | bytes 221188
  107.1 15.5 %copy-start.7 = (f32[1,72,256]{2,1,0:T(8,128)S(1)}, f32[1,72,256]{2,1,0:T(8,128)}, u32[]{:S(2)}) copy-start(f32[1,72,256]{2,1,0:T(8,128)} %param.12) | copy-start | bytes 221188

commit v5 on v4

--- a/solution.py
+++ b/solution.py
@@ -35,7 +35,34 @@
 
 
 def spread(rows, count):
-    return call(spread_kernel, [((count, *rows.shape), jnp.bfloat16)], [rows])[0]
+    steps = 2
+    return pl.pallas_call(
+        spread_kernel,
+        grid=(steps,),
+        in_specs=[pl.BlockSpec(rows.shape, lambda i: (0, 0))],
+        out_specs=pl.BlockSpec((count // steps, *rows.shape), lambda i: (i, 0, 0)),
+        out_shape=jax.ShapeDtypeStruct((count, *rows.shape), jnp.bfloat16),
+        name="spread",
+    )(rows)
+
+
+def update_kernel(piece_ref, master_ref, first_ref, second_ref, *outs):
+    gradient = piece_ref[0].astype(jnp.float32)
+    for i in range(1, piece_ref.shape[0]):
+        gradient += piece_ref[i].astype(jnp.float32)
+    master = master_ref[...]
+    new_first = beta_first * first_ref[...] + (1.0 - beta_first) * gradient
+    new_second = beta_second * second_ref[...] + (1.0 - beta_second) * gradient * gradient
+    new_master = master - learn_rate * (
+        new_first / (jnp.sqrt(new_second) + epsilon) + decay_rate * master
+    )
+    for out_ref, value in zip(outs, (new_master.astype(jnp.bfloat16), new_master, new_first, new_second)):
+        out_ref[...] = value
+
+
+def update(pieces, master, first, second):
+    outs = [(master.shape, jnp.bfloat16)] + [(master.shape, jnp.float32)] * 3
+    return call(update_kernel, outs, [pieces, master, first, second], off_chip=True)
 
 
 def add_kernel(one_ref, two_ref, out_ref):
@@ -277,10 +304,10 @@
     outs_down, outs_up = [], []
     for t in range(ticks):
         next_down = tick(down[t], acts_down[t], weight, width)[0]
-        if t + 1 < ticks:
+        if t == 1:
+            next_up, pair = tick(up[t], acts_up[t], weight, width, outs_up[0])
+        else:
             next_up = tick(up[t], acts_up[t], weight, width)[0]
-        else:
-            next_up, pair = tick(up[t], acts_up[t], weight, width, outs_up[1])
         outs_down.append(next_down)
         outs_up.append(next_up)
         if t + 1 < ticks:
@@ -288,24 +315,20 @@
             up.append((from_next(next_up), whole))
     hid_up = hidden_parts(acts_up)
     total = early_terms([*hid_down[:2], *hid_up[:2]], down[:2] + up[:2], width)
-    first = to_mirror(outs_up[0])
+    pair = to_mirror(pair)
     kept, given = last_terms(core, total, [hid_down[2], hid_up[2]], [down[2], up[2]], chips, width)
     taken = to_partner(given)
     both = pair_add(kept, taken)
     pieces = lax.all_to_all(both, CHIPS, 0, 0, tiled=True)
-    pair = to_mirror(pair)
-    gradient = jnp.sum(pieces.astype(jnp.float32), axis=0)
-    old_master = master[0]
-    new_first = beta_first * moment_first[0] + (1.0 - beta_first) * gradient
-    new_second = beta_second * moment_second[0] + (1.0 - beta_second) * gradient * gradient
-    new_master = old_master - learn_rate * (
-        new_first / (jnp.sqrt(new_second) + epsilon) + decay_rate * old_master
+    last = to_mirror(outs_up[2])
+    new_weight, new_master, new_first, new_second = update(
+        pieces, master[0], moment_first[0], moment_second[0]
     )
     shape = (ticks, 1, 1, height, width, channels)
     return (
         jnp.stack(outs_down).reshape(shape),
-        jnp.concatenate([first[None], pair]).reshape(shape),
-        new_master.astype(jnp.bfloat16)[None],
+        jnp.concatenate([pair, last[None]]).reshape(shape),
+        new_weight[None],
         new_master[None],
         new_first[None],
         new_second[None],

time: 124 us -> 126 us (1.016)
  Pallas kernels: 8.58 us -> 10.5 us
    pallas_call x0 -> x1, Pallas kernels: none -> 1.8 us  [spread(): pl.pallas_call(spread_kernel, grid=(steps,), in_specs=[pl.BlockSpec(rows....]
    unnamed x16 -> x12, local copies, waits for them, and re-layouts: 1.81 us -> 0.03 us
  transfers between devices with their start and end apart: 11 -> 11, of which waited for: 5 -> 6; matrix products, arithmetic and copies ran while one was open for 2% -> 4% of each run, Pallas kernels for 5% -> 5%
where the time goes in v5:
time: 126 us; the launch traced here: 125 us
  starting transfers between devices  52.4 us (42%)
  blocking collectives  28.2 us (22%)
  waiting for transfers between devices  28.2 us (22%)
  Pallas kernels  10.5 us (8%)
  other arithmetic  3.21 us (3%)
  local copies, waits for them, and re-layouts  1.67 us (1%)
    all_to_all x1, blocking collectives, step(): mine = lax.all_to_all(spread(master[0], chips), CHIPS, 0, 0, tiled=True)  28.2 us
    ppermute x4, waiting for transfers between devices, to_mirror(): lax.ppermute(value, SECTION, [(i, length - 1 - i) for i in range(length)])  22.2 us
    ppermute x4, starting transfers between devices, to_mirror(): lax.ppermute(value, SECTION, [(i, length - 1 - i) for i in range(length)])  21.2 us
    ppermute x4, starting transfers between devices, from_next(): return lax.ppermute(value, SECTION, [(i + 1, i) for i in range(length - 1)])  20.7 us
    pallas_call x14, Pallas kernels, call(): pl.pallas_call(body, in_specs=specs, out_specs=[VMEM] * len(outs), out_sh...  8.7 us
    all_to_all x1, starting transfers between devices, step(): pieces = lax.all_to_all(both, CHIPS, 0, 0, tiled=True)  6.68 us
    ppermute x4, waiting for transfers between devices, from_next(): return lax.ppermute(value, SECTION, [(i + 1, i) for i in range(length - 1)])  4.05 us
    ppermute x2, starting transfers between devices, to_partner(): return lax.ppermute(value, 'core', [(0, 1), (1, 0)])  3.83 us
  transfers between devices with their start and end apart: 11, of which 6 were waited for; matrix products, arithmetic and copies ran while one was open for 4% of the time, Pallas kernels for 5%

profile of v5, /device:TPU:6, one launch (start us, length us, event | category | flops | bytes accessed | tf_op | source)
XLA Modules:
  0.0 125.1 jit_solution(9247779291886810009)
XLA Ops:
  0.7 1.8 %spread.1 = bf16[16,72,256]{2,1,0:T(8,128)(2,1)} custom-call(f32[72,256]{1,0:T(8,128)} %bitcast.36), custom_call_target="tpu_custom_call" | custom-call | tf_op jit(solution)/shard_map/spread/pallas_call | solution.py:39
  2.5 28.2 %all_to_all.10.mine_ref = bf16[16,72,256]{2,1,0:T(8,128)(2,1)S(1)} all-to-all(bf16[16,72,256]{2,1,0:T(8,128)(2,1)} %spread.1), channel_id=1, replica_groups=mesh['x_lo'=2,'z'=8,'x_hi'=2,'y'=8,'core'=2] {'x_hi','y'}, dimensions={0} | all-to-all | bytes 1179648 | tf_op jit(solution)/shard_map/all_to_all | solution.py:294
  30.7 1.9 %collective-permute-start = (bf16[16,72,256]{2,1,0:T(8,128)(2,1)S(1)}, bf16[16,72,256]{2,1,0:T(8,128)(2,1)S(1)}, u32[]{:S(2)}, u32[]{:S(2)}) collective-permute-start(bf16[16,72,256]{2,1,0:T(8,128)(2,1)S(1)} %all_to_all.10.mine_ref), channel_id=1, source_target_pairs={{0,1},{1,0},{2,3},{3,2},{4,5},{5,4},{6,7},{7,6},{8,9},{9,8},{10,11... | collective-permute-start | bytes 1769480 | tf_op jit(solution)/shard_map/ppermute | solution.py:283
  32.6 0.9 slice.12
  33.5 1.6 %pad_maximum_fusion.2 = bf16[2,256,256]{2,1,0:T(8,128)(2,1)} fusion(bf16[1,256,256]{2,1,0:T(8,128)(2,1)S(1)} %bitcast.41, bf16[1,256,256]{2,1,0:T(8,128)(2,1)} %bitcast.43), kind=kLoop, calls=%fused_computation.2 | loop fusion | flops 131072 | bytes 524288 | tf_op jit(solution)/shard_map/stack | solution.py:295
  35.2 11.2 %collective-permute-start.3 = (bf16[2,256,256]{2,1,0:T(8,128)(2,1)}, bf16[2,256,256]{2,1,0:T(8,128)(2,1)S(1)}, u32[]{:S(2)}, u32[]{:S(2)}) collective-permute-start(bf16[2,256,256]{2,1,0:T(8,128)(2,1)} %pad_maximum_fusion.2), channel_id=1, source_target_pairs={{0,480},{32,448},{64,416},{96,384},{128,352},{160,320},{192,288},{... | collective-permute-start | bytes 786440 | tf_op jit(solution)/shard_map/ppermute | solution.py:274
  46.4 0.7 slice.14
  47.1 1.9 %collective-permute-start.5 = (bf16[2,256,256]{2,1,0:T(8,128)(2,1)}, bf16[2,256,256]{2,1,0:T(8,128)(2,1)S(1)}, u32[]{:S(2)}, u32[]{:S(2)}) collective-permute-start(bf16[2,256,256]{2,1,0:T(8,128)(2,1)} %bitcast.10), channel_id=1, source_target_pairs={{0,480},{32,448},{64,416},{96,384},{128,352},{160,320},{192,288},{... | collective-permute-start | bytes 786440 | tf_op jit(solution)/shard_map/ppermute | solution.py:274
  49.8 6.0 %collective-permute-start.1 = (bf16[256,256]{1,0:T(8,128)(2,1)S(1)}, bf16[256,256]{1,0:T(8,128)(2,1)S(1)}, u32[]{:S(2)}, u32[]{:S(2)}) collective-permute-start(bf16[256,256]{1,0:T(8,128)(2,1)S(1)} %shard_map.120), channel_id=1, source_target_pairs={{32,0},{64,32},{96,64},{128,96},{160,128},{192,160},{224,192},{256... | collective-permute-start | bytes 393224 | tf_op jit(solution)/shard_map/ppermute | solution.py:279
  55.8 8.9 %collective-permute-done.3.refs_0_.refs_1_.refs_6_ = bf16[2,256,256]{2,1,0:T(8,128)(2,1)S(1)} collective-permute-done((bf16[2,256,256]{2,1,0:T(8,128)(2,1)}, bf16[2,256,256]{2,1,0:T(8,128)(2,1)S(1)}, u32[]{:S(2)}, u32[]{:S(2)}) %collective-permute-start.3) | collective-permute-done | bytes 262176 | tf_op jit(solution)/shard_map/ppermute | solution.py:274
  64.8 0.6 shard_map.123.refs_3_
  65.4 6.2 %collective-permute-start.4 = (bf16[256,256]{1,0:T(8,128)(2,1)S(1)}, bf16[256,256]{1,0:T(8,128)(2,1)S(1)}, u32[]{:S(2)}, u32[]{:S(2)}) collective-permute-start(bf16[256,256]{1,0:T(8,128)(2,1)S(1)} %shard_map.123.refs_3_), channel_id=1, source_target_pairs={{32,0},{64,32},{96,64},{128,96},{160,128},{192,160},{224,192},{256... | collective-permute-start | bytes 393224 | tf_op jit(solution)/shard_map/ppermute | solution.py:279
  71.6 1.3 %collective-permute-done.1.refs_0_.refs_5_ = bf16[256,256]{1,0:T(8,128)(2,1)S(1)} collective-permute-done((bf16[256,256]{1,0:T(8,128)(2,1)S(1)}, bf16[256,256]{1,0:T(8,128)(2,1)S(1)}, u32[]{:S(2)}, u32[]{:S(2)}) %collective-permute-start.1) | collective-permute-done | bytes 131104 | tf_op jit(solution)/shard_map/ppermute | solution.py:279
  72.9 0.6 shard_map.121
  73.5 6.5 %collective-permute-start.2 = (bf16[256,256]{1,0:T(8,128)(2,1)S(1)}, bf16[256,256]{1,0:T(8,128)(2,1)S(1)}, u32[]{:S(2)}, u32[]{:S(2)}) collective-permute-start(bf16[256,256]{1,0:T(8,128)(2,1)S(1)} %shard_map.121), channel_id=1, source_target_pairs={{32,0},{64,32},{96,64},{128,96},{160,128},{192,160},{224,192},{256... | collective-permute-start | bytes 393224 | tf_op jit(solution)/shard_map/ppermute | solution.py:279
  80.1 0.6 shard_map.124
  80.7 1.9 %collective-permute-start.7 = (bf16[256,256]{1,0:T(8,128)(2,1)S(1)}, bf16[256,256]{1,0:T(8,128)(2,1)S(1)}, u32[]{:S(2)}, u32[]{:S(2)}) collective-permute-start(bf16[256,256]{1,0:T(8,128)(2,1)S(1)} %get-tuple-element.21), channel_id=1, source_target_pairs={{32,0},{64,32},{96,64},{128,96},{160,128},{192,160},{224,192},{256... | collective-permute-start | bytes 393224 | tf_op jit(solution)/shard_map/ppermute | solution.py:279
  83.3 1.4 %shard_map.128.total_ref = f32[2304,256]{1,0:T(8,128)S(1)} custom-call(bf16[256,256]{1,0:T(8,128)(2,1)S(1)} %get-tuple-element.22.refs_0_, bf16[256,256]{1,0:T(8,128)(2,1)S(1)} %get-tuple-element.23.refs_1_, bf16[256,256]{1,0:T(8,128)(2,1)S(1)} %get-tuple-element.24.refs_2_, bf16[256,256]{1,0:T(8,128)(2,1)S(1)} %get-tuple-element.25.refs_3_, ...), custom_call_target="tpu_custom_call" | custom-call | tf_op jit(solution)/shard_map/pallas_call | solution.py:21
  84.8 2.7 %collective-permute-done.7.refs_0_.refs_3_ = bf16[256,256]{1,0:T(8,128)(2,1)S(1)} collective-permute-done((bf16[256,256]{1,0:T(8,128)(2,1)S(1)}, bf16[256,256]{1,0:T(8,128)(2,1)S(1)}, u32[]{:S(2)}, u32[]{:S(2)}) %collective-permute-start.7) | collective-permute-done | bytes 131104 | tf_op jit(solution)/shard_map/ppermute | solution.py:279
  87.5 1.0 shard_map.129
  88.5 1.9 %collective-permute-start.9 = (bf16[16,72,256]{2,1,0:T(8,128)(2,1)S(1)}, bf16[16,72,256]{2,1,0:T(8,128)(2,1)S(1)}, u32[]{:S(2)}, u32[]{:S(2)}) collective-permute-start(bf16[16,72,256]{2,1,0:T(8,128)(2,1)S(1)} %get-tuple-element.29), channel_id=1, source_target_pairs={{0,1},{1,0},{2,3},{3,2},{4,5},{5,4},{6,7},{7,6},{8,9},{9,8},{10,11... | collective-permute-start | bytes 1769480 | tf_op jit(solution)/shard_map/ppermute | solution.py:283
  90.5 2.0 %collective-permute-done.9.two_ref = bf16[16,72,256]{2,1,0:T(8,128)(2,1)S(1)} collective-permute-done((bf16[16,72,256]{2,1,0:T(8,128)(2,1)S(1)}, bf16[16,72,256]{2,1,0:T(8,128)(2,1)S(1)}, u32[]{:S(2)}, u32[]{:S(2)}) %collective-permute-start.9) | collective-permute-done | bytes 589856 | tf_op jit(solution)/shard_map/ppermute | solution.py:283
  92.4 1.0 shard_map.130
  93.4 6.7 %all-to-all-start.1 = ((bf16[16,72,256]{2,1,0:T(8,128)(2,1)}), bf16[16,72,256]{2,1,0:T(8,128)(2,1)S(1)}, u32[]{:S(2)}, u32[]{:S(2)}) async-start(bf16[16,72,256]{2,1,0:T(8,128)(2,1)} %shard_map.130), calls=%async_computation.1 | async-start | bytes 1179648 | tf_op jit(solution)/shard_map/all_to_all | solution.py:322
  100.1 3.8 %collective-permute-start.6 = (bf16[2,256,256]{2,1,0:T(8,128)(2,1)S(1)}, bf16[2,256,256]{2,1,0:T(8,128)(2,1)S(1)}, u32[]{:S(2)}, u32[]{:S(2)}) collective-permute-start(bf16[2,256,256]{2,1,0:T(8,128)(2,1)S(1)} %get-tuple-element.20), channel_id=1, source_target_pairs={{0,480},{32,448},{64,416},{96,384},{128,352},{160,320},{192,288},{... | collective-permute-start | bytes 786440 | tf_op jit(solution)/shard_map/ppermute | solution.py:274
  103.9 0.6 shard_map.125
  104.5 4.3 %collective-permute-start.8 = (bf16[256,256]{1,0:T(8,128)(2,1)S(1)}, bf16[256,256]{1,0:T(8,128)(2,1)S(1)}, u32[]{:S(2)}, u32[]{:S(2)}) collective-permute-start(bf16[256,256]{1,0:T(8,128)(2,1)S(1)} %shard_map.125), channel_id=1, source_target_pairs={{0,480},{32,448},{64,416},{96,384},{128,352},{160,320},{192,288},{... | collective-permute-start | bytes 393224 | tf_op jit(solution)/shard_map/ppermute | solution.py:274
  109.4 0.8 pad_maximum_fusion
  110.2 10.5 %collective-permute-done.6 = bf16[2,256,256]{2,1,0:T(8,128)(2,1)S(1)} collective-permute-done((bf16[2,256,256]{2,1,0:T(8,128)(2,1)S(1)}, bf16[2,256,256]{2,1,0:T(8,128)(2,1)S(1)}, u32[]{:S(2)}, u32[]{:S(2)}) %collective-permute-start.6) | collective-permute-done | bytes 262176 | tf_op jit(solution)/shard_map/ppermute | solution.py:274
  120.7 2.7 %collective-permute-done.8 = bf16[256,256]{1,0:T(8,128)(2,1)S(1)} collective-permute-done((bf16[256,256]{1,0:T(8,128)(2,1)S(1)}, bf16[256,256]{1,0:T(8,128)(2,1)S(1)}, u32[]{:S(2)}, u32[]{:S(2)}) %collective-permute-start.8) | collective-permute-done | bytes 131104 | tf_op jit(solution)/shard_map/ppermute | solution.py:274
  123.4 0.8 pad_maximum_fusion.1
  124.2 0.8 shard_map.131
  (23 shorter events, 2.1 us)
Async XLA Ops:
  0.6 45.7 %copy-start.5 = (bf16[3,1,1,16,16,256]{5,4,3,2,1,0:T(8,128)(2,1)S(1)}, bf16[3,1,1,16,16,256]{5,4,3,2,1,0:T(8,128)(2,1)}, u32[]{:S(2)}) copy-start(bf16[3,1,1,16,16,256]{5,4,3,2,1,0:T(8,128)(2,1)} %param.8) | copy-start | bytes 1179652
  0.6 48.4 %copy-start.2 = (bf16[1,1,16,16,256]{4,3,2,1,0:T(8,128)(2,1)S(1)}, bf16[1,1,16,16,256]{4,3,2,1,0:T(8,128)(2,1)}, u32[]{:S(2)}) copy-start(bf16[1,1,16,16,256]{4,3,2,1,0:T(8,128)(2,1)} %param.9) | copy-start | bytes 393220
  2.5 46.7 %copy-start = (bf16[3,1,1,16,16,256]{5,4,3,2,1,0:T(8,128)(2,1)S(1)}, bf16[3,1,1,16,16,256]{5,4,3,2,1,0:T(8,128)(2,1)}, u32[]{:S(2)}) copy-start(bf16[3,1,1,16,16,256]{5,4,3,2,1,0:T(8,128)(2,1)} %param.7) | copy-start | bytes 1179652
  30.7 18.4 %collective-permute-start = (bf16[16,72,256]{2,1,0:T(8,128)(2,1)S(1)}, bf16[16,72,256]{2,1,0:T(8,128)(2,1)S(1)}, u32[]{:S(2)}, u32[]{:S(2)}) collective-permute-start(bf16[16,72,256]{2,1,0:T(8,128)(2,1)S(1)} %all_to_all.10.mine_ref), channel_id=1, source_target_pairs={{0,1},{1,0},{2,3},{3,2},{4,5},{5,4},{6,7},{7,6},{8,9},{9,8},{10,11... | collective-permute-start | bytes 1769480 | tf_op jit(solution)/shard_map/ppermute | solution.py:283
  35.2 29.6 %collective-permute-start.3 = (bf16[2,256,256]{2,1,0:T(8,128)(2,1)}, bf16[2,256,256]{2,1,0:T(8,128)(2,1)S(1)}, u32[]{:S(2)}, u32[]{:S(2)}) collective-permute-start(bf16[2,256,256]{2,1,0:T(8,128)(2,1)} %pad_maximum_fusion.2), channel_id=1, source_target_pairs={{0,480},{32,448},{64,416},{96,384},{128,352},{160,320},{192,288},{... | collective-permute-start | bytes 786440 | tf_op jit(solution)/shard_map/ppermute | solution.py:274
  47.1 32.9 %collective-permute-start.5 = (bf16[2,256,256]{2,1,0:T(8,128)(2,1)}, bf16[2,256,256]{2,1,0:T(8,128)(2,1)S(1)}, u32[]{:S(2)}, u32[]{:S(2)}) collective-permute-start(bf16[2,256,256]{2,1,0:T(8,128)(2,1)} %bitcast.10), channel_id=1, source_target_pairs={{0,480},{32,448},{64,416},{96,384},{128,352},{160,320},{192,288},{... | collective-permute-start | bytes 786440 | tf_op jit(solution)/shard_map/ppermute | solution.py:274
  49.8 23.1 %collective-permute-start.1 = (bf16[256,256]{1,0:T(8,128)(2,1)S(1)}, bf16[256,256]{1,0:T(8,128)(2,1)S(1)}, u32[]{:S(2)}, u32[]{:S(2)}) collective-permute-start(bf16[256,256]{1,0:T(8,128)(2,1)S(1)} %shard_map.120), channel_id=1, source_target_pairs={{32,0},{64,32},{96,64},{128,96},{160,128},{192,160},{224,192},{256... | collective-permute-start | bytes 393224 | tf_op jit(solution)/shard_map/ppermute | solution.py:279
  65.4 14.7 %collective-permute-start.4 = (bf16[256,256]{1,0:T(8,128)(2,1)S(1)}, bf16[256,256]{1,0:T(8,128)(2,1)S(1)}, u32[]{:S(2)}, u32[]{:S(2)}) collective-permute-start(bf16[256,256]{1,0:T(8,128)(2,1)S(1)} %shard_map.123.refs_3_), channel_id=1, source_target_pairs={{32,0},{64,32},{96,64},{128,96},{160,128},{192,160},{224,192},{256... | collective-permute-start | bytes 393224 | tf_op jit(solution)/shard_map/ppermute | solution.py:279
  73.5 11.3 %collective-permute-start.2 = (bf16[256,256]{1,0:T(8,128)(2,1)S(1)}, bf16[256,256]{1,0:T(8,128)(2,1)S(1)}, u32[]{:S(2)}, u32[]{:S(2)}) collective-permute-start(bf16[256,256]{1,0:T(8,128)(2,1)S(1)} %shard_map.121), channel_id=1, source_target_pairs={{32,0},{64,32},{96,64},{128,96},{160,128},{192,160},{224,192},{256... | collective-permute-start | bytes 393224 | tf_op jit(solution)/shard_map/ppermute | solution.py:279
  80.7 6.9 %collective-permute-start.7 = (bf16[256,256]{1,0:T(8,128)(2,1)S(1)}, bf16[256,256]{1,0:T(8,128)(2,1)S(1)}, u32[]{:S(2)}, u32[]{:S(2)}) collective-permute-start(bf16[256,256]{1,0:T(8,128)(2,1)S(1)} %get-tuple-element.21), channel_id=1, source_target_pairs={{32,0},{64,32},{96,64},{128,96},{160,128},{192,160},{224,192},{256... | collective-permute-start | bytes 393224 | tf_op jit(solution)/shard_map/ppermute | solution.py:279
  88.5 3.9 %collective-permute-start.9 = (bf16[16,72,256]{2,1,0:T(8,128)(2,1)S(1)}, bf16[16,72,256]{2,1,0:T(8,128)(2,1)S(1)}, u32[]{:S(2)}, u32[]{:S(2)}) collective-permute-start(bf16[16,72,256]{2,1,0:T(8,128)(2,1)S(1)} %get-tuple-element.29), channel_id=1, source_target_pairs={{0,1},{1,0},{2,3},{3,2},{4,5},{5,4},{6,7},{7,6},{8,9},{9,8},{10,11... | collective-permute-start | bytes 1769480 | tf_op jit(solution)/shard_map/ppermute | solution.py:283
  93.4 30.9 %all-to-all-start.1 = ((bf16[16,72,256]{2,1,0:T(8,128)(2,1)}), bf16[16,72,256]{2,1,0:T(8,128)(2,1)S(1)}, u32[]{:S(2)}, u32[]{:S(2)}) async-start(bf16[16,72,256]{2,1,0:T(8,128)(2,1)} %shard_map.130), calls=%async_computation.1 | async-start | bytes 1179648 | tf_op jit(solution)/shard_map/all_to_all | solution.py:322
  100.1 24.2 %copy-start.1 = (f32[1,72,256]{2,1,0:T(8,128)S(1)}, f32[1,72,256]{2,1,0:T(8,128)}, u32[]{:S(2)}) copy-start(f32[1,72,256]{2,1,0:T(8,128)} %param.11) | copy-start | bytes 221188
  100.1 24.2 %copy-start.3 = (f32[1,72,256]{2,1,0:T(8,128)S(1)}, f32[1,72,256]{2,1,0:T(8,128)}, u32[]{:S(2)}) copy-start(f32[1,72,256]{2,1,0:T(8,128)} %param.12) | copy-start | bytes 221188
  100.1 24.2 %copy-start.4 = (f32[1,72,256]{2,1,0:T(8,128)S(1)}, f32[1,72,256]{2,1,0:T(8,128)}, u32[]{:S(2)}) copy-start(f32[1,72,256]{2,1,0:T(8,128)} %param.13) | copy-start | bytes 221188
  100.1 20.6 %collective-permute-start.6 = (bf16[2,256,256]{2,1,0:T(8,128)(2,1)S(1)}, bf16[2,256,256]{2,1,0:T(8,128)(2,1)S(1)}, u32[]{:S(2)}, u32[]{:S(2)}) collective-permute-start(bf16[2,256,256]{2,1,0:T(8,128)(2,1)S(1)} %get-tuple-element.20), channel_id=1, source_target_pairs={{0,480},{32,448},{64,416},{96,384},{128,352},{160,320},{192,288},{... | collective-permute-start | bytes 786440 | tf_op jit(solution)/shard_map/ppermute | solution.py:274
  104.5 18.9 %collective-permute-start.8 = (bf16[256,256]{1,0:T(8,128)(2,1)S(1)}, bf16[256,256]{1,0:T(8,128)(2,1)S(1)}, u32[]{:S(2)}, u32[]{:S(2)}) collective-permute-start(bf16[256,256]{1,0:T(8,128)(2,1)S(1)} %shard_map.125), channel_id=1, source_target_pairs={{0,480},{32,448},{64,416},{96,384},{128,352},{160,320},{192,288},{... | collective-permute-start | bytes 393224 | tf_op jit(solution)/shard_map/ppermute | solution.py:274

commit v6 on v5

--- a/solution.py
+++ b/solution.py
@@ -28,20 +28,33 @@
     )(*args)
 
 
-def spread_kernel(rows_ref, out_ref):
-    rows = rows_ref[...].astype(jnp.bfloat16)
-    for i in range(out_ref.shape[0]):
-        out_ref[i] = rows
+def spread_kernel(rows_ref, out_ref, wide_ref, cast_ref, fetch_sem, store_sem):
+    fetch = pltpu.make_async_copy(rows_ref, wide_ref, fetch_sem)
+    fetch.start()
+    fetch.wait()
+    cast_ref[...] = wide_ref[...].astype(jnp.bfloat16)
+    stores = [
+        pltpu.make_async_copy(cast_ref, out_ref.at[i], store_sem.at[i])
+        for i in range(out_ref.shape[0])
+    ]
+    for store in stores:
+        store.start()
+    for store in stores:
+        store.wait()
 
 
 def spread(rows, count):
-    steps = 2
     return pl.pallas_call(
         spread_kernel,
-        grid=(steps,),
-        in_specs=[pl.BlockSpec(rows.shape, lambda i: (0, 0))],
-        out_specs=pl.BlockSpec((count // steps, *rows.shape), lambda i: (i, 0, 0)),
+        in_specs=[pl.BlockSpec(memory_space=pl.ANY)],
+        out_specs=pl.BlockSpec(memory_space=pl.ANY),
         out_shape=jax.ShapeDtypeStruct((count, *rows.shape), jnp.bfloat16),
+        scratch_shapes=[
+            pltpu.VMEM(rows.shape, jnp.float32),
+            pltpu.VMEM(rows.shape, jnp.bfloat16),
+            pltpu.SemaphoreType.DMA,
+            pltpu.SemaphoreType.DMA((count,)),
+        ],
         name="spread",
     )(rows)
 
@@ -292,15 +305,15 @@
     acts_down = acts_down.reshape(ticks, *flat)
     acts_up = acts_up.reshape(ticks, *flat)
     mine = lax.all_to_all(spread(master[0], chips), CHIPS, 0, 0, tiled=True)
-    far_first = to_mirror(jnp.stack([front_up.reshape(flat), acts_up[0]]))
-    far_rest = to_mirror(acts_up[1:])
+    front_up = to_mirror(front_up.reshape(flat))
+    acts_up = to_mirror(acts_up)
     front_down = keep(front_down.reshape(flat))
     acts_down = [(acts_down, t) for t in range(ticks)]
-    acts_up = [(far_first, 1)] + [(far_rest, t) for t in range(ticks - 1)]
+    acts_up = [(acts_up, t) for t in range(ticks)]
     hid_down = hidden_parts(acts_down)
     other = to_partner(mine)
     weight = weave(core, mine, other)
-    down, up = [(front_down, whole)], [(far_first, 0)]
+    down, up = [(front_down, whole)], [(front_up, whole)]
     outs_down, outs_up = [], []
     for t in range(ticks):
         next_down = tick(down[t], acts_down[t], weight, width)[0]

time: 126 us -> 126 us (level)
  waiting for transfers between devices: 28.2 us -> 30.4 us
  other arithmetic: 3.21 us -> 1.57 us
    ppermute x4, waiting for transfers between devices: 22.2 us -> 27.8 us  [to_mirror(): lax.ppermute(value, SECTION, [(i, length - 1 - i) for i in range(length)])]
    ppermute x4, waiting for transfers between devices: 4.05 us -> 0.63 us  [from_next(): return lax.ppermute(value, SECTION, [(i + 1, i) for i in range(length - 1)])]
    slice x2 -> x0, local copies, waits for them, and re-layouts: 1.64 us -> none  [the longest x1 0.92 us: step(): far_first = to_mirror(jnp.stack([front_up.reshape(flat), acts_up[0]]))]
    another operation x1 -> x0, other arithmetic: 1.63 us -> none  [step(): far_first = to_mirror(jnp.stack([front_up.reshape(flat), acts_up[0]]))]
    unnamed x12, local copies, waits for them, and re-layouts: 0.03 us -> 1.62 us
  transfers between devices with their start and end apart: 11 -> 11, of which waited for: 6 -> 6; matrix products, arithmetic and copies ran while one was open for 4% -> 1% of each run, Pallas kernels for 5% -> 5%
where the time goes in v6:
time: 126 us
  starting transfers between devices  52.4 us (42%)
  waiting for transfers between devices  30.4 us (24%)
  blocking collectives  28.1 us (22%)
  Pallas kernels  10.6 us (8%)
  local copies, waits for them, and re-layouts  1.62 us (1%)
  other arithmetic  1.57 us (1%)
    all_to_all x1, blocking collectives, step(): mine = lax.all_to_all(spread(master[0], chips), CHIPS, 0, 0, tiled=True)  28.1 us
    ppermute x4, waiting for transfers between devices, to_mirror(): lax.ppermute(value, SECTION, [(i, length - 1 - i) for i in range(length)])  27.8 us
    ppermute x4, starting transfers between devices, to_mirror(): lax.ppermute(value, SECTION, [(i, length - 1 - i) for i in range(length)])  21.2 us
    ppermute x4, starting transfers between devices, from_next(): return lax.ppermute(value, SECTION, [(i + 1, i) for i in range(length - 1)])  20.7 us
    pallas_call x14, Pallas kernels, call(): pl.pallas_call(body, in_specs=specs, out_specs=[VMEM] * len(outs), out_sh...  8.7 us
    all_to_all x1, starting transfers between devices, step(): pieces = lax.all_to_all(both, CHIPS, 0, 0, tiled=True)  6.68 us
    ppermute x2, starting transfers between devices, to_partner(): return lax.ppermute(value, 'core', [(0, 1), (1, 0)])  3.83 us
  transfers between devices with their start and end apart: 11, of which 6 were waited for; matrix products, arithmetic and copies ran while one was open for 1% of the time, Pallas kernels for 5%

profile of v6, /device:TPU:6, one launch (start us, length us, event | category | flops | bytes accessed | tf_op | source)
XLA Modules:
  0.0 125.6 jit_solution(13485008528224867907)
XLA Ops:
  0.6 1.9 %spread.1 = bf16[16,72,256]{2,1,0:T(8,128)(2,1)} custom-call(f32[72,256]{1,0:T(8,128)} %bitcast.35), custom_call_target="tpu_custom_call" | custom-call | tf_op jit(solution)/shard_map/spread/pallas_call | solution.py:47
  2.6 28.1 %all_to_all.10.mine_ref = bf16[16,72,256]{2,1,0:T(8,128)(2,1)S(1)} all-to-all(bf16[16,72,256]{2,1,0:T(8,128)(2,1)} %spread.1), channel_id=1, replica_groups=mesh['x_lo'=2,'z'=8,'x_hi'=2,'y'=8,'core'=2] {'x_hi','y'}, dimensions={0} | all-to-all | bytes 1179648 | tf_op jit(solution)/shard_map/all_to_all | solution.py:307
  30.7 1.9 %collective-permute-start = (bf16[16,72,256]{2,1,0:T(8,128)(2,1)S(1)}, bf16[16,72,256]{2,1,0:T(8,128)(2,1)S(1)}, u32[]{:S(2)}, u32[]{:S(2)}) collective-permute-start(bf16[16,72,256]{2,1,0:T(8,128)(2,1)S(1)} %all_to_all.10.mine_ref), channel_id=1, source_target_pairs={{0,1},{1,0},{2,3},{3,2},{4,5},{5,4},{6,7},{7,6},{8,9},{9,8},{10,11... | collective-permute-start | bytes 1769480 | tf_op jit(solution)/shard_map/ppermute | solution.py:296
  32.6 11.2 %collective-permute-start.4 = (bf16[3,256,256]{2,1,0:T(8,128)(2,1)}, bf16[3,256,256]{2,1,0:T(8,128)(2,1)S(1)}, u32[]{:S(2)}, u32[]{:S(2)}) collective-permute-start(bf16[3,256,256]{2,1,0:T(8,128)(2,1)} %bitcast.42), channel_id=1, source_target_pairs={{0,480},{32,448},{64,416},{96,384},{128,352},{160,320},{192,288},{... | collective-permute-start | bytes 1179656 | tf_op jit(solution)/shard_map/ppermute | solution.py:287
  43.8 1.9 %collective-permute-start.3 = (bf16[256,256]{1,0:T(8,128)(2,1)}, bf16[256,256]{1,0:T(8,128)(2,1)S(1)}, u32[]{:S(2)}, u32[]{:S(2)}) collective-permute-start(bf16[256,256]{1,0:T(8,128)(2,1)} %bitcast.43), channel_id=1, source_target_pairs={{0,480},{32,448},{64,416},{96,384},{128,352},{160,320},{192,288},{... | collective-permute-start | bytes 393224 | tf_op jit(solution)/shard_map/ppermute | solution.py:287
  45.8 0.9 copy-done.2
  46.8 0.6 shard_map.120
  47.4 6.0 %collective-permute-start.1 = (bf16[256,256]{1,0:T(8,128)(2,1)S(1)}, bf16[256,256]{1,0:T(8,128)(2,1)S(1)}, u32[]{:S(2)}, u32[]{:S(2)}) collective-permute-start(bf16[256,256]{1,0:T(8,128)(2,1)S(1)} %shard_map.120), channel_id=1, source_target_pairs={{32,0},{64,32},{96,64},{128,96},{160,128},{192,160},{224,192},{256... | collective-permute-start | bytes 393224 | tf_op jit(solution)/shard_map/ppermute | solution.py:292
  53.4 14.4 %collective-permute-done.3.refs_0_.refs_6_ = bf16[256,256]{1,0:T(8,128)(2,1)S(1)} collective-permute-done((bf16[256,256]{1,0:T(8,128)(2,1)}, bf16[256,256]{1,0:T(8,128)(2,1)S(1)}, u32[]{:S(2)}, u32[]{:S(2)}) %collective-permute-start.3) | collective-permute-done | bytes 131104 | tf_op jit(solution)/shard_map/ppermute | solution.py:287
  67.8 0.6 shard_map.123.refs_3_
  68.4 6.2 %collective-permute-start.5 = (bf16[256,256]{1,0:T(8,128)(2,1)S(1)}, bf16[256,256]{1,0:T(8,128)(2,1)S(1)}, u32[]{:S(2)}, u32[]{:S(2)}) collective-permute-start(bf16[256,256]{1,0:T(8,128)(2,1)S(1)} %shard_map.123.refs_3_), channel_id=1, source_target_pairs={{32,0},{64,32},{96,64},{128,96},{160,128},{192,160},{224,192},{256... | collective-permute-start | bytes 393224 | tf_op jit(solution)/shard_map/ppermute | solution.py:292
  74.7 0.6 shard_map.121
  75.3 1.9 %collective-permute-start.2 = (bf16[256,256]{1,0:T(8,128)(2,1)S(1)}, bf16[256,256]{1,0:T(8,128)(2,1)S(1)}, u32[]{:S(2)}, u32[]{:S(2)}) collective-permute-start(bf16[256,256]{1,0:T(8,128)(2,1)S(1)} %shard_map.121), channel_id=1, source_target_pairs={{32,0},{64,32},{96,64},{128,96},{160,128},{192,160},{224,192},{256... | collective-permute-start | bytes 393224 | tf_op jit(solution)/shard_map/ppermute | solution.py:292
  77.6 0.6 shard_map.124
  78.2 0.7 copy-done.5
  78.9 6.5 %collective-permute-start.7 = (bf16[256,256]{1,0:T(8,128)(2,1)S(1)}, bf16[256,256]{1,0:T(8,128)(2,1)S(1)}, u32[]{:S(2)}, u32[]{:S(2)}) collective-permute-start(bf16[256,256]{1,0:T(8,128)(2,1)S(1)} %get-tuple-element.21), channel_id=1, source_target_pairs={{32,0},{64,32},{96,64},{128,96},{160,128},{192,160},{224,192},{256... | collective-permute-start | bytes 393224 | tf_op jit(solution)/shard_map/ppermute | solution.py:292
  85.4 0.4 shard_map.126
  86.1 1.4 %shard_map.128.total_ref = f32[2304,256]{1,0:T(8,128)S(1)} custom-call(bf16[256,256]{1,0:T(8,128)(2,1)S(1)} %get-tuple-element.22.refs_0_, bf16[256,256]{1,0:T(8,128)(2,1)S(1)} %get-tuple-element.23.refs_1_, bf16[256,256]{1,0:T(8,128)(2,1)S(1)} %get-tuple-element.24.refs_2_, bf16[256,256]{1,0:T(8,128)(2,1)S(1)} %get-tuple-element.25.refs_3_, ...), custom_call_target="tpu_custom_call" | custom-call | tf_op jit(solution)/shard_map/pallas_call | solution.py:21
  87.9 1.0 shard_map.129
  88.9 1.9 %collective-permute-start.9 = (bf16[16,72,256]{2,1,0:T(8,128)(2,1)S(1)}, bf16[16,72,256]{2,1,0:T(8,128)(2,1)S(1)}, u32[]{:S(2)}, u32[]{:S(2)}) collective-permute-start(bf16[16,72,256]{2,1,0:T(8,128)(2,1)S(1)} %get-tuple-element.29), channel_id=1, source_target_pairs={{0,1},{1,0},{2,3},{3,2},{4,5},{5,4},{6,7},{7,6},{8,9},{9,8},{10,11... | collective-permute-start | bytes 1769480 | tf_op jit(solution)/shard_map/ppermute | solution.py:296
  90.8 2.0 %collective-permute-done.9.two_ref = bf16[16,72,256]{2,1,0:T(8,128)(2,1)S(1)} collective-permute-done((bf16[16,72,256]{2,1,0:T(8,128)(2,1)S(1)}, bf16[16,72,256]{2,1,0:T(8,128)(2,1)S(1)}, u32[]{:S(2)}, u32[]{:S(2)}) %collective-permute-start.9) | collective-permute-done | bytes 589856 | tf_op jit(solution)/shard_map/ppermute | solution.py:296
  92.8 1.0 shard_map.130
  93.7 6.7 %all-to-all-start.1 = ((bf16[16,72,256]{2,1,0:T(8,128)(2,1)}), bf16[16,72,256]{2,1,0:T(8,128)(2,1)S(1)}, u32[]{:S(2)}, u32[]{:S(2)}) async-start(bf16[16,72,256]{2,1,0:T(8,128)(2,1)} %shard_map.130), calls=%async_computation.1 | async-start | bytes 1179648 | tf_op jit(solution)/shard_map/all_to_all | solution.py:335
  100.4 6.0 %collective-permute-start.6 = (bf16[2,256,256]{2,1,0:T(8,128)(2,1)}, bf16[2,256,256]{2,1,0:T(8,128)(2,1)S(1)}, u32[]{:S(2)}, u32[]{:S(2)}) collective-permute-start(bf16[2,256,256]{2,1,0:T(8,128)(2,1)} %copy-done.5), channel_id=1, source_target_pairs={{0,480},{32,448},{64,416},{96,384},{128,352},{160,320},{192,288},{... | collective-permute-start | bytes 786440 | tf_op jit(solution)/shard_map/ppermute | solution.py:287
  106.4 0.6 shard_map.125
  107.0 2.1 %collective-permute-start.8 = (bf16[256,256]{1,0:T(8,128)(2,1)S(1)}, bf16[256,256]{1,0:T(8,128)(2,1)S(1)}, u32[]{:S(2)}, u32[]{:S(2)}) collective-permute-start(bf16[256,256]{1,0:T(8,128)(2,1)S(1)} %shard_map.125), channel_id=1, source_target_pairs={{0,480},{32,448},{64,416},{96,384},{128,352},{160,320},{192,288},{... | collective-permute-start | bytes 393224 | tf_op jit(solution)/shard_map/ppermute | solution.py:287
  109.1 0.6 shard_map.122
  109.8 0.8 pad_maximum_fusion
  110.5 10.7 %collective-permute-done.6 = bf16[2,256,256]{2,1,0:T(8,128)(2,1)S(1)} collective-permute-done((bf16[2,256,256]{2,1,0:T(8,128)(2,1)}, bf16[2,256,256]{2,1,0:T(8,128)(2,1)S(1)}, u32[]{:S(2)}, u32[]{:S(2)}) %collective-permute-start.6) | collective-permute-done | bytes 262176 | tf_op jit(solution)/shard_map/ppermute | solution.py:287
  121.2 2.7 %collective-permute-done.8 = bf16[256,256]{1,0:T(8,128)(2,1)S(1)} collective-permute-done((bf16[256,256]{1,0:T(8,128)(2,1)S(1)}, bf16[256,256]{1,0:T(8,128)(2,1)S(1)}, u32[]{:S(2)}, u32[]{:S(2)}) %collective-permute-start.8) | collective-permute-done | bytes 131104 | tf_op jit(solution)/shard_map/ppermute | solution.py:287
  124.0 0.8 pad_maximum_fusion.1
  124.8 0.8 shard_map.131
  (20 shorter events, 1.1 us)
Async XLA Ops:
  0.6 46.1 %copy-start = (bf16[3,1,1,16,16,256]{5,4,3,2,1,0:T(8,128)(2,1)S(1)}, bf16[3,1,1,16,16,256]{5,4,3,2,1,0:T(8,128)(2,1)}, u32[]{:S(2)}) copy-start(bf16[3,1,1,16,16,256]{5,4,3,2,1,0:T(8,128)(2,1)} %param.7) | copy-start | bytes 1179652
  30.7 16.0 %collective-permute-start = (bf16[16,72,256]{2,1,0:T(8,128)(2,1)S(1)}, bf16[16,72,256]{2,1,0:T(8,128)(2,1)S(1)}, u32[]{:S(2)}, u32[]{:S(2)}) collective-permute-start(bf16[16,72,256]{2,1,0:T(8,128)(2,1)S(1)} %all_to_all.10.mine_ref), channel_id=1, source_target_pairs={{0,1},{1,0},{2,3},{3,2},{4,5},{5,4},{6,7},{7,6},{8,9},{9,8},{10,11... | collective-permute-start | bytes 1769480 | tf_op jit(solution)/shard_map/ppermute | solution.py:296
  32.6 35.2 %collective-permute-start.4 = (bf16[3,256,256]{2,1,0:T(8,128)(2,1)}, bf16[3,256,256]{2,1,0:T(8,128)(2,1)S(1)}, u32[]{:S(2)}, u32[]{:S(2)}) collective-permute-start(bf16[3,256,256]{2,1,0:T(8,128)(2,1)} %bitcast.42), channel_id=1, source_target_pairs={{0,480},{32,448},{64,416},{96,384},{128,352},{160,320},{192,288},{... | collective-permute-start | bytes 1179656 | tf_op jit(solution)/shard_map/ppermute | solution.py:287
  43.8 24.0 %collective-permute-start.3 = (bf16[256,256]{1,0:T(8,128)(2,1)}, bf16[256,256]{1,0:T(8,128)(2,1)S(1)}, u32[]{:S(2)}, u32[]{:S(2)}) collective-permute-start(bf16[256,256]{1,0:T(8,128)(2,1)} %bitcast.43), channel_id=1, source_target_pairs={{0,480},{32,448},{64,416},{96,384},{128,352},{160,320},{192,288},{... | collective-permute-start | bytes 393224 | tf_op jit(solution)/shard_map/ppermute | solution.py:287
  45.7 0.9 copy-start.2
  47.4 27.3 %collective-permute-start.1 = (bf16[256,256]{1,0:T(8,128)(2,1)S(1)}, bf16[256,256]{1,0:T(8,128)(2,1)S(1)}, u32[]{:S(2)}, u32[]{:S(2)}) collective-permute-start(bf16[256,256]{1,0:T(8,128)(2,1)S(1)} %shard_map.120), channel_id=1, source_target_pairs={{32,0},{64,32},{96,64},{128,96},{160,128},{192,160},{224,192},{256... | collective-permute-start | bytes 393224 | tf_op jit(solution)/shard_map/ppermute | solution.py:292
  68.4 9.1 %collective-permute-start.5 = (bf16[256,256]{1,0:T(8,128)(2,1)S(1)}, bf16[256,256]{1,0:T(8,128)(2,1)S(1)}, u32[]{:S(2)}, u32[]{:S(2)}) collective-permute-start(bf16[256,256]{1,0:T(8,128)(2,1)S(1)} %shard_map.123.refs_3_), channel_id=1, source_target_pairs={{32,0},{64,32},{96,64},{128,96},{160,128},{192,160},{224,192},{256... | collective-permute-start | bytes 393224 | tf_op jit(solution)/shard_map/ppermute | solution.py:292
  75.3 12.2 %collective-permute-start.2 = (bf16[256,256]{1,0:T(8,128)(2,1)S(1)}, bf16[256,256]{1,0:T(8,128)(2,1)S(1)}, u32[]{:S(2)}, u32[]{:S(2)}) collective-permute-start(bf16[256,256]{1,0:T(8,128)(2,1)S(1)} %shard_map.121), channel_id=1, source_target_pairs={{32,0},{64,32},{96,64},{128,96},{160,128},{192,160},{224,192},{256... | collective-permute-start | bytes 393224 | tf_op jit(solution)/shard_map/ppermute | solution.py:292
  78.2 0.7 copy-start.5
  78.9 9.0 %collective-permute-start.7 = (bf16[256,256]{1,0:T(8,128)(2,1)S(1)}, bf16[256,256]{1,0:T(8,128)(2,1)S(1)}, u32[]{:S(2)}, u32[]{:S(2)}) collective-permute-start(bf16[256,256]{1,0:T(8,128)(2,1)S(1)} %get-tuple-element.21), channel_id=1, source_target_pairs={{32,0},{64,32},{96,64},{128,96},{160,128},{192,160},{224,192},{256... | collective-permute-start | bytes 393224 | tf_op jit(solution)/shard_map/ppermute | solution.py:292
  88.9 3.9 %collective-permute-start.9 = (bf16[16,72,256]{2,1,0:T(8,128)(2,1)S(1)}, bf16[16,72,256]{2,1,0:T(8,128)(2,1)S(1)}, u32[]{:S(2)}, u32[]{:S(2)}) collective-permute-start(bf16[16,72,256]{2,1,0:T(8,128)(2,1)S(1)} %get-tuple-element.29), channel_id=1, source_target_pairs={{0,1},{1,0},{2,3},{3,2},{4,5},{5,4},{6,7},{7,6},{8,9},{9,8},{10,11... | collective-permute-start | bytes 1769480 | tf_op jit(solution)/shard_map/ppermute | solution.py:296
  93.7 31.0 %all-to-all-start.1 = ((bf16[16,72,256]{2,1,0:T(8,128)(2,1)}), bf16[16,72,256]{2,1,0:T(8,128)(2,1)S(1)}, u32[]{:S(2)}, u32[]{:S(2)}) async-start(bf16[16,72,256]{2,1,0:T(8,128)(2,1)} %shard_map.130), calls=%async_computation.1 | async-start | bytes 1179648 | tf_op jit(solution)/shard_map/all_to_all | solution.py:335
  100.4 24.4 %copy-start.1 = (f32[1,72,256]{2,1,0:T(8,128)S(1)}, f32[1,72,256]{2,1,0:T(8,128)}, u32[]{:S(2)}) copy-start(f32[1,72,256]{2,1,0:T(8,128)} %param.11) | copy-start | bytes 221188
  100.4 24.3 %copy-start.3 = (f32[1,72,256]{2,1,0:T(8,128)S(1)}, f32[1,72,256]{2,1,0:T(8,128)}, u32[]{:S(2)}) copy-start(f32[1,72,256]{2,1,0:T(8,128)} %param.12) | copy-start | bytes 221188
  100.4 24.3 %copy-start.4 = (f32[1,72,256]{2,1,0:T(8,128)S(1)}, f32[1,72,256]{2,1,0:T(8,128)}, u32[]{:S(2)}) copy-start(f32[1,72,256]{2,1,0:T(8,128)} %param.13) | copy-start | bytes 221188
  100.4 20.8 %collective-permute-start.6 = (bf16[2,256,256]{2,1,0:T(8,128)(2,1)}, bf16[2,256,256]{2,1,0:T(8,128)(2,1)S(1)}, u32[]{:S(2)}, u32[]{:S(2)}) collective-permute-start(bf16[2,256,256]{2,1,0:T(8,128)(2,1)} %copy-done.5), channel_id=1, source_target_pairs={{0,480},{32,448},{64,416},{96,384},{128,352},{160,320},{192,288},{... | collective-permute-start | bytes 786440 | tf_op jit(solution)/shard_map/ppermute | solution.py:287
  107.0 16.9 %collective-permute-start.8 = (bf16[256,256]{1,0:T(8,128)(2,1)S(1)}, bf16[256,256]{1,0:T(8,128)(2,1)S(1)}, u32[]{:S(2)}, u32[]{:S(2)}) collective-permute-start(bf16[256,256]{1,0:T(8,128)(2,1)S(1)} %shard_map.125), channel_id=1, source_target_pairs={{0,480},{32,448},{64,416},{96,384},{128,352},{160,320},{192,288},{... | collective-permute-start | bytes 393224 | tf_op jit(solution)/shard_map/ppermute | solution.py:287

commit v7 on v6

--- a/solution.py
+++ b/solution.py
@@ -28,15 +28,16 @@
     )(*args)
 
 
-def spread_kernel(rows_ref, out_ref, wide_ref, cast_ref, fetch_sem, store_sem):
-    fetch = pltpu.make_async_copy(rows_ref, wide_ref, fetch_sem)
-    fetch.start()
-    fetch.wait()
-    cast_ref[...] = wide_ref[...].astype(jnp.bfloat16)
-    stores = [
-        pltpu.make_async_copy(cast_ref, out_ref.at[i], store_sem.at[i])
-        for i in range(out_ref.shape[0])
+def send_out(cast_ref, out_ref, sem, places):
+    return [
+        pltpu.make_async_copy(cast_ref.at[at], out_ref.at[to], sem.at[i])
+        for i, (at, to) in enumerate(places)
     ]
+
+
+def spread_kernel(rows_ref, out_ref, cast_ref, sem):
+    cast_ref[...] = rows_ref[...].astype(jnp.bfloat16)
+    stores = send_out(cast_ref, out_ref, sem, [(slice(None), i) for i in range(out_ref.shape[0])])
     for store in stores:
         store.start()
     for store in stores:
@@ -46,17 +47,16 @@
 def spread(rows, count):
     return pl.pallas_call(
         spread_kernel,
-        in_specs=[pl.BlockSpec(memory_space=pl.ANY)],
+        in_specs=[VMEM],
         out_specs=pl.BlockSpec(memory_space=pl.ANY),
         out_shape=jax.ShapeDtypeStruct((count, *rows.shape), jnp.bfloat16),
         scratch_shapes=[
-            pltpu.VMEM(rows.shape, jnp.float32),
             pltpu.VMEM(rows.shape, jnp.bfloat16),
-            pltpu.SemaphoreType.DMA,
             pltpu.SemaphoreType.DMA((count,)),
         ],
         name="spread",
-    )(rows)
+        compiler_params=pltpu.CompilerParams(vmem_limit_bytes=16 << 20),
+    )(on_chip(rows))
 
 
 def update_kernel(piece_ref, master_ref, first_ref, second_ref, *outs):
@@ -78,13 +78,29 @@
     return call(update_kernel, outs, [pieces, master, first, second], off_chip=True)
 
 
-def add_kernel(one_ref, two_ref, out_ref):
-    total = one_ref[...].astype(jnp.float32) + two_ref[...].astype(jnp.float32)
-    out_ref[...] = total.astype(jnp.bfloat16)
+def add_kernel(one_ref, two_ref, out_ref, cast_ref, sem):
+    chips = one_ref.shape[0]
+    step = chips // sem.shape[0]
+    places = [(slice(i, i + step), slice(i, i + step)) for i in range(0, chips, step)]
+    stores = send_out(cast_ref, out_ref, sem, places)
+    for store, (at, _) in zip(stores, places):
+        total = one_ref[at].astype(jnp.float32) + two_ref[at].astype(jnp.float32)
+        cast_ref[at] = total.astype(jnp.bfloat16)
+        store.start()
+    for store in stores:
+        store.wait()
 
 
 def pair_add(one, two):
-    return call(add_kernel, [(one.shape, jnp.bfloat16)], [one, two])[0]
+    return pl.pallas_call(
+        add_kernel,
+        in_specs=[VMEM] * 2,
+        out_specs=pl.BlockSpec(memory_space=pl.ANY),
+        out_shape=jax.ShapeDtypeStruct(one.shape, jnp.bfloat16),
+        scratch_shapes=[pltpu.VMEM(one.shape, jnp.bfloat16), pltpu.SemaphoreType.DMA((4,))],
+        name="pair_add",
+        compiler_params=pltpu.CompilerParams(vmem_limit_bytes=16 << 20),
+    )(on_chip(one), on_chip(two))
 
 
 def bend(x):

time: 126 us -> 126 us (level)
    pallas_call x14 -> x13, Pallas kernels: 8.7 us -> 7.74 us  [call(): pl.pallas_call(body, in_specs=specs, out_specs=[VMEM] * len(outs), out_sh...]
    unnamed x12 -> x14, local copies, waits for them, and re-layouts: 1.62 us -> 2.55 us
where the time goes in v7:
time: 126 us; the launch traced here: 125 us
  starting transfers between devices  52.4 us (42%)
  waiting for transfers between devices  30.4 us (24%)
  blocking collectives  27.9 us (22%)
  Pallas kernels  9.57 us (8%)
  local copies, waits for them, and re-layouts  2.55 us (2%)
  other arithmetic  1.57 us (1%)
    all_to_all x1, blocking collectives, step(): mine = lax.all_to_all(spread(master[0], chips), CHIPS, 0, 0, tiled=True)  27.9 us
    ppermute x4, waiting for transfers between devices, to_mirror(): lax.ppermute(value, SECTION, [(i, length - 1 - i) for i in range(length)])  27.8 us
    ppermute x4, starting transfers between devices, to_mirror(): lax.ppermute(value, SECTION, [(i, length - 1 - i) for i in range(length)])  21.2 us
    ppermute x4, starting transfers between devices, from_next(): return lax.ppermute(value, SECTION, [(i + 1, i) for i in range(length - 1)])  20.7 us
    pallas_call x13, Pallas kernels, call(): pl.pallas_call(body, in_specs=specs, out_specs=[VMEM] * len(outs), out_sh...  7.74 us
    all_to_all x1, starting transfers between devices, step(): pieces = lax.all_to_all(both, CHIPS, 0, 0, tiled=True)  6.69 us
    ppermute x2, starting transfers between devices, to_partner(): return lax.ppermute(value, 'core', [(0, 1), (1, 0)])  3.83 us
    unnamed x14, local copies, waits for them, and re-layouts  2.55 us
  transfers between devices with their start and end apart: 11, of which 6 were waited for; matrix products, arithmetic and copies ran while one was open for 1% of the time, Pallas kernels for 5%

profile of v7, /device:TPU:6, one launch (start us, length us, event | category | flops | bytes accessed | tf_op | source)
XLA Modules:
  0.0 125.3 jit_solution(9825308507363932731)
XLA Ops:
  0.7 0.9 copy-done.1
  1.6 0.9 spread.1
  2.5 27.9 %all_to_all.10.mine_ref = bf16[16,72,256]{2,1,0:T(8,128)(2,1)S(1)} all-to-all(bf16[16,72,256]{2,1,0:T(8,128)(2,1)S(1)} %spread.1), channel_id=1, replica_groups=mesh['x_lo'=2,'z'=8,'x_hi'=2,'y'=8,'core'=2] {'x_hi','y'}, dimensions={0} | all-to-all | bytes 1179648 | tf_op jit(solution)/shard_map/all_to_all | solution.py:323
  30.4 1.9 %collective-permute-start = (bf16[16,72,256]{2,1,0:T(8,128)(2,1)S(1)}, bf16[16,72,256]{2,1,0:T(8,128)(2,1)S(1)}, u32[]{:S(2)}, u32[]{:S(2)}) collective-permute-start(bf16[16,72,256]{2,1,0:T(8,128)(2,1)S(1)} %all_to_all.10.mine_ref), channel_id=1, source_target_pairs={{0,1},{1,0},{2,3},{3,2},{4,5},{5,4},{6,7},{7,6},{8,9},{9,8},{10,11... | collective-permute-start | bytes 1769480 | tf_op jit(solution)/shard_map/ppermute | solution.py:312
  32.3 11.2 %collective-permute-start.4 = (bf16[3,256,256]{2,1,0:T(8,128)(2,1)}, bf16[3,256,256]{2,1,0:T(8,128)(2,1)S(1)}, u32[]{:S(2)}, u32[]{:S(2)}) collective-permute-start(bf16[3,256,256]{2,1,0:T(8,128)(2,1)} %bitcast.42), channel_id=1, source_target_pairs={{0,480},{32,448},{64,416},{96,384},{128,352},{160,320},{192,288},{... | collective-permute-start | bytes 1179656 | tf_op jit(solution)/shard_map/ppermute | solution.py:303
  43.6 1.9 %collective-permute-start.3 = (bf16[256,256]{1,0:T(8,128)(2,1)}, bf16[256,256]{1,0:T(8,128)(2,1)S(1)}, u32[]{:S(2)}, u32[]{:S(2)}) collective-permute-start(bf16[256,256]{1,0:T(8,128)(2,1)} %bitcast.43), channel_id=1, source_target_pairs={{0,480},{32,448},{64,416},{96,384},{128,352},{160,320},{192,288},{... | collective-permute-start | bytes 393224 | tf_op jit(solution)/shard_map/ppermute | solution.py:303
  45.5 0.9 copy-done.3
  46.5 0.6 shard_map.120
  47.1 6.0 %collective-permute-start.1 = (bf16[256,256]{1,0:T(8,128)(2,1)S(1)}, bf16[256,256]{1,0:T(8,128)(2,1)S(1)}, u32[]{:S(2)}, u32[]{:S(2)}) collective-permute-start(bf16[256,256]{1,0:T(8,128)(2,1)S(1)} %shard_map.120), channel_id=1, source_target_pairs={{32,0},{64,32},{96,64},{128,96},{160,128},{192,160},{224,192},{256... | collective-permute-start | bytes 393224 | tf_op jit(solution)/shard_map/ppermute | solution.py:308
  53.2 14.4 %collective-permute-done.3.refs_0_.refs_6_ = bf16[256,256]{1,0:T(8,128)(2,1)S(1)} collective-permute-done((bf16[256,256]{1,0:T(8,128)(2,1)}, bf16[256,256]{1,0:T(8,128)(2,1)S(1)}, u32[]{:S(2)}, u32[]{:S(2)}) %collective-permute-start.3) | collective-permute-done | bytes 131104 | tf_op jit(solution)/shard_map/ppermute | solution.py:303
  67.6 0.6 shard_map.123.refs_3_
  68.2 6.2 %collective-permute-start.5 = (bf16[256,256]{1,0:T(8,128)(2,1)S(1)}, bf16[256,256]{1,0:T(8,128)(2,1)S(1)}, u32[]{:S(2)}, u32[]{:S(2)}) collective-permute-start(bf16[256,256]{1,0:T(8,128)(2,1)S(1)} %shard_map.123.refs_3_), channel_id=1, source_target_pairs={{32,0},{64,32},{96,64},{128,96},{160,128},{192,160},{224,192},{256... | collective-permute-start | bytes 393224 | tf_op jit(solution)/shard_map/ppermute | solution.py:308
  74.4 0.6 shard_map.121
  75.0 1.9 %collective-permute-start.2 = (bf16[256,256]{1,0:T(8,128)(2,1)S(1)}, bf16[256,256]{1,0:T(8,128)(2,1)S(1)}, u32[]{:S(2)}, u32[]{:S(2)}) collective-permute-start(bf16[256,256]{1,0:T(8,128)(2,1)S(1)} %shard_map.121), channel_id=1, source_target_pairs={{32,0},{64,32},{96,64},{128,96},{160,128},{192,160},{224,192},{256... | collective-permute-start | bytes 393224 | tf_op jit(solution)/shard_map/ppermute | solution.py:308
  77.3 0.6 shard_map.124
  77.9 0.7 copy-done.6
  78.6 6.5 %collective-permute-start.7 = (bf16[256,256]{1,0:T(8,128)(2,1)S(1)}, bf16[256,256]{1,0:T(8,128)(2,1)S(1)}, u32[]{:S(2)}, u32[]{:S(2)}) collective-permute-start(bf16[256,256]{1,0:T(8,128)(2,1)S(1)} %get-tuple-element.21), channel_id=1, source_target_pairs={{32,0},{64,32},{96,64},{128,96},{160,128},{192,160},{224,192},{256... | collective-permute-start | bytes 393224 | tf_op jit(solution)/shard_map/ppermute | solution.py:308
  85.8 1.4 %shard_map.128.total_ref = f32[2304,256]{1,0:T(8,128)S(1)} custom-call(bf16[256,256]{1,0:T(8,128)(2,1)S(1)} %get-tuple-element.22.refs_0_, bf16[256,256]{1,0:T(8,128)(2,1)S(1)} %get-tuple-element.23.refs_1_, bf16[256,256]{1,0:T(8,128)(2,1)S(1)} %get-tuple-element.24.refs_2_, bf16[256,256]{1,0:T(8,128)(2,1)S(1)} %get-tuple-element.25.refs_3_, ...), custom_call_target="tpu_custom_call" | custom-call | tf_op jit(solution)/shard_map/pallas_call | solution.py:21
  87.6 1.0 shard_map.129
  88.6 1.9 %collective-permute-start.9 = (bf16[16,72,256]{2,1,0:T(8,128)(2,1)S(1)}, bf16[16,72,256]{2,1,0:T(8,128)(2,1)S(1)}, u32[]{:S(2)}, u32[]{:S(2)}) collective-permute-start(bf16[16,72,256]{2,1,0:T(8,128)(2,1)S(1)} %get-tuple-element.29), channel_id=1, source_target_pairs={{0,1},{1,0},{2,3},{3,2},{4,5},{5,4},{6,7},{7,6},{8,9},{9,8},{10,11... | collective-permute-start | bytes 1769480 | tf_op jit(solution)/shard_map/ppermute | solution.py:312
  90.5 2.0 %collective-permute-done.9.two_ref = bf16[16,72,256]{2,1,0:T(8,128)(2,1)S(1)} collective-permute-done((bf16[16,72,256]{2,1,0:T(8,128)(2,1)S(1)}, bf16[16,72,256]{2,1,0:T(8,128)(2,1)S(1)}, u32[]{:S(2)}, u32[]{:S(2)}) %collective-permute-start.9) | collective-permute-done | bytes 589856 | tf_op jit(solution)/shard_map/ppermute | solution.py:312
  92.5 0.9 pair_add.1
  93.4 6.7 %all-to-all-start.1 = ((bf16[16,72,256]{2,1,0:T(8,128)(2,1)}), bf16[16,72,256]{2,1,0:T(8,128)(2,1)S(1)}, u32[]{:S(2)}, u32[]{:S(2)}) async-start(bf16[16,72,256]{2,1,0:T(8,128)(2,1)} %pair_add.1), calls=%async_computation.1 | async-start | bytes 1179648 | tf_op jit(solution)/shard_map/all_to_all | solution.py:351
  100.1 6.0 %collective-permute-start.6 = (bf16[2,256,256]{2,1,0:T(8,128)(2,1)}, bf16[2,256,256]{2,1,0:T(8,128)(2,1)S(1)}, u32[]{:S(2)}, u32[]{:S(2)}) collective-permute-start(bf16[2,256,256]{2,1,0:T(8,128)(2,1)} %copy-done.6), channel_id=1, source_target_pairs={{0,480},{32,448},{64,416},{96,384},{128,352},{160,320},{192,288},{... | collective-permute-start | bytes 786440 | tf_op jit(solution)/shard_map/ppermute | solution.py:303
  106.1 0.6 shard_map.125
  106.7 2.1 %collective-permute-start.8 = (bf16[256,256]{1,0:T(8,128)(2,1)S(1)}, bf16[256,256]{1,0:T(8,128)(2,1)S(1)}, u32[]{:S(2)}, u32[]{:S(2)}) collective-permute-start(bf16[256,256]{1,0:T(8,128)(2,1)S(1)} %shard_map.125), channel_id=1, source_target_pairs={{0,480},{32,448},{64,416},{96,384},{128,352},{160,320},{192,288},{... | collective-permute-start | bytes 393224 | tf_op jit(solution)/shard_map/ppermute | solution.py:303
  108.8 0.6 shard_map.122
  109.5 0.8 pad_maximum_fusion
  110.2 10.7 %collective-permute-done.6 = bf16[2,256,256]{2,1,0:T(8,128)(2,1)S(1)} collective-permute-done((bf16[2,256,256]{2,1,0:T(8,128)(2,1)}, bf16[2,256,256]{2,1,0:T(8,128)(2,1)S(1)}, u32[]{:S(2)}, u32[]{:S(2)}) %collective-permute-start.6) | collective-permute-done | bytes 262176 | tf_op jit(solution)/shard_map/ppermute | solution.py:303
  120.9 2.7 %collective-permute-done.8 = bf16[256,256]{1,0:T(8,128)(2,1)S(1)} collective-permute-done((bf16[256,256]{1,0:T(8,128)(2,1)S(1)}, bf16[256,256]{1,0:T(8,128)(2,1)S(1)}, u32[]{:S(2)}, u32[]{:S(2)}) %collective-permute-start.8) | collective-permute-done | bytes 131104 | tf_op jit(solution)/shard_map/ppermute | solution.py:303
  123.7 0.8 pad_maximum_fusion.1
  124.5 0.8 shard_map.130
  (22 shorter events, 1.5 us)
Async XLA Ops:
  0.6 45.9 %copy-start = (bf16[3,1,1,16,16,256]{5,4,3,2,1,0:T(8,128)(2,1)S(1)}, bf16[3,1,1,16,16,256]{5,4,3,2,1,0:T(8,128)(2,1)}, u32[]{:S(2)}) copy-start(bf16[3,1,1,16,16,256]{5,4,3,2,1,0:T(8,128)(2,1)} %param.7) | copy-start | bytes 1179652
  0.6 0.9 copy-start.1
  30.4 16.0 %collective-permute-start = (bf16[16,72,256]{2,1,0:T(8,128)(2,1)S(1)}, bf16[16,72,256]{2,1,0:T(8,128)(2,1)S(1)}, u32[]{:S(2)}, u32[]{:S(2)}) collective-permute-start(bf16[16,72,256]{2,1,0:T(8,128)(2,1)S(1)} %all_to_all.10.mine_ref), channel_id=1, source_target_pairs={{0,1},{1,0},{2,3},{3,2},{4,5},{5,4},{6,7},{7,6},{8,9},{9,8},{10,11... | collective-permute-start | bytes 1769480 | tf_op jit(solution)/shard_map/ppermute | solution.py:312
  32.3 35.2 %collective-permute-start.4 = (bf16[3,256,256]{2,1,0:T(8,128)(2,1)}, bf16[3,256,256]{2,1,0:T(8,128)(2,1)S(1)}, u32[]{:S(2)}, u32[]{:S(2)}) collective-permute-start(bf16[3,256,256]{2,1,0:T(8,128)(2,1)} %bitcast.42), channel_id=1, source_target_pairs={{0,480},{32,448},{64,416},{96,384},{128,352},{160,320},{192,288},{... | collective-permute-start | bytes 1179656 | tf_op jit(solution)/shard_map/ppermute | solution.py:303
  43.6 24.0 %collective-permute-start.3 = (bf16[256,256]{1,0:T(8,128)(2,1)}, bf16[256,256]{1,0:T(8,128)(2,1)S(1)}, u32[]{:S(2)}, u32[]{:S(2)}) collective-permute-start(bf16[256,256]{1,0:T(8,128)(2,1)} %bitcast.43), channel_id=1, source_target_pairs={{0,480},{32,448},{64,416},{96,384},{128,352},{160,320},{192,288},{... | collective-permute-start | bytes 393224 | tf_op jit(solution)/shard_map/ppermute | solution.py:303
  45.5 0.9 copy-start.3
  47.1 27.3 %collective-permute-start.1 = (bf16[256,256]{1,0:T(8,128)(2,1)S(1)}, bf16[256,256]{1,0:T(8,128)(2,1)S(1)}, u32[]{:S(2)}, u32[]{:S(2)}) collective-permute-start(bf16[256,256]{1,0:T(8,128)(2,1)S(1)} %shard_map.120), channel_id=1, source_target_pairs={{32,0},{64,32},{96,64},{128,96},{160,128},{192,160},{224,192},{256... | collective-permute-start | bytes 393224 | tf_op jit(solution)/shard_map/ppermute | solution.py:308
  68.2 9.1 %collective-permute-start.5 = (bf16[256,256]{1,0:T(8,128)(2,1)S(1)}, bf16[256,256]{1,0:T(8,128)(2,1)S(1)}, u32[]{:S(2)}, u32[]{:S(2)}) collective-permute-start(bf16[256,256]{1,0:T(8,128)(2,1)S(1)} %shard_map.123.refs_3_), channel_id=1, source_target_pairs={{32,0},{64,32},{96,64},{128,96},{160,128},{192,160},{224,192},{256... | collective-permute-start | bytes 393224 | tf_op jit(solution)/shard_map/ppermute | solution.py:308
  75.0 12.2 %collective-permute-start.2 = (bf16[256,256]{1,0:T(8,128)(2,1)S(1)}, bf16[256,256]{1,0:T(8,128)(2,1)S(1)}, u32[]{:S(2)}, u32[]{:S(2)}) collective-permute-start(bf16[256,256]{1,0:T(8,128)(2,1)S(1)} %shard_map.121), channel_id=1, source_target_pairs={{32,0},{64,32},{96,64},{128,96},{160,128},{192,160},{224,192},{256... | collective-permute-start | bytes 393224 | tf_op jit(solution)/shard_map/ppermute | solution.py:308
  77.9 0.7 copy-start.6
  78.6 9.0 %collective-permute-start.7 = (bf16[256,256]{1,0:T(8,128)(2,1)S(1)}, bf16[256,256]{1,0:T(8,128)(2,1)S(1)}, u32[]{:S(2)}, u32[]{:S(2)}) collective-permute-start(bf16[256,256]{1,0:T(8,128)(2,1)S(1)} %get-tuple-element.21), channel_id=1, source_target_pairs={{32,0},{64,32},{96,64},{128,96},{160,128},{192,160},{224,192},{256... | collective-permute-start | bytes 393224 | tf_op jit(solution)/shard_map/ppermute | solution.py:308
  88.6 3.9 %collective-permute-start.9 = (bf16[16,72,256]{2,1,0:T(8,128)(2,1)S(1)}, bf16[16,72,256]{2,1,0:T(8,128)(2,1)S(1)}, u32[]{:S(2)}, u32[]{:S(2)}) collective-permute-start(bf16[16,72,256]{2,1,0:T(8,128)(2,1)S(1)} %get-tuple-element.29), channel_id=1, source_target_pairs={{0,1},{1,0},{2,3},{3,2},{4,5},{5,4},{6,7},{7,6},{8,9},{9,8},{10,11... | collective-permute-start | bytes 1769480 | tf_op jit(solution)/shard_map/ppermute | solution.py:312
  93.4 31.0 %all-to-all-start.1 = ((bf16[16,72,256]{2,1,0:T(8,128)(2,1)}), bf16[16,72,256]{2,1,0:T(8,128)(2,1)S(1)}, u32[]{:S(2)}, u32[]{:S(2)}) async-start(bf16[16,72,256]{2,1,0:T(8,128)(2,1)} %pair_add.1), calls=%async_computation.1 | async-start | bytes 1179648 | tf_op jit(solution)/shard_map/all_to_all | solution.py:351
  100.1 24.4 %copy-start.2 = (f32[1,72,256]{2,1,0:T(8,128)S(1)}, f32[1,72,256]{2,1,0:T(8,128)}, u32[]{:S(2)}) copy-start(f32[1,72,256]{2,1,0:T(8,128)} %param.11) | copy-start | bytes 221188
  100.1 24.3 %copy-start.4 = (f32[1,72,256]{2,1,0:T(8,128)S(1)}, f32[1,72,256]{2,1,0:T(8,128)}, u32[]{:S(2)}) copy-start(f32[1,72,256]{2,1,0:T(8,128)} %param.12) | copy-start | bytes 221188
  100.1 24.3 %copy-start.5 = (f32[1,72,256]{2,1,0:T(8,128)S(1)}, f32[1,72,256]{2,1,0:T(8,128)}, u32[]{:S(2)}) copy-start(f32[1,72,256]{2,1,0:T(8,128)} %param.13) | copy-start | bytes 221188
  100.1 20.8 %collective-permute-start.6 = (bf16[2,256,256]{2,1,0:T(8,128)(2,1)}, bf16[2,256,256]{2,1,0:T(8,128)(2,1)S(1)}, u32[]{:S(2)}, u32[]{:S(2)}) collective-permute-start(bf16[2,256,256]{2,1,0:T(8,128)(2,1)} %copy-done.6), channel_id=1, source_target_pairs={{0,480},{32,448},{64,416},{96,384},{128,352},{160,320},{192,288},{... | collective-permute-start | bytes 786440 | tf_op jit(solution)/shard_map/ppermute | solution.py:303
  106.7 16.9 %collective-permute-start.8 = (bf16[256,256]{1,0:T(8,128)(2,1)S(1)}, bf16[256,256]{1,0:T(8,128)(2,1)S(1)}, u32[]{:S(2)}, u32[]{:S(2)}) collective-permute-start(bf16[256,256]{1,0:T(8,128)(2,1)S(1)} %shard_map.125), channel_id=1, source_target_pairs={{0,480},{32,448},{64,416},{96,384},{128,352},{160,320},{192,288},{... | collective-permute-start | bytes 393224 | tf_op jit(solution)/shard_map/ppermute | solution.py:303
